TPU v7x, 512 devices: a whole 4x8x8 slice. The times are simulated.
512 devices in a mesh: gx: 4 (over z_lo, core), gy: 4 (over z_hi), gz: 32 (over y, x).
Axes of the slice: x: 4, y: 8, z: 8 (z_hi: 4, z_lo: 2; z = z_hi * 2 + z_lo), core: 2. Of those that a mesh axis runs over, the one named last changes fastest.
Arguments:
- gram_factor: bfloat16 [6144, 384, 384], P(('gx', 'gy', 'gz')), may hold values from -0.3125 to 0.3125
- coupling: bfloat16 [6144, 384, 128], P(('gx', 'gy', 'gz')), may hold values from -0.375 to 0.375
- order_class: int32 [6144], P(('gx', 'gy', 'gz')), may hold values from 0 to 2
- first_moves: int32 [1536], P(('gx', 'gy', 'gz')), may hold values from 0 to 11, as said below
- second_moves: int32 [1536], P(('gx', 'gy', 'gz')), may hold values from 0 to 11, as said below
- trace_index: int32 [6144, 128], P(('gx', 'gy', 'gz')), may hold values from 1 to 322, as said below
- owner_index: int32 [6144, 128], P(('gx', 'gy', 'gz')), may hold values from 0 to 255
- traces: bfloat16 [64, 4, 512, 256], P('gx', 'gy', 'gz'), may hold values from -6 to 6
Outputs:
- applied: float32 [64, 4, 512, 256], P('gx', 'gy', 'gz')
Inputs may be any that keep to these rules, and one draw needn't show every extreme that they name: `first_moves`: on each device the 3 entries are distinct slots. `second_moves`: on each device the 3 entries are distinct slots. `trace_index`: never a corner cell of the extended grid.
All inputs are finite; a program needn't handle non-finite values.
Results may differ from a plain program's by a relative error of at most 0.0044.
Values may be sent and summed in bfloat16 or wider, within the bound.
No kernel may reach another device: no remote copies, remote signals or barrier semaphores. Data moves between devices by JAX's collectives and lax.ppermute only.
A program may use at most 64 MiB of HBM per device.

v0:
```python
import jax
import jax.numpy as jnp
from jax import lax
from jax.sharding import PartitionSpec as P


def swapped(block, axis, bit):
    count = lax.axis_size(axis)
    route = []
    for low in range(count):
        high = low | 1 << bit
        if high != low and high < count:
            route += [(low, high), (high, low)]
    return lax.ppermute(block, axis, route)


def with_halo(block, sides, width):
    for axis, dim in sides:
        count = lax.axis_size(axis)
        forward = [(i, i + 1) for i in range(count - 1)]
        backward = [(target, source) for source, target in forward]
        low = lax.ppermute(
            lax.slice_in_dim(block, block.shape[dim] - width, None, axis=dim), axis, forward
        )
        high = lax.ppermute(lax.slice_in_dim(block, 0, width, axis=dim), axis, backward)
        block = jnp.concatenate([low, block, high], axis=dim)
    return block


def product_of(masked, coupling):
    return jnp.einsum("ewv,evk->ewk", masked, coupling, preferred_element_type=jnp.float32).astype(
        jnp.bfloat16
    )


def body(
    gram_factor, coupling, order_class, first_moves, second_moves, trace_index, owner_index, traces
):
    width_full = gram_factor.shape[1]
    rows = lax.broadcasted_iota(jnp.int32, (1, width_full), 1)
    widths = width_full * (2 + order_class) // 4
    keep = (rows < widths[:, None]).astype(gram_factor.dtype)
    masked = gram_factor * keep[:, :, None]
    second_bit = lax.axis_size("gz").bit_length() - 1
    operator = product_of(masked, coupling)
    given = swapped(operator[first_moves], "gz", 0)
    operator = operator.at[first_moves].set(given)
    given_two = swapped(operator[second_moves], ("gy", "gz"), second_bit)
    operator = operator.at[second_moves].set(given_two)
    rows_x = traces.shape[0]
    rows_z = traces.shape[2]
    columns = traces.shape[3]
    targets = owner_index.reshape(-1)

    def apply_field(field):
        extended = with_halo(field, (("gx", 0), ("gz", 1)), 1)
        flattened = extended.reshape(-1, columns)
        gathered = flattened[trace_index]
        tested = jnp.einsum(
            "ewk,ekr->ewr", operator, gathered, preferred_element_type=jnp.float32
        ).astype(jnp.bfloat16)
        element_out = jnp.einsum(
            "ewk,ewr->ekr", operator, tested, preferred_element_type=jnp.float32
        )
        result = (
            jnp.zeros((rows_x * rows_z, columns), jnp.float32)
            .at[targets]
            .add(element_out.reshape(-1, columns))
        )
        return result.reshape(rows_x, rows_z, columns)

    first = apply_field(traces[:, 0]).astype(jnp.bfloat16)
    second = apply_field(first)
    return second[:, None]


def solution(mesh):
    return jax.shard_map(
        body,
        mesh=mesh,
        in_specs=(
            P(("gx", "gy", "gz"), None, None),
            P(("gx", "gy", "gz"), None, None),
            P(("gx", "gy", "gz")),
            P(("gx", "gy", "gz")),
            P(("gx", "gy", "gz")),
            P(("gx", "gy", "gz"), None),
            P(("gx", "gy", "gz"), None),
            P("gx", "gy", "gz", None),
        ),
        out_specs=P("gx", "gy", "gz", None),
        check_vma=False,
    )
```

profile of v0, /device:TPU:31, one launch (start us, length us, event | category | flops | bytes accessed | tf_op | source)
XLA Modules:
  0.0 97.9 jit_solution(6698490572956433385)
XLA Ops:
  0.0 0.0 copy-start
  0.0 0.8 slice_bitcast_fusion.3
  0.8 4.5 %collective-permute-start.2 = (bf16[1,16,256]{2,1,0:T(8,128)(2,1)S(1)}, bf16[1,16,256]{2,1,0:T(8,128)(2,1)S(1)}, u32[]{:S(2)}, u32[]{:S(2)}) collective-permute-start(bf16[1,16,256]{2,1,0:T(8,128)(2,1)S(1)} %get-tuple-element.11), channel_id=1, source_target_pairs={{0,128},{128,256},{256,384},{1,129},{129,257},{257,385},{2,130},{1... | collective-permute-start | bytes 24584 | tf_op jit(solution)/shard_map/ppermute | solution.py:22
  5.4 1.9 %collective-permute-start.3 = (bf16[1,16,256]{2,1,0:T(8,128)(2,1)S(1)}, bf16[1,16,256]{2,1,0:T(8,128)(2,1)S(1)}, u32[]{:S(2)}, u32[]{:S(2)}) collective-permute-start(bf16[1,16,256]{2,1,0:T(8,128)(2,1)S(1)} %get-tuple-element.12), channel_id=1, source_target_pairs={{128,0},{256,128},{384,256},{129,1},{257,129},{385,257},{130,2},{2... | collective-permute-start | bytes 24584 | tf_op jit(solution)/shard_map/ppermute | solution.py:25
  7.3 0.7 and_select_fusion
  8.0 0.1 fusion.18
  8.0 0.7 compare_select_fusion.3
  8.7 0.0 copy-done
  8.7 0.0 copy-start.2
  8.7 0.0 copy-start.3
  8.7 0.0 copy-start.4
  8.8 3.2 %fusion.11 = bf16[12,384,128]{2,1,0:T(8,128)(2,1)S(1)} fusion(bf16[12,384,128]{2,1,0:T(8,128)(2,1)S(1)} %copy-done, bf16[12,384,384]{2,1,0:T(8,128)(2,1)} %param.8, bf16[12,384]{1,0:T(8,128)(2,1)S(1)} %fusion.18), kind=kOutput, calls=%fused_computation.17 | convolution fusion | flops 455344128 | bytes 5907456 | tf_op jit(solution)/shard_map/ewv,evk->ewk/dot_general | solution.py:31
  11.9 0.0 copy-start.1
  11.9 0.6 gather_fusion
  12.5 2.5 %collective-permute-start = (bf16[3,384,128]{2,1,0:T(8,128)(2,1)S(1)}, bf16[3,384,128]{2,1,0:T(8,128)(2,1)S(1)}, u32[]{:S(2)}, u32[]{:S(2)}) collective-permute-start(bf16[3,384,128]{2,1,0:T(8,128)(2,1)S(1)} %gather_fusion), channel_id=1, source_target_pairs={{0,1},{1,0},{2,3},{3,2},{4,5},{5,4},{6,7},{7,6},{8,9},{9,8},{10,11... | collective-permute-start | bytes 884744 | tf_op jit(solution)/shard_map/ppermute | solution.py:14
  15.0 0.0 copy-done.2
  15.0 0.0 copy-done.3
  15.1 5.7 %collective-permute-done = bf16[3,384,128]{2,1,0:T(8,128)(2,1)S(1)} collective-permute-done((bf16[3,384,128]{2,1,0:T(8,128)(2,1)S(1)}, bf16[3,384,128]{2,1,0:T(8,128)(2,1)S(1)}, u32[]{:S(2)}, u32[]{:S(2)}) %collective-permute-start) | collective-permute-done | bytes 294944 | tf_op jit(solution)/shard_map/ppermute | solution.py:14
  20.9 0.8 scatter_fusion
  21.6 1.3 %gather_fusion.1 = bf16[3,384,128]{2,1,0:T(8,128)(2,1)} fusion(bf16[12,384,128]{2,1,0:T(8,128)(2,1)S(1)} %scatter_fusion, s32[1024]{0:T(1024)S(1)} %pad_clamp_fusion.1), kind=kCustom, calls=%fused_computation.1 | custom fusion | bytes 589836 | tf_op jit(solution)/shard_map/gather | solution.py:48
  22.9 5.8 %collective-permute-start.1 = (bf16[3,384,128]{2,1,0:T(8,128)(2,1)}, bf16[3,384,128]{2,1,0:T(8,128)(2,1)}, u32[]{:S(2)}, u32[]{:S(2)}) collective-permute-start(bf16[3,384,128]{2,1,0:T(8,128)(2,1)} %gather_fusion.1), channel_id=1, source_target_pairs={{0,32},{32,0},{1,33},{33,1},{2,34},{34,2},{3,35},{35,3},{4,36},{36... | collective-permute-start | bytes 884744 | tf_op jit(solution)/shard_map/ppermute | solution.py:14
  28.7 0.0 collective-permute-done.2
  28.7 0.0 collective-permute-done.3
  28.8 0.0 copy-done.1
  28.8 4.3 %collective-permute-start.4 = (bf16[18,1,256]{2,1,0:T(2,128)(2,1)S(1)}, bf16[18,1,256]{2,1,0:T(2,128)(2,1)S(1)}, u32[]{:S(2)}, u32[]{:S(2)}) collective-permute-start(bf16[18,1,256]{2,1,0:T(2,128)(2,1)S(1)} %get-tuple-element.7), channel_id=1, source_target_pairs={{0,1},{1,2},{2,3},{3,4},{4,5},{5,6},{6,7},{7,8},{8,9},{9,10},{10,1... | collective-permute-start | bytes 27656 | tf_op jit(solution)/shard_map/ppermute | solution.py:22
  33.1 1.9 %collective-permute-start.5 = (bf16[18,1,256]{2,1,0:T(2,128)(2,1)S(1)}, bf16[18,1,256]{2,1,0:T(2,128)(2,1)S(1)}, u32[]{:S(2)}, u32[]{:S(2)}) collective-permute-start(bf16[18,1,256]{2,1,0:T(2,128)(2,1)S(1)} %get-tuple-element.8), channel_id=1, source_target_pairs={{1,0},{2,1},{3,2},{4,3},{5,4},{6,5},{7,6},{8,7},{9,8},{10,9},{11,1... | collective-permute-start | bytes 27656 | tf_op jit(solution)/shard_map/ppermute | solution.py:25
  35.1 0.0 collective-permute-done.4
  35.1 5.9 %collective-permute-done.5 = bf16[18,1,256]{2,1,0:T(2,128)(2,1)S(1)} collective-permute-done((bf16[18,1,256]{2,1,0:T(2,128)(2,1)S(1)}, bf16[18,1,256]{2,1,0:T(2,128)(2,1)S(1)}, u32[]{:S(2)}, u32[]{:S(2)}) %collective-permute-start.5) | collective-permute-done | bytes 9248 | tf_op jit(solution)/shard_map/ppermute | solution.py:25
  41.0 0.1 pad_maximum_fusion
  41.1 0.1 reshape.72
  41.2 4.8 %gather_fusion.2 = bf16[1536,256]{1,0:T(8,128)(2,1)S(1)} fusion(bf16[324,256]{1,0:T(8,128)(2,1)S(1)} %reshape.72, s32[2048]{0:T(1024)S(1)} %pad_clamp_fusion), kind=kCustom, calls=%fused_computation.2 | custom fusion | bytes 1579008 | tf_op jit(solution)/shard_map/gather | solution.py:58
  45.9 0.0 collective-permute-done.1
  45.9 1.6 %scatter_fusion.1 = bf16[12,384,128]{2,1,0:T(8,128)(2,1)S(1)} fusion(bf16[12,384,128]{2,1,0:T(8,128)(2,1)S(1)} %scatter_fusion, s32[3]{0:T(128)S(1)} %compare_select_fusion.2, bf16[3,384,128]{2,1,0:T(8,128)(2,1)} %collective-permute-done.1), kind=kCustom, calls=%fused_computation.5 | custom fusion | bytes 884748 | tf_op jit(solution)/shard_map/scatter | solution.py:49
  47.5 2.4 %fusion.4 = f32[12,128,256]{2,1,0:T(8,128)} fusion(bf16[12,384,128]{2,1,0:T(8,128)(2,1)S(1)} %scatter_fusion.1, bf16[12,128,256]{2,1,0:T(8,128)(2,1)S(1)} %bitcast.29), kind=kOutput, calls=%fused_computation.12 | convolution fusion | flops 605159424 | bytes 3538944 | tf_op jit(solution)/shard_map/ewk,ewr->ekr/dot_general | solution.py:62
  49.9 9.3 %scatter_custom_fusion.2 = f32[256,256]{1,0:T(8,128)S(1)} fusion(s32[1536]{0:T(1024)S(1)} %fusion.20, f32[1536,256]{1,0:T(8,128)} %bitcast.32, f32[]{:T(128)} %constant.10.clone.1), kind=kCustom, calls=%fused_computation.22 | custom fusion | flops 393216 | bytes 262656 | tf_op jit(solution)/shard_map/scatter-add | solution.py:68
  59.2 6.6 %collective-permute-start.6 = (bf16[1,16,256]{2,1,0:T(8,128)(2,1)S(1)}, bf16[1,16,256]{2,1,0:T(8,128)(2,1)S(1)}, u32[]{:S(2)}, u32[]{:S(2)}) collective-permute-start(bf16[1,16,256]{2,1,0:T(8,128)(2,1)S(1)} %get-tuple-element.9), channel_id=1, source_target_pairs={{0,128},{128,256},{256,384},{1,129},{129,257},{257,385},{2,130},{1... | collective-permute-start | bytes 24584 | tf_op jit(solution)/shard_map/ppermute | solution.py:22
  65.9 1.9 %collective-permute-start.7 = (bf16[1,16,256]{2,1,0:T(8,128)(2,1)S(1)}, bf16[1,16,256]{2,1,0:T(8,128)(2,1)S(1)}, u32[]{:S(2)}, u32[]{:S(2)}) collective-permute-start(bf16[1,16,256]{2,1,0:T(8,128)(2,1)S(1)} %get-tuple-element.10), channel_id=1, source_target_pairs={{128,0},{256,128},{384,256},{129,1},{257,129},{385,257},{130,2},{2... | collective-permute-start | bytes 24584 | tf_op jit(solution)/shard_map/ppermute | solution.py:25
  67.8 0.0 collective-permute-done.6
  67.8 3.0 %collective-permute-done.7 = bf16[1,16,256]{2,1,0:T(8,128)(2,1)S(1)} collective-permute-done((bf16[1,16,256]{2,1,0:T(8,128)(2,1)S(1)}, bf16[1,16,256]{2,1,0:T(8,128)(2,1)S(1)}, u32[]{:S(2)}, u32[]{:S(2)}) %collective-permute-start.7) | collective-permute-done | bytes 8224 | tf_op jit(solution)/shard_map/ppermute | solution.py:25
  70.9 1.9 %collective-permute-start.8 = (bf16[18,1,256]{2,1,0:T(2,128)(2,1)S(1)}, bf16[18,1,256]{2,1,0:T(2,128)(2,1)S(1)}, u32[]{:S(2)}, u32[]{:S(2)}) collective-permute-start(bf16[18,1,256]{2,1,0:T(2,128)(2,1)S(1)} %get-tuple-element.5), channel_id=1, source_target_pairs={{0,1},{1,2},{2,3},{3,4},{4,5},{5,6},{6,7},{7,8},{8,9},{9,10},{10,1... | collective-permute-start | bytes 27656 | tf_op jit(solution)/shard_map/ppermute | solution.py:22
  72.8 3.4 %collective-permute-start.9 = (bf16[18,1,256]{2,1,0:T(2,128)(2,1)S(1)}, bf16[18,1,256]{2,1,0:T(2,128)(2,1)S(1)}, u32[]{:S(2)}, u32[]{:S(2)}) collective-permute-start(bf16[18,1,256]{2,1,0:T(2,128)(2,1)S(1)} %get-tuple-element.6), channel_id=1, source_target_pairs={{1,0},{2,1},{3,2},{4,3},{5,4},{6,5},{7,6},{8,7},{9,8},{10,9},{11,1... | collective-permute-start | bytes 27656 | tf_op jit(solution)/shard_map/ppermute | solution.py:25
  76.2 0.0 collective-permute-done.8
  76.2 4.4 %collective-permute-done.9 = bf16[18,1,256]{2,1,0:T(2,128)(2,1)S(1)} collective-permute-done((bf16[18,1,256]{2,1,0:T(2,128)(2,1)S(1)}, bf16[18,1,256]{2,1,0:T(2,128)(2,1)S(1)}, u32[]{:S(2)}, u32[]{:S(2)}) %collective-permute-start.9) | collective-permute-done | bytes 9248 | tf_op jit(solution)/shard_map/ppermute | solution.py:25
  80.6 0.1 pad_maximum_fusion.1
  80.8 0.1 reshape.74
  80.8 4.8 %gather_fusion.3 = bf16[1536,256]{1,0:T(8,128)(2,1)S(1)} fusion(bf16[324,256]{1,0:T(8,128)(2,1)S(1)} %reshape.74, s32[2048]{0:T(1024)S(1)} %pad_clamp_fusion), kind=kCustom, calls=%fused_computation.3 | custom fusion | bytes 1579008 | tf_op jit(solution)/shard_map/gather | solution.py:58
  85.6 2.4 %fusion.2 = f32[12,128,256]{2,1,0:T(8,128)} fusion(bf16[12,384,128]{2,1,0:T(8,128)(2,1)S(1)} %scatter_fusion.1, bf16[12,128,256]{2,1,0:T(8,128)(2,1)S(1)} %bitcast.30), kind=kOutput, calls=%fused_computation.10 | convolution fusion | flops 605159424 | bytes 3538944 | tf_op jit(solution)/shard_map/ewk,ewr->ekr/dot_general | solution.py:62
  88.0 9.9 %scatter_custom_fusion.3 = f32[256,256]{1,0:T(8,128)} fusion(s32[1536]{0:T(1024)S(1)} %fusion.20, f32[1536,256]{1,0:T(8,128)} %bitcast.31, f32[]{:T(128)} %constant.10.clone.1), kind=kCustom, calls=%fused_computation.20 | custom fusion | flops 393216 | bytes 262656 | tf_op jit(solution)/shard_map/scatter-add | solution.py:68
  (11 shorter events, 0.1 us)
Async XLA Ops:
  0.0 8.7 %copy-start = (bf16[12,384,128]{2,1,0:T(8,128)(2,1)S(1)}, bf16[12,384,128]{2,1,0:T(8,128)(2,1)}, u32[]{:S(2)}) copy-start(bf16[12,384,128]{2,1,0:T(8,128)(2,1)} %param.9) | copy-start | bytes 3538948
  0.8 27.9 %collective-permute-start.2 = (bf16[1,16,256]{2,1,0:T(8,128)(2,1)S(1)}, bf16[1,16,256]{2,1,0:T(8,128)(2,1)S(1)}, u32[]{:S(2)}, u32[]{:S(2)}) collective-permute-start(bf16[1,16,256]{2,1,0:T(8,128)(2,1)S(1)} %get-tuple-element.11), channel_id=1, source_target_pairs={{0,128},{128,256},{256,384},{1,129},{129,257},{257,385},{2,130},{1... | collective-permute-start | bytes 24584 | tf_op jit(solution)/shard_map/ppermute | solution.py:22
  5.4 23.4 %collective-permute-start.3 = (bf16[1,16,256]{2,1,0:T(8,128)(2,1)S(1)}, bf16[1,16,256]{2,1,0:T(8,128)(2,1)S(1)}, u32[]{:S(2)}, u32[]{:S(2)}) collective-permute-start(bf16[1,16,256]{2,1,0:T(8,128)(2,1)S(1)} %get-tuple-element.12), channel_id=1, source_target_pairs={{128,0},{256,128},{384,256},{129,1},{257,129},{385,257},{130,2},{2... | collective-permute-start | bytes 24584 | tf_op jit(solution)/shard_map/ppermute | solution.py:25
  8.7 6.3 %copy-start.2 = (s32[12,128]{1,0:T(8,128)S(1)}, s32[12,128]{1,0:T(8,128)}, u32[]{:S(2)}) copy-start(s32[12,128]{1,0:T(8,128)} %param.13) | copy-start | bytes 18436
  8.7 6.3 %copy-start.3 = (s32[12,128]{1,0:T(8,128)S(1)}, s32[12,128]{1,0:T(8,128)}, u32[]{:S(2)}) copy-start(s32[12,128]{1,0:T(8,128)} %param.14) | copy-start | bytes 18436
  8.7 6.3 %copy-start.4 = (s32[3]{0:T(128)S(1)}, s32[3]{0:T(128)}, u32[]{:S(2)}) copy-start(s32[3]{0:T(128)} %param.12) | copy-start | bytes 40
  11.9 16.8 %copy-start.1 = (bf16[16,1,16,256]{3,2,1,0:T(8,128)(2,1)S(1)}, bf16[16,1,16,256]{3,2,1,0:T(8,128)(2,1)}, u32[]{:S(2)}) copy-start(bf16[16,1,16,256]{3,2,1,0:T(8,128)(2,1)} %param.15) | copy-start | bytes 393220
  12.5 8.3 %collective-permute-start = (bf16[3,384,128]{2,1,0:T(8,128)(2,1)S(1)}, bf16[3,384,128]{2,1,0:T(8,128)(2,1)S(1)}, u32[]{:S(2)}, u32[]{:S(2)}) collective-permute-start(bf16[3,384,128]{2,1,0:T(8,128)(2,1)S(1)} %gather_fusion), channel_id=1, source_target_pairs={{0,1},{1,0},{2,3},{3,2},{4,5},{5,4},{6,7},{7,6},{8,9},{9,8},{10,11... | collective-permute-start | bytes 884744 | tf_op jit(solution)/shard_map/ppermute | solution.py:14
  22.9 23.0 %collective-permute-start.1 = (bf16[3,384,128]{2,1,0:T(8,128)(2,1)}, bf16[3,384,128]{2,1,0:T(8,128)(2,1)}, u32[]{:S(2)}, u32[]{:S(2)}) collective-permute-start(bf16[3,384,128]{2,1,0:T(8,128)(2,1)} %gather_fusion.1), channel_id=1, source_target_pairs={{0,32},{32,0},{1,33},{33,1},{2,34},{34,2},{3,35},{35,3},{4,36},{36... | collective-permute-start | bytes 884744 | tf_op jit(solution)/shard_map/ppermute | solution.py:14
  28.8 6.3 %collective-permute-start.4 = (bf16[18,1,256]{2,1,0:T(2,128)(2,1)S(1)}, bf16[18,1,256]{2,1,0:T(2,128)(2,1)S(1)}, u32[]{:S(2)}, u32[]{:S(2)}) collective-permute-start(bf16[18,1,256]{2,1,0:T(2,128)(2,1)S(1)} %get-tuple-element.7), channel_id=1, source_target_pairs={{0,1},{1,2},{2,3},{3,4},{4,5},{5,6},{6,7},{7,8},{8,9},{9,10},{10,1... | collective-permute-start | bytes 27656 | tf_op jit(solution)/shard_map/ppermute | solution.py:22
  33.1 7.8 %collective-permute-start.5 = (bf16[18,1,256]{2,1,0:T(2,128)(2,1)S(1)}, bf16[18,1,256]{2,1,0:T(2,128)(2,1)S(1)}, u32[]{:S(2)}, u32[]{:S(2)}) collective-permute-start(bf16[18,1,256]{2,1,0:T(2,128)(2,1)S(1)} %get-tuple-element.8), channel_id=1, source_target_pairs={{1,0},{2,1},{3,2},{4,3},{5,4},{6,5},{7,6},{8,7},{9,8},{10,9},{11,1... | collective-permute-start | bytes 27656 | tf_op jit(solution)/shard_map/ppermute | solution.py:25
  59.2 8.6 %collective-permute-start.6 = (bf16[1,16,256]{2,1,0:T(8,128)(2,1)S(1)}, bf16[1,16,256]{2,1,0:T(8,128)(2,1)S(1)}, u32[]{:S(2)}, u32[]{:S(2)}) collective-permute-start(bf16[1,16,256]{2,1,0:T(8,128)(2,1)S(1)} %get-tuple-element.9), channel_id=1, source_target_pairs={{0,128},{128,256},{256,384},{1,129},{129,257},{257,385},{2,130},{1... | collective-permute-start | bytes 24584 | tf_op jit(solution)/shard_map/ppermute | solution.py:22
  65.9 5.0 %collective-permute-start.7 = (bf16[1,16,256]{2,1,0:T(8,128)(2,1)S(1)}, bf16[1,16,256]{2,1,0:T(8,128)(2,1)S(1)}, u32[]{:S(2)}, u32[]{:S(2)}) collective-permute-start(bf16[1,16,256]{2,1,0:T(8,128)(2,1)S(1)} %get-tuple-element.10), channel_id=1, source_target_pairs={{128,0},{256,128},{384,256},{129,1},{257,129},{385,257},{130,2},{2... | collective-permute-start | bytes 24584 | tf_op jit(solution)/shard_map/ppermute | solution.py:25
  70.9 5.3 %collective-permute-start.8 = (bf16[18,1,256]{2,1,0:T(2,128)(2,1)S(1)}, bf16[18,1,256]{2,1,0:T(2,128)(2,1)S(1)}, u32[]{:S(2)}, u32[]{:S(2)}) collective-permute-start(bf16[18,1,256]{2,1,0:T(2,128)(2,1)S(1)} %get-tuple-element.5), channel_id=1, source_target_pairs={{0,1},{1,2},{2,3},{3,4},{4,5},{5,6},{6,7},{7,8},{8,9},{9,10},{10,1... | collective-permute-start | bytes 27656 | tf_op jit(solution)/shard_map/ppermute | solution.py:22
  72.8 7.8 %collective-permute-start.9 = (bf16[18,1,256]{2,1,0:T(2,128)(2,1)S(1)}, bf16[18,1,256]{2,1,0:T(2,128)(2,1)S(1)}, u32[]{:S(2)}, u32[]{:S(2)}) collective-permute-start(bf16[18,1,256]{2,1,0:T(2,128)(2,1)S(1)} %get-tuple-element.6), channel_id=1, source_target_pairs={{1,0},{2,1},{3,2},{4,3},{5,4},{6,5},{7,6},{8,7},{9,8},{10,9},{11,1... | collective-permute-start | bytes 27656 | tf_op jit(solution)/shard_map/ppermute | solution.py:25
where the time goes:
time: 98.3 us; the launch traced here: 97.9 us
  starting transfers between devices  34.8 us (35%)
  other arithmetic  21 us (21%)
  waiting for transfers between devices  19.1 us (19%)
  local copies, waits for them, and re-layouts  14.7 us (15%)
  matrix products  7.87 us (8%)
    scatter-add x2, other arithmetic, apply_field(): result = jnp.zeros((rows_x * rows_z, columns), jnp.float32).at[targets].a...  19.2 us
    ppermute x4, starting transfers between devices, with_halo(): lax.ppermute(lax.slice_in_dim(block, block.shape[dim] - width, None, axis...  17.4 us
    ppermute x4, waiting for transfers between devices, with_halo(): lax.ppermute(lax.slice_in_dim(block, 0, width, axis=dim), axis, backward)  13.3 us
    gather x2, local copies, waits for them, and re-layouts, apply_field(): gathered = flattened[trace_index]  9.52 us
    ppermute x4, starting transfers between devices, with_halo(): lax.ppermute(lax.slice_in_dim(block, 0, width, axis=dim), axis, backward)  9.12 us
    ppermute x2, starting transfers between devices, swapped(): return lax.ppermute(block, axis, route)  8.26 us
    ppermute x2, waiting for transfers between devices, swapped(): return lax.ppermute(block, axis, route)  5.75 us
    dot_general x2, matrix products, apply_field(): jnp.einsum('ewk,ewr->ekr', operator, tested, preferred_element_type=jnp.f...  4.72 us
  transfers between devices with their start and end apart: 10, of which 4 were waited for; matrix products, arithmetic and copies ran while one was open for 13% of the time, Pallas kernels for 0%

commit v1 on v0

v1 whole, which is shorter than its diff:
```python
import functools

import jax
import jax.numpy as jnp
from jax import lax
from jax.experimental import pallas as pl
from jax.experimental.pallas import tpu as pltpu
from jax.sharding import PartitionSpec as P

BF16 = jnp.bfloat16
F32 = jnp.float32
I32 = jnp.int32
HBM = pl.BlockSpec(memory_space=pltpu.MemorySpace.HBM)
VMEM = pl.BlockSpec(memory_space=pltpu.MemorySpace.VMEM)
SMEM = pl.BlockSpec(memory_space=pltpu.MemorySpace.SMEM)


def params(mebibytes):
    return pltpu.CompilerParams(vmem_limit_bytes=mebibytes << 20)


def swap_route(count, bit):
    return [(low, low ^ (1 << bit)) for low in range(count) if low ^ (1 << bit) < count]


def dot(a, b, dims):
    return lax.dot_general(a, b, (dims, ((), ())), preferred_element_type=F32)


def halves(value):
    high = value.astype(BF16)
    return high, (value - high.astype(F32)).astype(BF16)


def gram_of(factor, coupling, order):
    rows = factor.shape[0]
    product = dot(factor, coupling, ((1,), (0,)))
    keep = lax.broadcasted_iota(I32, product.shape, 0) < rows * (2 + order) // 4
    operator = jnp.where(keep, product, 0.0).astype(BF16)
    return dot(operator, operator, ((0,), (0,)))


def one_hot(index, rows):
    hit = lax.broadcasted_iota(I32, (rows, index.shape[1]), 0) == index
    return jnp.where(hit, 1.0, 0.0).astype(BF16)


def cell_of(cell, fx, fz):
    pitch = fz + 2
    row = jnp.zeros_like(cell)
    for edge in range(1, fx + 2):
        row = row + jnp.where(cell >= edge * pitch, 1, 0)
    column = cell - row * pitch
    own = fx * fz
    out = (row - 1) * fz + column - 1
    out = jnp.where(column == fz + 1, own + 2 * fz + fx + row - 1, out)
    out = jnp.where(column == 0, own + 2 * fz + row - 1, out)
    out = jnp.where(row == fx + 1, own + fz + column - 1, out)
    return jnp.where(row == 0, own + column - 1, out)


def matrix_of(elements, own, padded):
    left, right = [], []
    for gram, reads, writes in elements:
        scatter, gather = one_hot(writes, own), one_hot(reads, padded)
        if gram.dtype == F32:
            spread = sum(dot(scatter, half, ((1,), (0,))) for half in halves(gram))
            parts = halves(spread)
        else:
            parts = [dot(scatter, gram, ((1,), (0,))).astype(BF16)]
        left += parts
        right += [gather] * len(parts)
    return dot(jnp.concatenate(left, axis=1), jnp.concatenate(right, axis=1), ((1,), (1,)))


def given_kernel(f, s, order, factor, coupling, given_f, given_s, fbuf, cbuf, sem):
    moves = f.shape[0]
    slots = [f[i] for i in range(moves)] + [s[i] for i in range(moves)]
    copies = []
    for i, slot in enumerate(slots):
        pair = (
            pltpu.make_async_copy(factor.at[slot], fbuf.at[i], sem.at[i, 0]),
            pltpu.make_async_copy(coupling.at[slot], cbuf.at[i], sem.at[i, 1]),
        )
        for copy in pair:
            copy.start()
        copies.append(pair)
    for i, slot in enumerate(slots):
        for copy in copies[i]:
            copy.wait()
        out = given_f if i < moves else given_s
        out[i % moves] = gram_of(fbuf[i], cbuf[i], order[slot]).astype(BF16)


def store_edges(field, edges, fx, fz):
    last, first, right, left = edges
    own = fx * fz
    last[...] = field[own - fz :, :]
    first[...] = field[:fz, :]
    row = lax.broadcasted_iota(I32, (2 * fx, own), 0)
    wanted = jnp.where(row < fx, row * fz + fz - 1, (row - fx) * fz)
    hit = lax.broadcasted_iota(I32, (2 * fx, own), 1) == wanted
    sides = dot(jnp.where(hit, 1.0, 0.0).astype(BF16), field, ((1,), (0,))).astype(BF16)
    right[...] = sides[:fx]
    left[...] = sides[fx:]


def kept_kernel(
    fx, fz, f, s, order, reads, writes, factor, coupling, traces,
    part, e0, e1, e2, e3, fbuf, cbuf, kept, sem,
):
    slots, moves = reads.shape[0], f.shape[0]
    most = slots - moves
    for i in range(slots):
        kept[i] = 0
    count = jnp.int32(0)
    for slot in range(slots):
        moved = f[0] == slot
        for i in range(moves):
            moved = moved | (f[i] == slot) | (s[i] == slot)
        kept[count] = slot
        count = count + jnp.where(moved, 0, 1)
    copies = []
    for i in range(most):
        slot = kept[i]
        pair = (
            pltpu.make_async_copy(factor.at[slot], fbuf.at[i], sem.at[i, 0]),
            pltpu.make_async_copy(coupling.at[slot], cbuf.at[i], sem.at[i, 1]),
        )
        for copy in pair:
            copy.start()
        copies.append(pair)
    store_edges(traces[...], (e0, e1, e2, e3), fx, fz)
    elements = []
    for i in range(most):
        slot = kept[i]
        valid = i < count
        read = jnp.where(valid, cell_of(reads[pl.ds(slot, 1), :], fx, fz), -1)
        write = jnp.where(valid, writes[pl.ds(slot, 1), :], -1)
        for copy in copies[i]:
            copy.wait()
        elements.append((gram_of(fbuf[i], cbuf[i], order[slot]), read, write))
    part[...] = matrix_of(elements, fx * fz, part.shape[1])


def relay_kernel(f, s, given_s, got, out):
    moves = f.shape[0]
    for i in range(moves):
        value = given_s[i]
        for j in range(moves):
            value = jnp.where(s[i] == f[j], got[j], value)
        out[i] = value


def halo_dot(parts, field, halos, own):
    frame = jnp.concatenate([halo[...] for halo in halos], axis=0)
    total = 0.0
    for part in parts:
        total = total + dot(part[:, :own], field, ((1,), (0,)))
        total = total + dot(part[:, own : own + frame.shape[0]], frame, ((1,), (0,)))
    return total


def first_kernel(
    fx, fz, f, s, reads, writes, got_f, got_s, part, traces, h0, h1, h2, h3,
    matrix, first, e0, e1, e2, e3,
):
    own, moves = fx * fz, f.shape[0]
    elements = []
    for i in range(moves):
        slot = s[i]
        read = cell_of(reads[pl.ds(slot, 1), :], fx, fz)
        elements.append((got_s[i], read, writes[pl.ds(slot, 1), :]))
    for i in range(moves):
        slot = f[i]
        stays = slot != s[0]
        for j in range(1, moves):
            stays = stays & (slot != s[j])
        read = jnp.where(stays, cell_of(reads[pl.ds(slot, 1), :], fx, fz), -1)
        write = jnp.where(stays, writes[pl.ds(slot, 1), :], -1)
        elements.append((got_f[i], read, write))
    whole = part[...] + matrix_of(elements, own, part.shape[1])
    parts = halves(whole)
    matrix[0], matrix[1] = parts
    field = halo_dot(parts, traces[...], (h0, h1, h2, h3), own).astype(BF16)
    first[...] = field
    store_edges(field, (e0, e1, e2, e3), fx, fz)


def second_kernel(own, matrix, first, h0, h1, h2, h3, out):
    out[...] = halo_dot((matrix[0], matrix[1]), first[...], (h0, h1, h2, h3), own)


def exchange(edges):
    last, first, right, left = edges
    out = []
    for axis, up, down in (("gx", last, first), ("gz", right, left)):
        count = lax.axis_size(axis)
        forward = [(i, i + 1) for i in range(count - 1)]
        backward = [(target, source) for source, target in forward]
        out += [lax.ppermute(up, axis, forward), lax.ppermute(down, axis, backward)]
    return out


def body(
    gram_factor, coupling, order_class, first_moves, second_moves, trace_index, owner_index, traces
):
    slots, width, unknowns = coupling.shape
    moves = first_moves.shape[0]
    fx, _, fz, columns = traces.shape
    own = fx * fz
    padded = -(-(own + 2 * (fx + fz)) // 128) * 128
    most = slots - moves
    field = traces.reshape(own, columns)
    grams = jax.ShapeDtypeStruct((moves, unknowns, unknowns), BF16)
    edges = [jax.ShapeDtypeStruct((n, columns), BF16) for n in (fz, fz, fx, fx)]

    given_f, given_s = pl.pallas_call(
        given_kernel,
        out_shape=(grams, grams),
        in_specs=[SMEM] * 3 + [HBM] * 2,
        out_specs=(VMEM, VMEM),
        scratch_shapes=[
            pltpu.VMEM((2 * moves, width, width), BF16),
            pltpu.VMEM((2 * moves, width, unknowns), BF16),
            pltpu.SemaphoreType.DMA((2 * moves, 2)),
        ],
        compiler_params=params(53),
        name="given",
    )(first_moves, second_moves, order_class, gram_factor, coupling)

    given_f, given_s, field = lax.optimization_barrier((given_f, given_s, field))
    got_f = lax.ppermute(given_f, "gz", swap_route(lax.axis_size("gz"), 0))

    part, *trace_edges = pl.pallas_call(
        functools.partial(kept_kernel, fx, fz),
        out_shape=(jax.ShapeDtypeStruct((own, padded), F32), *edges),
        in_specs=[SMEM] * 3 + [VMEM] * 2 + [HBM] * 2 + [VMEM],
        out_specs=(VMEM,) * 5,
        scratch_shapes=[
            pltpu.VMEM((most, width, width), BF16),
            pltpu.VMEM((most, width, unknowns), BF16),
            pltpu.SMEM((slots,), I32),
            pltpu.SemaphoreType.DMA((most, 2)),
        ],
        cost_estimate=pl.CostEstimate(
            flops=2 * most * width * unknowns * (width + unknowns),
            bytes_accessed=2 * most * width * (width + unknowns),
            transcendentals=0,
        ),
        compiler_params=params(53),
        name="kept",
    )(
        first_moves, second_moves, order_class, trace_index, owner_index,
        gram_factor, coupling, field,
    )

    given_s, part = lax.optimization_barrier((given_s, part))
    relayed = pl.pallas_call(
        relay_kernel,
        out_shape=grams,
        in_specs=[SMEM] * 2 + [VMEM] * 2,
        out_specs=VMEM,
        compiler_params=params(2),
        name="relay",
    )(first_moves, second_moves, given_s, got_f)
    both = lax.axis_size("gy") * lax.axis_size("gz")
    second_bit = lax.axis_size("gz").bit_length() - 1
    got_s = lax.ppermute(relayed, ("gy", "gz"), swap_route(both, second_bit))

    halos = exchange(trace_edges)
    matrix, first, *first_edges = pl.pallas_call(
        functools.partial(first_kernel, fx, fz),
        out_shape=(
            jax.ShapeDtypeStruct((2, own, padded), BF16),
            jax.ShapeDtypeStruct((own, columns), BF16),
            *edges,
        ),
        in_specs=[SMEM] * 2 + [VMEM] * 10,
        out_specs=(VMEM,) * 6,
        compiler_params=params(12),
        name="first",
    )(
        first_moves, second_moves, trace_index, owner_index, got_f, got_s, part, field, *halos
    )

    halos = exchange(first_edges)
    second = pl.pallas_call(
        functools.partial(second_kernel, own),
        out_shape=jax.ShapeDtypeStruct((own, columns), F32),
        in_specs=[VMEM] * 6,
        out_specs=VMEM,
        compiler_params=params(6),
        name="second",
    )(matrix, first, *halos)
    return second.reshape(traces.shape)


def solution(mesh):
    return jax.shard_map(
        body,
        mesh=mesh,
        in_specs=(
            P(("gx", "gy", "gz"), None, None),
            P(("gx", "gy", "gz"), None, None),
            P(("gx", "gy", "gz")),
            P(("gx", "gy", "gz")),
            P(("gx", "gy", "gz")),
            P(("gx", "gy", "gz"), None),
            P(("gx", "gy", "gz"), None),
            P("gx", "gy", "gz", None),
        ),
        out_specs=P("gx", "gy", "gz", None),
        check_vma=False,
    )
```

time: 98.3 us -> 61.4 us (0.62)
  the two profiles are of different devices: /device:TPU:31 before, /device:TPU:94 now
where the time goes in v1:
time: 61.4 us; the launch traced here: 61 us
  starting transfers between devices  33 us (54%)
  Pallas kernels  14 us (23%)
  waiting for transfers between devices  11.8 us (19%)
  local copies, waits for them, and re-layouts  2.01 us (3%)
    ppermute x8, starting transfers between devices, exchange(): out += [lax.ppermute(up, axis, forward), lax.ppermute(down, axis, backward)]  24.2 us
    ppermute x8, waiting for transfers between devices, exchange(): out += [lax.ppermute(up, axis, forward), lax.ppermute(down, axis, backward)]  11.8 us
    pallas_call x1, Pallas kernels, body(): pl.pallas_call(functools.partial(kept_kernel, fx, fz), out_shape=(jax.Sha...  6.58 us
    ppermute x1, starting transfers between devices, body(): got_s = lax.ppermute(relayed, ('gy', 'gz'), swap_route(both, second_bit))  6.09 us
    pallas_call x1, Pallas kernels, body(): pl.pallas_call(given_kernel, out_shape=(grams, grams), in_specs=[SMEM] *...  4.21 us
    ppermute x1, starting transfers between devices, body(): got_f = lax.ppermute(given_f, 'gz', swap_route(lax.axis_size('gz'), 0))  2.74 us
    unnamed x12, local copies, waits for them, and re-layouts  2.01 us
    pallas_call x1, Pallas kernels, body(): pl.pallas_call(functools.partial(first_kernel, fx, fz), out_shape=(jax.Sh...  1.64 us
  transfers between devices with their start and end apart: 10, of which 2 were waited for; matrix products, arithmetic and copies ran while one was open for 0% of the time, Pallas kernels for 11%

profile of v1, /device:TPU:94, one launch (start us, length us, event | category | flops | bytes accessed | tf_op | source)
XLA Modules:
  0.0 61.0 jit_solution(3791013914711147004)
XLA Ops:
  0.0 0.0 copy-start
  0.0 0.0 copy-start.2
  0.0 0.0 copy-start.3
  0.0 0.7 %copy-done.3 = s32[3]{0:T(128)S(1)} copy-done((s32[3]{0:T(128)S(1)}, s32[3]{0:T(128)}, u32[]{:S(2)}) %copy-start.3) | copy-done | bytes 36
  0.7 0.0 copy-start.4
  0.7 0.7 %copy-done.4 = s32[3]{0:T(128)S(1)} copy-done((s32[3]{0:T(128)S(1)}, s32[3]{0:T(128)}, u32[]{:S(2)}) %copy-start.4) | copy-done | bytes 36
  1.4 0.0 copy-start.5
  1.4 0.7 %copy-done.5 = s32[12]{0:T(128)S(1)} copy-done((s32[12]{0:T(128)S(1)}, s32[12]{0:T(128)}, u32[]{:S(2)}) %copy-start.5) | copy-done | bytes 72
  2.0 0.0 copy-start.1
  2.0 4.2 %given.1 = (bf16[3,128,128]{2,1,0:T(8,128)(2,1)S(1)}, bf16[3,128,128]{2,1,0:T(8,128)(2,1)S(1)}) custom-call(s32[3]{0:T(128)S(1)} %copy-done.3, s32[3]{0:T(128)S(1)} %copy-done.4, s32[12]{0:T(128)S(1)} %copy-done.5, bf16[12,384,384]{2,1,0:T(8,128)(2,1)} %factor.3, bf16[12,384,128]{2,1,0:T(8,128)(2,1)} %coupling.3), custom_call_target="tpu_custom_call" | custom-call | tf_op jit(solution)/shard_map/given/pallas_call | solution.py:218
  6.2 2.7 %collective-permute-start = (bf16[3,128,128]{2,1,0:T(8,128)(2,1)S(1)}, bf16[3,128,128]{2,1,0:T(8,128)(2,1)S(1)}, u32[]{:S(2)}, u32[]{:S(2)}) collective-permute-start(bf16[3,128,128]{2,1,0:T(8,128)(2,1)S(1)} %get-tuple-element.25), channel_id=1, source_target_pairs={{0,1},{1,0},{2,3},{3,2},{4,5},{5,4},{6,7},{7,6},{8,9},{9,8},{10,11... | collective-permute-start | bytes 294920 | tf_op jit(solution)/shard_map/ppermute | solution.py:233
  9.0 0.0 copy-done
  9.0 0.0 copy-done.2
  9.0 0.0 copy-done.1
  9.0 6.6 %kept.1 = (f32[256,384]{1,0:T(8,128)S(1)}, bf16[16,256]{1,0:T(8,128)(2,1)S(1)}, bf16[16,256]{1,0:T(8,128)(2,1)S(1)}, bf16[16,256]{1,0:T(8,128)(2,1)S(1)}, bf16[16,256]{1,0:T(8,128)(2,1)S(1)}) custom-call(s32[3]{0:T(128)S(1)} %copy-done.3, s32[3]{0:T(128)S(1)} %copy-done.4, s32[12]{0:T(128)S(1)} %copy-done.5, s32[12,128]{1,0:T(8,128)S(1)} %copy-done.1, ...), custom_call_target="tpu_custom_call" | custom-call | flops 452984832 | bytes 3538944 | tf_op jit(solution)/shard_map/kept/pallas_call | solution.py:235
  15.6 0.0 collective-permute-done.got.got_f
  15.6 0.6 relay.1
  16.2 6.1 %collective-permute-start.1 = (bf16[3,128,128]{2,1,0:T(8,128)(2,1)S(1)}, bf16[3,128,128]{2,1,0:T(8,128)(2,1)S(1)}, u32[]{:S(2)}, u32[]{:S(2)}) collective-permute-start(bf16[3,128,128]{2,1,0:T(8,128)(2,1)S(1)} %relay.1), channel_id=1, source_target_pairs={{0,32},{1,33},{2,34},{3,35},{4,36},{5,37},{6,38},{7,39},{8,40},{9,... | collective-permute-start | bytes 294920 | tf_op jit(solution)/shard_map/ppermute | solution.py:269
  22.3 1.9 %collective-permute-start.2 = (bf16[16,256]{1,0:T(8,128)(2,1)S(1)}, bf16[16,256]{1,0:T(8,128)(2,1)S(1)}, u32[]{:S(2)}, u32[]{:S(2)}) collective-permute-start(bf16[16,256]{1,0:T(8,128)(2,1)S(1)} %get-tuple-element.31), channel_id=1, source_target_pairs={{0,128},{128,256},{256,384},{1,129},{129,257},{257,385},{2,130},{1... | collective-permute-start | bytes 24584 | tf_op jit(solution)/shard_map/ppermute | solution.py:201
  24.2 3.6 %collective-permute-start.3 = (bf16[16,256]{1,0:T(8,128)(2,1)S(1)}, bf16[16,256]{1,0:T(8,128)(2,1)S(1)}, u32[]{:S(2)}, u32[]{:S(2)}) collective-permute-start(bf16[16,256]{1,0:T(8,128)(2,1)S(1)} %get-tuple-element.32), channel_id=1, source_target_pairs={{128,0},{256,128},{384,256},{129,1},{257,129},{385,257},{130,2},{2... | collective-permute-start | bytes 24584 | tf_op jit(solution)/shard_map/ppermute | solution.py:201
  27.9 5.3 %collective-permute-start.4 = (bf16[16,256]{1,0:T(8,128)(2,1)S(1)}, bf16[16,256]{1,0:T(8,128)(2,1)S(1)}, u32[]{:S(2)}, u32[]{:S(2)}) collective-permute-start(bf16[16,256]{1,0:T(8,128)(2,1)S(1)} %get-tuple-element.33), channel_id=1, source_target_pairs={{0,1},{1,2},{2,3},{3,4},{4,5},{5,6},{6,7},{7,8},{8,9},{9,10},{10,1... | collective-permute-start | bytes 24584 | tf_op jit(solution)/shard_map/ppermute | solution.py:201
  33.1 1.9 %collective-permute-start.5 = (bf16[16,256]{1,0:T(8,128)(2,1)S(1)}, bf16[16,256]{1,0:T(8,128)(2,1)S(1)}, u32[]{:S(2)}, u32[]{:S(2)}) collective-permute-start(bf16[16,256]{1,0:T(8,128)(2,1)S(1)} %get-tuple-element.34), channel_id=1, source_target_pairs={{1,0},{2,1},{3,2},{4,3},{5,4},{6,5},{7,6},{8,7},{9,8},{10,9},{11,1... | collective-permute-start | bytes 24584 | tf_op jit(solution)/shard_map/ppermute | solution.py:201
  35.1 0.0 collective-permute-done.2.h0
  35.1 0.0 collective-permute-done.3.h1
  35.1 0.0 collective-permute-done.4.h2
  35.1 6.9 %collective-permute-done.5.h3 = bf16[16,256]{1,0:T(8,128)(2,1)S(1)} collective-permute-done((bf16[16,256]{1,0:T(8,128)(2,1)S(1)}, bf16[16,256]{1,0:T(8,128)(2,1)S(1)}, u32[]{:S(2)}, u32[]{:S(2)}) %collective-permute-start.5) | collective-permute-done | bytes 8224 | tf_op jit(solution)/shard_map/ppermute | solution.py:201
  42.0 0.0 collective-permute-done.1.got_s
  42.0 1.6 %first.1 = (bf16[2,256,384]{2,1,0:T(8,128)(2,1)S(1)}, bf16[256,256]{1,0:T(8,128)(2,1)S(1)}, bf16[16,256]{1,0:T(8,128)(2,1)S(1)}, bf16[16,256]{1,0:T(8,128)(2,1)S...) custom-call(s32[3]{0:T(128)S(1)} %copy-done.3, s32[3]{0:T(128)S(1)} %copy-done.4, s32[12,128]{1,0:T(8,128)S(1)} %copy-done.1, ...), custom_call_target="tpu_custom_call" | custom-call | tf_op jit(solution)/shard_map/first/pallas_call | solution.py:272
  43.7 1.9 %collective-permute-start.6 = (bf16[16,256]{1,0:T(8,128)(2,1)S(1)}, bf16[16,256]{1,0:T(8,128)(2,1)S(1)}, u32[]{:S(2)}, u32[]{:S(2)}) collective-permute-start(bf16[16,256]{1,0:T(8,128)(2,1)S(1)} %get-tuple-element.37), channel_id=1, source_target_pairs={{0,128},{128,256},{256,384},{1,129},{129,257},{257,385},{2,130},{1... | collective-permute-start | bytes 24584 | tf_op jit(solution)/shard_map/ppermute | solution.py:201
  45.6 3.6 %collective-permute-start.7 = (bf16[16,256]{1,0:T(8,128)(2,1)S(1)}, bf16[16,256]{1,0:T(8,128)(2,1)S(1)}, u32[]{:S(2)}, u32[]{:S(2)}) collective-permute-start(bf16[16,256]{1,0:T(8,128)(2,1)S(1)} %get-tuple-element.38), channel_id=1, source_target_pairs={{128,0},{256,128},{384,256},{129,1},{257,129},{385,257},{130,2},{2... | collective-permute-start | bytes 24584 | tf_op jit(solution)/shard_map/ppermute | solution.py:201
  49.2 1.9 %collective-permute-start.8 = (bf16[16,256]{1,0:T(8,128)(2,1)S(1)}, bf16[16,256]{1,0:T(8,128)(2,1)S(1)}, u32[]{:S(2)}, u32[]{:S(2)}) collective-permute-start(bf16[16,256]{1,0:T(8,128)(2,1)S(1)} %get-tuple-element.39), channel_id=1, source_target_pairs={{0,1},{1,2},{2,3},{3,4},{4,5},{5,6},{6,7},{7,8},{8,9},{9,10},{10,1... | collective-permute-start | bytes 24584 | tf_op jit(solution)/shard_map/ppermute | solution.py:201
  51.2 3.9 %collective-permute-start.9 = (bf16[16,256]{1,0:T(8,128)(2,1)S(1)}, bf16[16,256]{1,0:T(8,128)(2,1)S(1)}, u32[]{:S(2)}, u32[]{:S(2)}) collective-permute-start(bf16[16,256]{1,0:T(8,128)(2,1)S(1)} %get-tuple-element.40), channel_id=1, source_target_pairs={{1,0},{2,1},{3,2},{4,3},{5,4},{6,5},{7,6},{8,7},{9,8},{10,9},{11,1... | collective-permute-start | bytes 24584 | tf_op jit(solution)/shard_map/ppermute | solution.py:201
  55.1 0.0 collective-permute-done.6.h0
  55.1 0.0 collective-permute-done.7.h1
  55.1 0.0 collective-permute-done.8.h2
  55.1 4.9 %collective-permute-done.9.h3 = bf16[16,256]{1,0:T(8,128)(2,1)S(1)} collective-permute-done((bf16[16,256]{1,0:T(8,128)(2,1)S(1)}, bf16[16,256]{1,0:T(8,128)(2,1)S(1)}, u32[]{:S(2)}, u32[]{:S(2)}) %collective-permute-start.9) | collective-permute-done | bytes 8224 | tf_op jit(solution)/shard_map/ppermute | solution.py:201
  60.0 1.0 %second.1 = f32[256,256]{1,0:T(8,128)} custom-call(bf16[2,256,384]{2,1,0:T(8,128)(2,1)S(1)} %get-tuple-element.35.matrix, bf16[256,256]{1,0:T(8,128)(2,1)S(1)} %get-tuple-element.36.first, bf16[16,256]{1,0:T(8,128)(2,1)S(1)} %collective-permute-done.6.h0, bf16[16,256]{1,0:T(8,128)(2,1)S(1)} %collective-permute-done.7.h1, ...), custom_call_target="tpu_custom_call" | custom-call | tf_op jit(solution)/shard_map/second/pallas_call | solution.py:288
Async XLA Ops:
  0.0 9.0 %copy-start = (bf16[16,1,16,256]{3,2,1,0:T(8,128)(2,1)S(1)}, bf16[16,1,16,256]{3,2,1,0:T(8,128)(2,1)}, u32[]{:S(2)}) copy-start(bf16[16,1,16,256]{3,2,1,0:T(8,128)(2,1)} %param.15) | copy-start | bytes 393220
  0.0 9.0 %copy-start.2 = (s32[12,128]{1,0:T(8,128)S(1)}, s32[12,128]{1,0:T(8,128)}, u32[]{:S(2)}) copy-start(s32[12,128]{1,0:T(8,128)} %writes.3) | copy-start | bytes 18436
  0.0 0.7 %copy-start.3 = (s32[3]{0:T(128)S(1)}, s32[3]{0:T(128)}, u32[]{:S(2)}) copy-start(s32[3]{0:T(128)} %f.7) | copy-start | bytes 40
  0.7 0.7 %copy-start.4 = (s32[3]{0:T(128)S(1)}, s32[3]{0:T(128)}, u32[]{:S(2)}) copy-start(s32[3]{0:T(128)} %s.7) | copy-start | bytes 40
  1.4 0.7 %copy-start.5 = (s32[12]{0:T(128)S(1)}, s32[12]{0:T(128)}, u32[]{:S(2)}) copy-start(s32[12]{0:T(128)} %order.3) | copy-start | bytes 148
  2.0 7.0 %copy-start.1 = (s32[12,128]{1,0:T(8,128)S(1)}, s32[12,128]{1,0:T(8,128)}, u32[]{:S(2)}) copy-start(s32[12,128]{1,0:T(8,128)} %reads.3) | copy-start | bytes 18436
  6.2 9.4 %collective-permute-start = (bf16[3,128,128]{2,1,0:T(8,128)(2,1)S(1)}, bf16[3,128,128]{2,1,0:T(8,128)(2,1)S(1)}, u32[]{:S(2)}, u32[]{:S(2)}) collective-permute-start(bf16[3,128,128]{2,1,0:T(8,128)(2,1)S(1)} %get-tuple-element.25), channel_id=1, source_target_pairs={{0,1},{1,0},{2,3},{3,2},{4,5},{5,4},{6,7},{7,6},{8,9},{9,8},{10,11... | collective-permute-start | bytes 294920 | tf_op jit(solution)/shard_map/ppermute | solution.py:233
  16.2 25.8 %collective-permute-start.1 = (bf16[3,128,128]{2,1,0:T(8,128)(2,1)S(1)}, bf16[3,128,128]{2,1,0:T(8,128)(2,1)S(1)}, u32[]{:S(2)}, u32[]{:S(2)}) collective-permute-start(bf16[3,128,128]{2,1,0:T(8,128)(2,1)S(1)} %relay.1), channel_id=1, source_target_pairs={{0,32},{1,33},{2,34},{3,35},{4,36},{5,37},{6,38},{7,39},{8,40},{9,... | collective-permute-start | bytes 294920 | tf_op jit(solution)/shard_map/ppermute | solution.py:269
  22.3 12.8 %collective-permute-start.2 = (bf16[16,256]{1,0:T(8,128)(2,1)S(1)}, bf16[16,256]{1,0:T(8,128)(2,1)S(1)}, u32[]{:S(2)}, u32[]{:S(2)}) collective-permute-start(bf16[16,256]{1,0:T(8,128)(2,1)S(1)} %get-tuple-element.31), channel_id=1, source_target_pairs={{0,128},{128,256},{256,384},{1,129},{129,257},{257,385},{2,130},{1... | collective-permute-start | bytes 24584 | tf_op jit(solution)/shard_map/ppermute | solution.py:201
  24.2 10.9 %collective-permute-start.3 = (bf16[16,256]{1,0:T(8,128)(2,1)S(1)}, bf16[16,256]{1,0:T(8,128)(2,1)S(1)}, u32[]{:S(2)}, u32[]{:S(2)}) collective-permute-start(bf16[16,256]{1,0:T(8,128)(2,1)S(1)} %get-tuple-element.32), channel_id=1, source_target_pairs={{128,0},{256,128},{384,256},{129,1},{257,129},{385,257},{130,2},{2... | collective-permute-start | bytes 24584 | tf_op jit(solution)/shard_map/ppermute | solution.py:201
  27.9 7.2 %collective-permute-start.4 = (bf16[16,256]{1,0:T(8,128)(2,1)S(1)}, bf16[16,256]{1,0:T(8,128)(2,1)S(1)}, u32[]{:S(2)}, u32[]{:S(2)}) collective-permute-start(bf16[16,256]{1,0:T(8,128)(2,1)S(1)} %get-tuple-element.33), channel_id=1, source_target_pairs={{0,1},{1,2},{2,3},{3,4},{4,5},{5,6},{6,7},{7,8},{8,9},{9,10},{10,1... | collective-permute-start | bytes 24584 | tf_op jit(solution)/shard_map/ppermute | solution.py:201
  33.1 8.9 %collective-permute-start.5 = (bf16[16,256]{1,0:T(8,128)(2,1)S(1)}, bf16[16,256]{1,0:T(8,128)(2,1)S(1)}, u32[]{:S(2)}, u32[]{:S(2)}) collective-permute-start(bf16[16,256]{1,0:T(8,128)(2,1)S(1)} %get-tuple-element.34), channel_id=1, source_target_pairs={{1,0},{2,1},{3,2},{4,3},{5,4},{6,5},{7,6},{8,7},{9,8},{10,9},{11,1... | collective-permute-start | bytes 24584 | tf_op jit(solution)/shard_map/ppermute | solution.py:201
  43.7 11.4 %collective-permute-start.6 = (bf16[16,256]{1,0:T(8,128)(2,1)S(1)}, bf16[16,256]{1,0:T(8,128)(2,1)S(1)}, u32[]{:S(2)}, u32[]{:S(2)}) collective-permute-start(bf16[16,256]{1,0:T(8,128)(2,1)S(1)} %get-tuple-element.37), channel_id=1, source_target_pairs={{0,128},{128,256},{256,384},{1,129},{129,257},{257,385},{2,130},{1... | collective-permute-start | bytes 24584 | tf_op jit(solution)/shard_map/ppermute | solution.py:201
  45.6 9.5 %collective-permute-start.7 = (bf16[16,256]{1,0:T(8,128)(2,1)S(1)}, bf16[16,256]{1,0:T(8,128)(2,1)S(1)}, u32[]{:S(2)}, u32[]{:S(2)}) collective-permute-start(bf16[16,256]{1,0:T(8,128)(2,1)S(1)} %get-tuple-element.38), channel_id=1, source_target_pairs={{128,0},{256,128},{384,256},{129,1},{257,129},{385,257},{130,2},{2... | collective-permute-start | bytes 24584 | tf_op jit(solution)/shard_map/ppermute | solution.py:201
  49.2 5.9 %collective-permute-start.8 = (bf16[16,256]{1,0:T(8,128)(2,1)S(1)}, bf16[16,256]{1,0:T(8,128)(2,1)S(1)}, u32[]{:S(2)}, u32[]{:S(2)}) collective-permute-start(bf16[16,256]{1,0:T(8,128)(2,1)S(1)} %get-tuple-element.39), channel_id=1, source_target_pairs={{0,1},{1,2},{2,3},{3,4},{4,5},{5,6},{6,7},{7,8},{8,9},{9,10},{10,1... | collective-permute-start | bytes 24584 | tf_op jit(solution)/shard_map/ppermute | solution.py:201
  51.2 8.9 %collective-permute-start.9 = (bf16[16,256]{1,0:T(8,128)(2,1)S(1)}, bf16[16,256]{1,0:T(8,128)(2,1)S(1)}, u32[]{:S(2)}, u32[]{:S(2)}) collective-permute-start(bf16[16,256]{1,0:T(8,128)(2,1)S(1)} %get-tuple-element.40), channel_id=1, source_target_pairs={{1,0},{2,1},{3,2},{4,3},{5,4},{6,5},{7,6},{8,7},{9,8},{10,9},{11,1... | collective-permute-start | bytes 24584 | tf_op jit(solution)/shard_map/ppermute | solution.py:201

commit v2 on v1

v2 whole, which is shorter than its diff:
```python
import functools

import jax
import jax.numpy as jnp
from jax import lax
from jax.experimental import pallas as pl
from jax.experimental.pallas import tpu as pltpu
from jax.sharding import PartitionSpec as P

BF16 = jnp.bfloat16
F32 = jnp.float32
I32 = jnp.int32
HBM = pl.BlockSpec(memory_space=pltpu.MemorySpace.HBM)
VMEM = pl.BlockSpec(memory_space=pltpu.MemorySpace.VMEM)
SMEM = pl.BlockSpec(memory_space=pltpu.MemorySpace.SMEM)


def params(mebibytes):
    return pltpu.CompilerParams(vmem_limit_bytes=mebibytes << 20)


def swap_route(count, bit):
    return [(low, low ^ (1 << bit)) for low in range(count) if low ^ (1 << bit) < count]


def dot(a, b, dims):
    return lax.dot_general(a, b, (dims, ((), ())), preferred_element_type=F32)


def halves(value):
    high = value.astype(BF16)
    return high, (value - high.astype(F32)).astype(BF16)


def gram_of(factor, coupling, order):
    rows = factor.shape[0]
    product = dot(factor, coupling, ((1,), (0,)))
    keep = lax.broadcasted_iota(I32, product.shape, 0) < rows * (2 + order) // 4
    operator = jnp.where(keep, product, 0.0).astype(BF16)
    return dot(operator, operator, ((0,), (0,)))


def one_hot(index, rows):
    hit = lax.broadcasted_iota(I32, (rows, index.shape[1]), 0) == index
    return jnp.where(hit, 1.0, 0.0).astype(BF16)


def parities():
    return lax.axis_index("gx") % 2, lax.axis_index("gz") % 2


def cell_of(cell, fx, fz):
    odd_x, odd_z = parities()
    pitch = fz + 2
    row = jnp.zeros_like(cell)
    for edge in range(1, fx + 2):
        row = row + jnp.where(cell >= edge * pitch, 1, 0)
    column = cell - row * pitch
    base_x = fx * fz
    base_z = base_x + 2 * fz
    out = (row - 1) * fz + column - 1
    out = jnp.where(column == fz + 1, base_z + odd_z * fx + row - 1, out)
    out = jnp.where(column == 0, base_z + (1 - odd_z) * fx + row - 1, out)
    out = jnp.where(row == fx + 1, base_x + odd_x * fz + column - 1, out)
    return jnp.where(row == 0, base_x + (1 - odd_x) * fz + column - 1, out)


def edges_of(field, fx, fz):
    odd_x, odd_z = parities()
    own = fx * fz
    last, first = field[own - fz :, :], field[:fz, :]
    row = lax.broadcasted_iota(I32, (2 * fx, own), 0)
    wanted = jnp.where(row < fx, row * fz + fz - 1, (row - fx) * fz)
    hit = lax.broadcasted_iota(I32, (2 * fx, own), 1) == wanted
    sides = dot(jnp.where(hit, 1.0, 0.0).astype(BF16), field, ((1,), (0,)))
    right, left = sides[:fx], sides[fx:]
    flip_x, flip_z = odd_x == 1, odd_z == 1
    return (
        jnp.where(flip_x, first, last),
        jnp.where(flip_x, last, first),
        jnp.where(flip_z, left, right).astype(BF16),
        jnp.where(flip_z, right, left).astype(BF16),
    )


def matrix_of(elements, own, padded):
    left, right = [], []
    for gram, reads, writes in elements:
        scatter, gather = one_hot(writes, own), one_hot(reads, padded)
        if gram.dtype == F32:
            spread = sum(dot(scatter, half, ((1,), (0,))) for half in halves(gram))
            parts = halves(spread)
        else:
            parts = [dot(scatter, gram, ((1,), (0,))).astype(BF16)]
        left += parts
        right += [gather] * len(parts)
    return dot(jnp.concatenate(left, axis=1), jnp.concatenate(right, axis=1), ((1,), (1,)))


def fetch(slots, factor, coupling, fbuf, cbuf, sem):
    copies = []
    for i, slot in enumerate(slots):
        pair = (
            pltpu.make_async_copy(factor.at[slot], fbuf.at[i], sem.at[i, 0]),
            pltpu.make_async_copy(coupling.at[slot], cbuf.at[i], sem.at[i, 1]),
        )
        for copy in pair:
            copy.start()
        copies.append(pair)
    return copies


def given_kernel(
    fx, fz, moves, with_edges, f, order, factor, coupling, *rest
):
    if with_edges:
        traces, out, e0, e1, e3, fbuf, cbuf, sem = rest
    else:
        out, fbuf, cbuf, sem = rest
    slots = [f[i] for i in range(moves)]
    copies = fetch(slots, factor, coupling, fbuf, cbuf, sem)
    unknowns = coupling.shape[2]
    if with_edges:
        field = traces[...]
        e0[...], e1[...], side, e3[...] = edges_of(field, fx, fz)
        for i in range(field.shape[1] // unknowns):
            out[pl.ds(moves * unknowns + i * fx, fx), :] = side[:, i * unknowns : (i + 1) * unknowns]
    for i, slot in enumerate(slots):
        for copy in copies[i]:
            copy.wait()
        gram = gram_of(fbuf[i], cbuf[i], order[slot])
        out[pl.ds(i * unknowns, unknowns), :] = gram.astype(BF16)


def kept_kernel(fx, fz, f, s, order, reads, writes, factor, coupling, part, fbuf, cbuf, kept, sem):
    slots, moves = reads.shape[0], f.shape[0]
    most = slots - moves
    for i in range(slots):
        kept[i] = 0
    count = jnp.int32(0)
    for slot in range(slots):
        moved = f[0] == slot
        for i in range(moves):
            moved = moved | (f[i] == slot) | (s[i] == slot)
        kept[count] = slot
        count = count + jnp.where(moved, 0, 1)
    slots = [kept[i] for i in range(most)]
    copies = fetch(slots, factor, coupling, fbuf, cbuf, sem)
    elements = []
    for i, slot in enumerate(slots):
        valid = i < count
        read = jnp.where(valid, cell_of(reads[pl.ds(slot, 1), :], fx, fz), -1)
        write = jnp.where(valid, writes[pl.ds(slot, 1), :], -1)
        for copy in copies[i]:
            copy.wait()
        elements.append((gram_of(fbuf[i], cbuf[i], order[slot]), read, write))
    part[...] = matrix_of(elements, fx * fz, part.shape[1])


def relay_kernel(f, s, given, got, out):
    moves = f.shape[0]
    unknowns = given.shape[0] // moves
    for i in range(moves):
        value = given[pl.ds(i * unknowns, unknowns), :]
        for j in range(moves):
            value = jnp.where(s[i] == f[j], got[pl.ds(j * unknowns, unknowns), :], value)
        out[pl.ds(i * unknowns, unknowns), :] = value


def halo_dot(parts, field, frame, own):
    total = 0.0
    for part in parts:
        total = total + dot(part[:, :own], field, ((1,), (0,)))
        total = total + dot(part[:, own : own + frame.shape[0]], frame, ((1,), (0,)))
    return total


def first_kernel(
    fx, fz, f, s, reads, writes, got, got_s, part, traces, h0, h1, h3,
    matrix, first, e0, e1, e2, e3,
):
    own, moves = fx * fz, f.shape[0]
    unknowns = reads.shape[1]
    columns = traces.shape[1]
    elements = []
    for i in range(moves):
        slot = s[i]
        read = cell_of(reads[pl.ds(slot, 1), :], fx, fz)
        gram = got_s[pl.ds(i * unknowns, unknowns), :]
        elements.append((gram, read, writes[pl.ds(slot, 1), :]))
    for i in range(moves):
        slot = f[i]
        stays = slot != s[0]
        for j in range(1, moves):
            stays = stays & (slot != s[j])
        read = jnp.where(stays, cell_of(reads[pl.ds(slot, 1), :], fx, fz), -1)
        write = jnp.where(stays, writes[pl.ds(slot, 1), :], -1)
        elements.append((got[pl.ds(i * unknowns, unknowns), :], read, write))
    whole = part[...] + matrix_of(elements, own, part.shape[1])
    parts = halves(whole)
    matrix[0], matrix[1] = parts
    side = [
        got[pl.ds(moves * unknowns + i * fx, fx), :] for i in range(columns // unknowns)
    ]
    side = jnp.concatenate(side, axis=1)
    frame = jnp.concatenate([h0[...], h1[...], side, h3[...]], axis=0)
    field = halo_dot(parts, traces[...], frame, own).astype(BF16)
    first[...] = field
    e0[...], e1[...], e2[...], e3[...] = edges_of(field, fx, fz)


def second_kernel(own, matrix, first, h0, h1, h2, h3, out):
    frame = jnp.concatenate([h0[...], h1[...], h2[...], h3[...]], axis=0)
    out[...] = halo_dot((matrix[0], matrix[1]), first[...], frame, own)


def pairs(count, odd):
    route = []
    for low in range(odd, count - 1, 2):
        route += [(low, low + 1), (low + 1, low)]
    return route


def swapped(edge, axis, odd):
    return lax.ppermute(edge, axis, pairs(lax.axis_size(axis), odd))


def body(
    gram_factor, coupling, order_class, first_moves, second_moves, trace_index, owner_index, traces
):
    slots, width, unknowns = coupling.shape
    moves = first_moves.shape[0]
    fx, _, fz, columns = traces.shape
    own = fx * fz
    padded = -(-(own + 2 * (fx + fz)) // 128) * 128
    most = slots - moves
    field = traces.reshape(own, columns)
    grams = jax.ShapeDtypeStruct((moves * unknowns, unknowns), BF16)
    load = jax.ShapeDtypeStruct((moves * unknowns + fx * columns // unknowns, unknowns), BF16)
    edges = [jax.ShapeDtypeStruct((n, columns), BF16) for n in (fz, fz, fx, fx)]

    def element_cost(count):
        return pl.CostEstimate(
            flops=2 * count * width * unknowns * (width + unknowns),
            bytes_accessed=2 * count * width * (width + unknowns),
            transcendentals=0,
        )

    def buffers(count):
        return [
            pltpu.VMEM((count, width, width), BF16),
            pltpu.VMEM((count, width, unknowns), BF16),
        ]

    given, t0, t1, t3 = pl.pallas_call(
        functools.partial(given_kernel, fx, fz, moves, True),
        out_shape=(load, edges[0], edges[1], edges[3]),
        in_specs=[SMEM] * 2 + [HBM] * 2 + [VMEM],
        out_specs=(VMEM,) * 4,
        scratch_shapes=[*buffers(moves), pltpu.SemaphoreType.DMA((moves, 2))],
        compiler_params=params(53),
        cost_estimate=element_cost(moves),
        name="given",
    )(first_moves, order_class, gram_factor, coupling, field)
    given, t0, t1, t3, second_moves = lax.optimization_barrier((given, t0, t1, t3, second_moves))
    got = swapped(given, "gz", 0)

    given_s = pl.pallas_call(
        functools.partial(given_kernel, fx, fz, moves, False),
        out_shape=grams,
        in_specs=[SMEM] * 2 + [HBM] * 2,
        out_specs=VMEM,
        scratch_shapes=[*buffers(moves), pltpu.SemaphoreType.DMA((moves, 2))],
        compiler_params=params(53),
        cost_estimate=element_cost(moves),
        name="passed",
    )(second_moves, order_class, gram_factor, coupling)

    given_s, t3 = lax.optimization_barrier((given_s, t3))
    h3 = swapped(t3, "gz", 1)

    relayed = pl.pallas_call(
        relay_kernel,
        out_shape=grams,
        in_specs=[SMEM] * 2 + [VMEM] * 2,
        out_specs=VMEM,
        compiler_params=params(2),
        name="relay",
    )(first_moves, second_moves, given_s, got)
    relayed, t0, t1, order_class = lax.optimization_barrier((relayed, t0, t1, order_class))
    both = lax.axis_size("gy") * lax.axis_size("gz")
    second_bit = lax.axis_size("gz").bit_length() - 1
    got_s = lax.ppermute(relayed, ("gy", "gz"), swap_route(both, second_bit))
    h1 = swapped(t1, "gx", 1)
    h0 = swapped(t0, "gx", 0)

    part = pl.pallas_call(
        functools.partial(kept_kernel, fx, fz),
        out_shape=jax.ShapeDtypeStruct((own, padded), F32),
        in_specs=[SMEM] * 3 + [VMEM] * 2 + [HBM] * 2,
        out_specs=VMEM,
        scratch_shapes=[
            *buffers(most), pltpu.SMEM((slots,), I32), pltpu.SemaphoreType.DMA((most, 2))
        ],
        compiler_params=params(53),
        cost_estimate=element_cost(most),
        name="kept",
    )(
        first_moves, second_moves, order_class, trace_index, owner_index, gram_factor, coupling
    )

    matrix, first, *first_edges = pl.pallas_call(
        functools.partial(first_kernel, fx, fz),
        out_shape=(
            jax.ShapeDtypeStruct((2, own, padded), BF16),
            jax.ShapeDtypeStruct((own, columns), BF16),
            *edges,
        ),
        in_specs=[SMEM] * 2 + [VMEM] * 9,
        out_specs=(VMEM,) * 6,
        compiler_params=params(12),
        name="first",
    )(
        first_moves, second_moves, trace_index, owner_index, got, got_s, part, field, h0, h1, h3
    )

    e0, e1, e2, e3 = first_edges
    h1 = swapped(e1, "gx", 1)
    h2 = swapped(e2, "gz", 0)
    h3 = swapped(e3, "gz", 1)
    h0 = swapped(e0, "gx", 0)
    second = pl.pallas_call(
        functools.partial(second_kernel, own),
        out_shape=jax.ShapeDtypeStruct((own, columns), F32),
        in_specs=[VMEM] * 6,
        out_specs=VMEM,
        compiler_params=params(6),
        name="second",
    )(matrix, first, h0, h1, h2, h3)
    return second.reshape(traces.shape)


def solution(mesh):
    return jax.shard_map(
        body,
        mesh=mesh,
        in_specs=(
            P(("gx", "gy", "gz"), None, None),
            P(("gx", "gy", "gz"), None, None),
            P(("gx", "gy", "gz")),
            P(("gx", "gy", "gz")),
            P(("gx", "gy", "gz")),
            P(("gx", "gy", "gz"), None),
            P(("gx", "gy", "gz"), None),
            P("gx", "gy", "gz", None),
        ),
        out_specs=P("gx", "gy", "gz", None),
        check_vma=False,
    )
```

time: 61.4 us -> 53.4 us (0.87)
  the two profiles are of different devices: /device:TPU:94 before, /device:TPU:96 now
where the time goes in v2:
time: 53.4 us; the launch traced here: 53 us
  starting transfers between devices  30.1 us (56%)
  Pallas kernels  15.6 us (29%)
  waiting for transfers between devices  4.86 us (9%)
  local copies, waits for them, and re-layouts  2.26 us (4%)
    ppermute x8, starting transfers between devices, swapped(): return lax.ppermute(edge, axis, pairs(lax.axis_size(axis), odd))  24 us
    pallas_call x1, Pallas kernels, body(): pl.pallas_call(functools.partial(kept_kernel, fx, fz), out_shape=jax.Shap...  6.57 us
    ppermute x1, starting transfers between devices, body(): got_s = lax.ppermute(relayed, ('gy', 'gz'), swap_route(both, second_bit))  6.09 us
    ppermute x8, waiting for transfers between devices, swapped(): return lax.ppermute(edge, axis, pairs(lax.axis_size(axis), odd))  4.86 us
    pallas_call x1, Pallas kernels, body(): pl.pallas_call(functools.partial(given_kernel, fx, fz, moves, True), out_...  2.89 us
    pallas_call x1, Pallas kernels, body(): pl.pallas_call(functools.partial(given_kernel, fx, fz, moves, False), out...  2.87 us
    unnamed x16, local copies, waits for them, and re-layouts  2.26 us
    pallas_call x1, Pallas kernels, body(): pl.pallas_call(functools.partial(first_kernel, fx, fz), out_shape=(jax.Sh...  1.66 us
  transfers between devices with their start and end apart: 9, of which 2 were waited for; matrix products, arithmetic and copies ran while one was open for 0% of the time, Pallas kernels for 18%

profile of v2, /device:TPU:96, one launch (start us, length us, event | category | flops | bytes accessed | tf_op | source)
XLA Modules:
  0.0 53.0 jit_solution(5810500157980162028)
XLA Ops:
  0.0 0.0 copy-start.6
  0.0 0.0 copy-start
  0.0 0.9 %copy-done = bf16[16,1,16,256]{3,2,1,0:T(8,128)(2,1)S(1)} copy-done((bf16[16,1,16,256]{3,2,1,0:T(8,128)(2,1)S(1)}, bf16[16,1,16,256]{3,2,1,0:T(8,128)(2,1)}, u32[]{:S(2)}) %copy-start) | copy-done | bytes 131096
  0.9 0.0 copy-start.4
  0.9 0.7 %copy-done.4 = s32[3]{0:T(128)S(1)} copy-done((s32[3]{0:T(128)S(1)}, s32[3]{0:T(128)}, u32[]{:S(2)}) %copy-start.4) | copy-done | bytes 36
  1.6 0.0 copy-start.7
  1.6 0.7 %copy-done.7 = s32[12]{0:T(128)S(1)} copy-done((s32[12]{0:T(128)S(1)}, s32[12]{0:T(128)}, u32[]{:S(2)}) %copy-start.7) | copy-done | bytes 72
  2.2 2.9 %given.1 = (bf16[416,128]{1,0:T(8,128)(2,1)S(1)}, bf16[16,256]{1,0:T(8,128)(2,1)S(1)}, bf16[16,256]{1,0:T(8,128)(2,1)S(1)}, bf16[16,256]{1,0:T(8,128)(2,1)S(1)}) custom-call(s32[3]{0:T(128)S(1)} %copy-done.4, s32[12]{0:T(128)S(1)} %copy-done.7, bf16[12,384,384]{2,1,0:T(8,128)(2,1)} %factor.5, bf16[12,384,128]{2,1,0:T(8,128)(2,1)} %coupling.5, ...), custom_call_target="tpu_custom_call" | custom-call | flops 150994944 | bytes 1179648 | tf_op jit(solution)/shard_map/given/pallas_call | solution.py:255
  5.1 0.0 copy-start.5
  5.1 0.0 copy-start.2
  5.2 0.0 copy-start.3
  5.2 3.5 %collective-permute-start = (bf16[416,128]{1,0:T(8,128)(2,1)S(1)}, bf16[416,128]{1,0:T(8,128)(2,1)S(1)}, u32[]{:S(2)}, u32[]{:S(2)}) collective-permute-start(bf16[416,128]{1,0:T(8,128)(2,1)S(1)} %get-tuple-element.31), channel_id=1, source_target_pairs={{0,1},{1,0},{2,3},{3,2},{4,5},{5,4},{6,7},{7,6},{8,9},{9,8},{10,11... | collective-permute-start | bytes 319496 | tf_op jit(solution)/shard_map/ppermute | solution.py:225
  8.7 0.0 copy-done.6
  8.7 2.9 %passed.1.given = bf16[384,128]{1,0:T(8,128)(2,1)S(1)} custom-call(s32[3]{0:T(128)S(1)} %copy-done.6, s32[12]{0:T(128)S(1)} %copy-done.7, bf16[12,384,384]{2,1,0:T(8,128)(2,1)} %factor.5, bf16[12,384,128]{2,1,0:T(8,128)(2,1)} %coupling.5), custom_call_target="tpu_custom_call" | custom-call | flops 150994944 | bytes 1179648 | tf_op jit(solution)/shard_map/passed/pallas_call | solution.py:268
  11.6 0.0 copy-start.1
  11.6 0.3 collective-permute-done.got
  11.9 0.0 copy-done.5
  11.9 0.6 %relay.1 = bf16[384,128]{1,0:T(8,128)(2,1)S(1)} custom-call(s32[3]{0:T(128)S(1)} %copy-done.5, s32[3]{0:T(128)S(1)} %copy-done.6, bf16[384,128]{1,0:T(8,128)(2,1)S(1)} %passed.1.given, bf16[416,128]{1,0:T(8,128)(2,1)S(1)} %collective-permute-done.got), custom_call_target="tpu_custom_call" | custom-call | tf_op jit(solution)/shard_map/relay/pallas_call | solution.py:282
  12.5 6.1 %collective-permute-start.1 = (bf16[384,128]{1,0:T(8,128)(2,1)S(1)}, bf16[384,128]{1,0:T(8,128)(2,1)S(1)}, u32[]{:S(2)}, u32[]{:S(2)}) collective-permute-start(bf16[384,128]{1,0:T(8,128)(2,1)S(1)} %relay.1), channel_id=1, source_target_pairs={{0,32},{1,33},{2,34},{3,35},{4,36},{5,37},{6,38},{7,39},{8,40},{9,... | collective-permute-start | bytes 294920 | tf_op jit(solution)/shard_map/ppermute | solution.py:293
  18.6 4.6 %collective-permute-start.4 = (bf16[16,256]{1,0:T(8,128)(2,1)S(1)}, bf16[16,256]{1,0:T(8,128)(2,1)S(1)}, u32[]{:S(2)}, u32[]{:S(2)}) collective-permute-start(bf16[16,256]{1,0:T(8,128)(2,1)S(1)} %get-tuple-element.40), channel_id=1, source_target_pairs={{1,2},{2,1},{3,4},{4,3},{5,6},{6,5},{7,8},{8,7},{9,10},{10,9},{11,... | collective-permute-start | bytes 24584 | tf_op jit(solution)/shard_map/ppermute | solution.py:225
  23.1 1.9 %collective-permute-start.2 = (bf16[16,256]{1,0:T(8,128)(2,1)S(1)}, bf16[16,256]{1,0:T(8,128)(2,1)S(1)}, u32[]{:S(2)}, u32[]{:S(2)}) collective-permute-start(bf16[16,256]{1,0:T(8,128)(2,1)S(1)} %get-tuple-element.38), channel_id=1, source_target_pairs={{0,128},{128,0},{256,384},{384,256},{1,129},{129,1},{257,385},{385... | collective-permute-start | bytes 24584 | tf_op jit(solution)/shard_map/ppermute | solution.py:225
  25.1 1.9 %collective-permute-start.3 = (bf16[16,256]{1,0:T(8,128)(2,1)S(1)}, bf16[16,256]{1,0:T(8,128)(2,1)S(1)}, u32[]{:S(2)}, u32[]{:S(2)}) collective-permute-start(bf16[16,256]{1,0:T(8,128)(2,1)S(1)} %get-tuple-element.39), channel_id=1, source_target_pairs={{128,256},{256,128},{129,257},{257,129},{130,258},{258,130},{131,2... | collective-permute-start | bytes 24584 | tf_op jit(solution)/shard_map/ppermute | solution.py:225
  27.0 0.0 copy-done.2
  27.0 0.0 copy-done.3
  27.0 6.6 %kept.1.part = f32[256,384]{1,0:T(8,128)S(1)} custom-call(s32[3]{0:T(128)S(1)} %copy-done.5, s32[3]{0:T(128)S(1)} %copy-done.6, s32[12]{0:T(128)S(1)} %copy-done.7, s32[12,128]{1,0:T(8,128)S(1)} %copy-done.2, s32[12,128]{1,0:T(8,128)S(1)} %copy-done.3, bf16[12,384,384]{2,1,0:T(8,128)(2,1)} %factor.5, bf16[12,384,128]{2,1,0:T(8,128)(2,1)} %coupling.5), custom_call_target="tpu_custom_call" | custom-call | flops 452984832 | bytes 3538944 | tf_op jit(solution)/shard_map/kept/pallas_call | solution.py:297
  33.6 0.0 collective-permute-done.4.h3
  33.6 0.0 collective-permute-done.2.h0
  33.6 0.0 collective-permute-done.3.h1
  33.6 0.0 collective-permute-done.1.got_s
  33.6 0.0 copy-done.1
  33.7 1.7 %first.1 = (bf16[2,256,384]{2,1,0:T(8,128)(2,1)S(1)}, bf16[256,256]{1,0:T(8,128)(2,1)S(1)}, bf16[16,256]{1,0:T(8,128)(2,1)S(1)}, bf16[16,256]{1,0:T(8,128)(2,1)S...) custom-call(s32[3]{0:T(128)S(1)} %copy-done.5, s32[3]{0:T(128)S(1)} %copy-done.6, s32[12,128]{1,0:T(8,128)S(1)} %copy-done.2, ...), custom_call_target="tpu_custom_call" | custom-call | tf_op jit(solution)/shard_map/first/pallas_call | solution.py:312
  35.3 1.9 %collective-permute-start.5 = (bf16[16,256]{1,0:T(8,128)(2,1)S(1)}, bf16[16,256]{1,0:T(8,128)(2,1)S(1)}, u32[]{:S(2)}, u32[]{:S(2)}) collective-permute-start(bf16[16,256]{1,0:T(8,128)(2,1)S(1)} %get-tuple-element.43), channel_id=1, source_target_pairs={{0,128},{128,0},{256,384},{384,256},{1,129},{129,1},{257,385},{385... | collective-permute-start | bytes 24584 | tf_op jit(solution)/shard_map/ppermute | solution.py:225
  37.2 3.6 %collective-permute-start.6 = (bf16[16,256]{1,0:T(8,128)(2,1)S(1)}, bf16[16,256]{1,0:T(8,128)(2,1)S(1)}, u32[]{:S(2)}, u32[]{:S(2)}) collective-permute-start(bf16[16,256]{1,0:T(8,128)(2,1)S(1)} %get-tuple-element.44), channel_id=1, source_target_pairs={{128,256},{256,128},{129,257},{257,129},{130,258},{258,130},{131,2... | collective-permute-start | bytes 24584 | tf_op jit(solution)/shard_map/ppermute | solution.py:225
  40.9 2.2 %collective-permute-start.7 = (bf16[16,256]{1,0:T(8,128)(2,1)S(1)}, bf16[16,256]{1,0:T(8,128)(2,1)S(1)}, u32[]{:S(2)}, u32[]{:S(2)}) collective-permute-start(bf16[16,256]{1,0:T(8,128)(2,1)S(1)} %get-tuple-element.45), channel_id=1, source_target_pairs={{0,1},{1,0},{2,3},{3,2},{4,5},{5,4},{6,7},{7,6},{8,9},{9,8},{10,11... | collective-permute-start | bytes 24584 | tf_op jit(solution)/shard_map/ppermute | solution.py:225
  43.1 4.3 %collective-permute-start.8 = (bf16[16,256]{1,0:T(8,128)(2,1)S(1)}, bf16[16,256]{1,0:T(8,128)(2,1)S(1)}, u32[]{:S(2)}, u32[]{:S(2)}) collective-permute-start(bf16[16,256]{1,0:T(8,128)(2,1)S(1)} %get-tuple-element.46), channel_id=1, source_target_pairs={{1,2},{2,1},{3,4},{4,3},{5,6},{6,5},{7,8},{8,7},{9,10},{10,9},{11,... | collective-permute-start | bytes 24584 | tf_op jit(solution)/shard_map/ppermute | solution.py:225
  47.4 0.0 collective-permute-done.5.h0
  47.5 0.0 collective-permute-done.6.h1
  47.5 0.0 collective-permute-done.7.h2
  47.5 4.5 %collective-permute-done.8.h3 = bf16[16,256]{1,0:T(8,128)(2,1)S(1)} collective-permute-done((bf16[16,256]{1,0:T(8,128)(2,1)S(1)}, bf16[16,256]{1,0:T(8,128)(2,1)S(1)}, u32[]{:S(2)}, u32[]{:S(2)}) %collective-permute-start.8) | collective-permute-done | bytes 8224 | tf_op jit(solution)/shard_map/ppermute | solution.py:225
  52.0 1.0 %second.1 = f32[256,256]{1,0:T(8,128)} custom-call(bf16[2,256,384]{2,1,0:T(8,128)(2,1)S(1)} %get-tuple-element.41.matrix, bf16[256,256]{1,0:T(8,128)(2,1)S(1)} %get-tuple-element.42.first, bf16[16,256]{1,0:T(8,128)(2,1)S(1)} %collective-permute-done.5.h0, bf16[16,256]{1,0:T(8,128)(2,1)S(1)} %collective-permute-done.6.h1, ...), custom_call_target="tpu_custom_call" | custom-call | tf_op jit(solution)/shard_map/second/pallas_call | solution.py:332
Async XLA Ops:
  0.0 8.7 %copy-start.6 = (s32[3]{0:T(128)S(1)}, s32[3]{0:T(128)}, u32[]{:S(2)}) copy-start(s32[3]{0:T(128)} %s.2) | copy-start | bytes 40
  0.0 0.9 %copy-start = (bf16[16,1,16,256]{3,2,1,0:T(8,128)(2,1)S(1)}, bf16[16,1,16,256]{3,2,1,0:T(8,128)(2,1)}, u32[]{:S(2)}) copy-start(bf16[16,1,16,256]{3,2,1,0:T(8,128)(2,1)} %param.15) | copy-start | bytes 393220
  0.9 0.7 %copy-start.4 = (s32[3]{0:T(128)S(1)}, s32[3]{0:T(128)}, u32[]{:S(2)}) copy-start(s32[3]{0:T(128)} %f.8) | copy-start | bytes 40
  1.6 0.7 %copy-start.7 = (s32[12]{0:T(128)S(1)}, s32[12]{0:T(128)}, u32[]{:S(2)}) copy-start(s32[12]{0:T(128)} %order.4) | copy-start | bytes 148
  5.1 6.8 %copy-start.5 = (s32[3]{0:T(128)S(1)}, s32[3]{0:T(128)}, u32[]{:S(2)}) copy-start(s32[3]{0:T(128)} %f.8) | copy-start | bytes 40
  5.1 21.9 %copy-start.2 = (s32[12,128]{1,0:T(8,128)S(1)}, s32[12,128]{1,0:T(8,128)}, u32[]{:S(2)}) copy-start(s32[12,128]{1,0:T(8,128)} %reads.3) | copy-start | bytes 18436
  5.2 21.9 %copy-start.3 = (s32[12,128]{1,0:T(8,128)S(1)}, s32[12,128]{1,0:T(8,128)}, u32[]{:S(2)}) copy-start(s32[12,128]{1,0:T(8,128)} %writes.3) | copy-start | bytes 18436
  5.2 6.7 %collective-permute-start = (bf16[416,128]{1,0:T(8,128)(2,1)S(1)}, bf16[416,128]{1,0:T(8,128)(2,1)S(1)}, u32[]{:S(2)}, u32[]{:S(2)}) collective-permute-start(bf16[416,128]{1,0:T(8,128)(2,1)S(1)} %get-tuple-element.31), channel_id=1, source_target_pairs={{0,1},{1,0},{2,3},{3,2},{4,5},{5,4},{6,7},{7,6},{8,9},{9,8},{10,11... | collective-permute-start | bytes 319496 | tf_op jit(solution)/shard_map/ppermute | solution.py:225
  11.6 22.1 %copy-start.1 = (bf16[16,1,16,256]{3,2,1,0:T(8,128)(2,1)S(1)}, bf16[16,1,16,256]{3,2,1,0:T(8,128)(2,1)}, u32[]{:S(2)}) copy-start(bf16[16,1,16,256]{3,2,1,0:T(8,128)(2,1)} %param.15) | copy-start | bytes 393220
  12.5 21.1 %collective-permute-start.1 = (bf16[384,128]{1,0:T(8,128)(2,1)S(1)}, bf16[384,128]{1,0:T(8,128)(2,1)S(1)}, u32[]{:S(2)}, u32[]{:S(2)}) collective-permute-start(bf16[384,128]{1,0:T(8,128)(2,1)S(1)} %relay.1), channel_id=1, source_target_pairs={{0,32},{1,33},{2,34},{3,35},{4,36},{5,37},{6,38},{7,39},{8,40},{9,... | collective-permute-start | bytes 294920 | tf_op jit(solution)/shard_map/ppermute | solution.py:293
  18.6 15.0 %collective-permute-start.4 = (bf16[16,256]{1,0:T(8,128)(2,1)S(1)}, bf16[16,256]{1,0:T(8,128)(2,1)S(1)}, u32[]{:S(2)}, u32[]{:S(2)}) collective-permute-start(bf16[16,256]{1,0:T(8,128)(2,1)S(1)} %get-tuple-element.40), channel_id=1, source_target_pairs={{1,2},{2,1},{3,4},{4,3},{5,6},{6,5},{7,8},{8,7},{9,10},{10,9},{11,... | collective-permute-start | bytes 24584 | tf_op jit(solution)/shard_map/ppermute | solution.py:225
  23.1 10.5 %collective-permute-start.2 = (bf16[16,256]{1,0:T(8,128)(2,1)S(1)}, bf16[16,256]{1,0:T(8,128)(2,1)S(1)}, u32[]{:S(2)}, u32[]{:S(2)}) collective-permute-start(bf16[16,256]{1,0:T(8,128)(2,1)S(1)} %get-tuple-element.38), channel_id=1, source_target_pairs={{0,128},{128,0},{256,384},{384,256},{1,129},{129,1},{257,385},{385... | collective-permute-start | bytes 24584 | tf_op jit(solution)/shard_map/ppermute | solution.py:225
  25.1 8.6 %collective-permute-start.3 = (bf16[16,256]{1,0:T(8,128)(2,1)S(1)}, bf16[16,256]{1,0:T(8,128)(2,1)S(1)}, u32[]{:S(2)}, u32[]{:S(2)}) collective-permute-start(bf16[16,256]{1,0:T(8,128)(2,1)S(1)} %get-tuple-element.39), channel_id=1, source_target_pairs={{128,256},{256,128},{129,257},{257,129},{130,258},{258,130},{131,2... | collective-permute-start | bytes 24584 | tf_op jit(solution)/shard_map/ppermute | solution.py:225
  35.3 12.1 %collective-permute-start.5 = (bf16[16,256]{1,0:T(8,128)(2,1)S(1)}, bf16[16,256]{1,0:T(8,128)(2,1)S(1)}, u32[]{:S(2)}, u32[]{:S(2)}) collective-permute-start(bf16[16,256]{1,0:T(8,128)(2,1)S(1)} %get-tuple-element.43), channel_id=1, source_target_pairs={{0,128},{128,0},{256,384},{384,256},{1,129},{129,1},{257,385},{385... | collective-permute-start | bytes 24584 | tf_op jit(solution)/shard_map/ppermute | solution.py:225
  37.2 10.2 %collective-permute-start.6 = (bf16[16,256]{1,0:T(8,128)(2,1)S(1)}, bf16[16,256]{1,0:T(8,128)(2,1)S(1)}, u32[]{:S(2)}, u32[]{:S(2)}) collective-permute-start(bf16[16,256]{1,0:T(8,128)(2,1)S(1)} %get-tuple-element.44), channel_id=1, source_target_pairs={{128,256},{256,128},{129,257},{257,129},{130,258},{258,130},{131,2... | collective-permute-start | bytes 24584 | tf_op jit(solution)/shard_map/ppermute | solution.py:225
  40.9 6.6 %collective-permute-start.7 = (bf16[16,256]{1,0:T(8,128)(2,1)S(1)}, bf16[16,256]{1,0:T(8,128)(2,1)S(1)}, u32[]{:S(2)}, u32[]{:S(2)}) collective-permute-start(bf16[16,256]{1,0:T(8,128)(2,1)S(1)} %get-tuple-element.45), channel_id=1, source_target_pairs={{0,1},{1,0},{2,3},{3,2},{4,5},{5,4},{6,7},{7,6},{8,9},{9,8},{10,11... | collective-permute-start | bytes 24584 | tf_op jit(solution)/shard_map/ppermute | solution.py:225
  43.1 8.9 %collective-permute-start.8 = (bf16[16,256]{1,0:T(8,128)(2,1)S(1)}, bf16[16,256]{1,0:T(8,128)(2,1)S(1)}, u32[]{:S(2)}, u32[]{:S(2)}) collective-permute-start(bf16[16,256]{1,0:T(8,128)(2,1)S(1)} %get-tuple-element.46), channel_id=1, source_target_pairs={{1,2},{2,1},{3,4},{4,3},{5,6},{6,5},{7,8},{8,7},{9,10},{10,9},{11,... | collective-permute-start | bytes 24584 | tf_op jit(solution)/shard_map/ppermute | solution.py:225

commit v3 on v2

v3 whole, which is shorter than its diff:
```python
import functools

import jax
import jax.numpy as jnp
from jax import lax
from jax.experimental import pallas as pl
from jax.experimental.pallas import tpu as pltpu
from jax.sharding import PartitionSpec as P

BF16 = jnp.bfloat16
F32 = jnp.float32
I32 = jnp.int32
HBM = pl.BlockSpec(memory_space=pltpu.MemorySpace.HBM)
VMEM = pl.BlockSpec(memory_space=pltpu.MemorySpace.VMEM)
SMEM = pl.BlockSpec(memory_space=pltpu.MemorySpace.SMEM)


def params(mebibytes):
    return pltpu.CompilerParams(vmem_limit_bytes=mebibytes << 20)


def swap_route(count, bit):
    return [(low, low ^ (1 << bit)) for low in range(count) if low ^ (1 << bit) < count]


def dot(a, b, dims):
    return lax.dot_general(a, b, (dims, ((), ())), preferred_element_type=F32)


def halves(value):
    high = value.astype(BF16)
    return high, (value - high.astype(F32)).astype(BF16)


def grams_of(slots, order, fbuf, cbuf):
    products = [dot(fbuf[i], cbuf[i], ((1,), (0,))) for i in range(len(slots))]
    operators = []
    for slot, product in zip(slots, products):
        width = product.shape[0] * (2 + order[slot]) // 4
        keep = lax.broadcasted_iota(I32, product.shape, 0) < width
        operators.append(jnp.where(keep, product, 0.0).astype(BF16))
    return [dot(operator, operator, ((0,), (0,))) for operator in operators]


def one_hot(index, rows):
    hit = lax.broadcasted_iota(I32, (rows, index.shape[1]), 0) == index
    return jnp.where(hit, 1.0, 0.0).astype(BF16)


def parities():
    return lax.axis_index("gx") % 2, lax.axis_index("gz") % 2


def cell_of(cell, fx, fz):
    odd_x, odd_z = parities()
    pitch = fz + 2
    row = jnp.zeros_like(cell)
    for edge in range(1, fx + 2):
        row = row + jnp.where(cell >= edge * pitch, 1, 0)
    column = cell - row * pitch
    base_x = fx * fz
    base_z = base_x + 2 * fz
    out = (row - 1) * fz + column - 1
    out = jnp.where(column == fz + 1, base_z + odd_z * fx + row - 1, out)
    out = jnp.where(column == 0, base_z + (1 - odd_z) * fx + row - 1, out)
    out = jnp.where(row == fx + 1, base_x + odd_x * fz + column - 1, out)
    return jnp.where(row == 0, base_x + (1 - odd_x) * fz + column - 1, out)


def edges_of(field, fx, fz):
    odd_x, odd_z = parities()
    own = fx * fz
    last, first = field[own - fz :, :], field[:fz, :]
    row = lax.broadcasted_iota(I32, (2 * fx, own), 0)
    wanted = jnp.where(row < fx, row * fz + fz - 1, (row - fx) * fz)
    hit = lax.broadcasted_iota(I32, (2 * fx, own), 1) == wanted
    sides = dot(jnp.where(hit, 1.0, 0.0).astype(BF16), field, ((1,), (0,)))
    right, left = sides[:fx], sides[fx:]
    flip_x, flip_z = odd_x == 1, odd_z == 1
    return (
        jnp.where(flip_x, first, last),
        jnp.where(flip_x, last, first),
        jnp.where(flip_z, left, right).astype(BF16),
        jnp.where(flip_z, right, left).astype(BF16),
    )


def started(*copies):
    for copy in copies:
        copy.start()
    return copies


def waited(copies):
    for copy in copies:
        copy.wait()


def fetch(slots, factor, coupling, fbuf, cbuf, sem):
    copies = []
    for i, slot in enumerate(slots):
        copies += started(
            pltpu.make_async_copy(factor.at[slot], fbuf.at[i], sem.at[i, 0]),
            pltpu.make_async_copy(coupling.at[slot], cbuf.at[i], sem.at[i, 1]),
        )
    return copies


def given_kernel(
    fx, fz, f_hbm, order_hbm, factor, coupling, traces_hbm, out, e0, e1, e3,
    f, order, traces, fbuf, cbuf, sem, small,
):
    moves = f.shape[0]
    unknowns = coupling.shape[2]
    index, rest, block = started(
        pltpu.make_async_copy(f_hbm, f, small.at[0]),
        pltpu.make_async_copy(order_hbm, order, small.at[1]),
        pltpu.make_async_copy(traces_hbm, traces, small.at[2]),
    )
    index.wait()
    slots = [f[i] for i in range(moves)]
    copies = fetch(slots, factor, coupling, fbuf, cbuf, sem)
    block.wait()
    e0[...], e1[...], side, e3[...] = edges_of(traces[...], fx, fz)
    for i in range(side.shape[1] // unknowns):
        part = side[:, i * unknowns : (i + 1) * unknowns]
        out[pl.ds(moves * unknowns + i * fx, fx), :] = part
    rest.wait()
    waited(copies)
    for i, gram in enumerate(grams_of(slots, order, fbuf, cbuf)):
        out[pl.ds(i * unknowns, unknowns), :] = gram.astype(BF16)


def kept_kernel(
    fx, fz, f, s, order, reads, writes, factor, coupling, given, part, moved_to, moved_from,
    fbuf, cbuf, to, origin, kept, sem,
):
    slots, moves = reads.shape[0], f.shape[0]
    unknowns = reads.shape[1]
    most = slots - moves
    own, cells = fx * fz, origin.shape[0]
    for i in range(slots):
        kept[i] = 0
    count = jnp.int32(0)
    for slot in range(slots):
        moved = f[0] == slot
        for i in range(moves):
            moved = moved | (f[i] == slot) | (s[i] == slot)
        kept[count] = slot
        count = count + jnp.where(moved, 0, 1)
    wanted = [s[i] for i in range(moves)] + [kept[i] for i in range(most)]
    copies = fetch(wanted, factor, coupling, fbuf, cbuf, sem)

    def place(slot, valid, to_ref, from_ref, i):
        read = jnp.where(valid, cell_of(reads[pl.ds(slot, 1), :], fx, fz), -1)
        write = jnp.where(valid, writes[pl.ds(slot, 1), :], -1)
        columns = pl.ds(i * unknowns, unknowns)
        to_ref[:, columns] = one_hot(write, own)
        from_ref[:, columns] = one_hot(read, cells)

    for i in range(moves):
        place(s[i], True, moved_to, moved_from, i)
        stays = f[i] != s[0]
        for j in range(1, moves):
            stays = stays & (f[i] != s[j])
        place(f[i], stays, moved_to, moved_from, moves + i)
    for i in range(most):
        place(kept[i], i < count, to, origin, i)

    waited(copies)
    grams = grams_of(wanted, order, fbuf, cbuf)
    for i in range(moves):
        given[pl.ds(i * unknowns, unknowns), :] = grams[i].astype(BF16)
    highs, lows = [], []
    for i in range(most):
        scatter = to[:, pl.ds(i * unknowns, unknowns)]
        gram = jnp.concatenate(halves(grams[moves + i]), axis=0)
        spread = dot(jnp.concatenate([scatter, scatter], axis=1), gram, ((1,), (0,)))
        high, low = halves(spread)
        highs.append(high)
        lows.append(low)
    left = jnp.concatenate(
        [jnp.concatenate(highs, axis=1), jnp.concatenate(lows, axis=1)], axis=0
    )
    both = dot(left, origin[...], ((1,), (1,)))
    part[...] = both[:own] + both[own:]


def relay_kernel(f, s, given, got, out):
    moves = f.shape[0]
    unknowns = given.shape[0] // moves
    for i in range(moves):
        value = given[pl.ds(i * unknowns, unknowns), :]
        for j in range(moves):
            value = jnp.where(s[i] == f[j], got[pl.ds(j * unknowns, unknowns), :], value)
        out[pl.ds(i * unknowns, unknowns), :] = value


def applied(matrix, field, frame):
    both = dot(matrix, jnp.concatenate([field, frame], axis=0), ((1,), (0,)))
    own = matrix.shape[0] // 2
    return both[:own] + both[own:]


def first_kernel(
    fx, fz, moves, got, got_s, part, moved_to, moved_from, traces, h0, h1, h3,
    matrix, first, e0, e1, e2, e3,
):
    columns = traces.shape[1]
    unknowns = got.shape[1]
    spread = []
    for i in range(2 * moves):
        source = got_s if i < moves else got
        gram = source[pl.ds(i % moves * unknowns, unknowns), :]
        scatter = moved_to[:, pl.ds(i * unknowns, unknowns)]
        spread.append(dot(scatter, gram, ((1,), (0,))).astype(BF16))
    moved = dot(jnp.concatenate(spread, axis=1), moved_from[...], ((1,), (1,)))
    whole = jnp.concatenate(halves(part[...] + moved), axis=0)
    matrix[...] = whole
    side = [
        got[pl.ds(moves * unknowns + i * fx, fx), :] for i in range(columns // unknowns)
    ]
    side = jnp.concatenate(side, axis=1)
    frame = jnp.concatenate([h0[...], h1[...], side, h3[...]], axis=0)
    field = applied(whole, traces[...], frame).astype(BF16)
    first[...] = field
    e0[...], e1[...], e2[...], e3[...] = edges_of(field, fx, fz)


def second_kernel(matrix, first, h0, h1, h2, h3, out):
    frame = jnp.concatenate([h0[...], h1[...], h2[...], h3[...]], axis=0)
    out[...] = applied(matrix[...], first[...], frame)


def pairs(count, odd):
    route = []
    for low in range(odd, count - 1, 2):
        route += [(low, low + 1), (low + 1, low)]
    return route


def swapped(edge, axis, odd):
    return lax.ppermute(edge, axis, pairs(lax.axis_size(axis), odd))


def body(
    gram_factor, coupling, order_class, first_moves, second_moves, trace_index, owner_index, traces
):
    slots, width, unknowns = coupling.shape
    moves = first_moves.shape[0]
    fx, _, fz, columns = traces.shape
    own = fx * fz
    cells = own + 2 * (fx + fz)
    most = slots - moves
    field = traces.reshape(own, columns)
    grams = jax.ShapeDtypeStruct((moves * unknowns, unknowns), BF16)
    load = jax.ShapeDtypeStruct((moves * unknowns + fx * columns // unknowns, unknowns), BF16)
    edges = [jax.ShapeDtypeStruct((n, columns), BF16) for n in (fz, fz, fx, fx)]

    def in_hbm(array):
        return pltpu.with_memory_space_constraint(array, pltpu.MemorySpace.HBM)

    gram_factor, coupling = in_hbm(gram_factor), in_hbm(coupling)

    def element_cost(count):
        return pl.CostEstimate(
            flops=2 * count * width * unknowns * (width + unknowns),
            bytes_accessed=2 * count * width * (width + unknowns),
            transcendentals=0,
        )

    def buffers(count):
        return [
            pltpu.VMEM((count, width, width), BF16),
            pltpu.VMEM((count, width, unknowns), BF16),
        ]

    given, t0, t1, t3 = pl.pallas_call(
        functools.partial(given_kernel, fx, fz),
        out_shape=(load, edges[0], edges[1], edges[3]),
        in_specs=[HBM] * 5,
        out_specs=(VMEM,) * 4,
        scratch_shapes=[
            pltpu.SMEM((moves,), I32),
            pltpu.SMEM((slots,), I32),
            pltpu.VMEM((own, columns), BF16),
            *buffers(moves),
            pltpu.SemaphoreType.DMA((moves, 2)),
            pltpu.SemaphoreType.DMA((3,)),
        ],
        compiler_params=params(12),
        cost_estimate=element_cost(moves),
        name="given",
    )(in_hbm(first_moves), in_hbm(order_class), gram_factor, coupling, in_hbm(field))
    given, t0, t1, t3, second_moves = lax.optimization_barrier((given, t0, t1, t3, second_moves))
    got = swapped(given, "gz", 0)

    given_s, part, moved_to, moved_from = pl.pallas_call(
        functools.partial(kept_kernel, fx, fz),
        out_shape=(
            grams,
            jax.ShapeDtypeStruct((own, cells), F32),
            jax.ShapeDtypeStruct((own, 2 * moves * unknowns), BF16),
            jax.ShapeDtypeStruct((cells, 2 * moves * unknowns), BF16),
        ),
        in_specs=[SMEM] * 3 + [VMEM] * 2 + [HBM] * 2,
        out_specs=(VMEM,) * 4,
        scratch_shapes=[
            *buffers(slots),
            pltpu.VMEM((own, most * unknowns), BF16),
            pltpu.VMEM((cells, most * unknowns), BF16),
            pltpu.SMEM((slots,), I32),
            pltpu.SemaphoreType.DMA((slots, 2)),
        ],
        compiler_params=params(24),
        cost_estimate=element_cost(slots),
        name="kept",
    )(
        first_moves, second_moves, order_class, trace_index, owner_index, gram_factor, coupling
    )

    relayed = pl.pallas_call(
        relay_kernel,
        out_shape=grams,
        in_specs=[SMEM] * 2 + [VMEM] * 2,
        out_specs=VMEM,
        compiler_params=params(2),
        name="relay",
    )(first_moves, second_moves, given_s, got)
    both = lax.axis_size("gy") * lax.axis_size("gz")
    second_bit = lax.axis_size("gz").bit_length() - 1
    got_s = lax.ppermute(relayed, ("gy", "gz"), swap_route(both, second_bit))
    h1 = swapped(t1, "gx", 1)
    h3 = swapped(t3, "gz", 1)
    h0 = swapped(t0, "gx", 0)

    matrix, first, *first_edges = pl.pallas_call(
        functools.partial(first_kernel, fx, fz, moves),
        out_shape=(
            jax.ShapeDtypeStruct((2 * own, cells), BF16),
            jax.ShapeDtypeStruct((own, columns), BF16),
            *edges,
        ),
        in_specs=[VMEM] * 9,
        out_specs=(VMEM,) * 6,
        compiler_params=params(12),
        name="first",
    )(got, got_s, part, moved_to, moved_from, field, h0, h1, h3)

    e0, e1, e2, e3 = first_edges
    h1 = swapped(e1, "gx", 1)
    h2 = swapped(e2, "gz", 0)
    h3 = swapped(e3, "gz", 1)
    h0 = swapped(e0, "gx", 0)
    second = pl.pallas_call(
        second_kernel,
        out_shape=jax.ShapeDtypeStruct((own, columns), F32),
        in_specs=[VMEM] * 6,
        out_specs=VMEM,
        compiler_params=params(6),
        name="second",
    )(matrix, first, h0, h1, h2, h3)
    return second.reshape(traces.shape)


def solution(mesh):
    return jax.shard_map(
        body,
        mesh=mesh,
        in_specs=(
            P(("gx", "gy", "gz"), None, None),
            P(("gx", "gy", "gz"), None, None),
            P(("gx", "gy", "gz")),
            P(("gx", "gy", "gz")),
            P(("gx", "gy", "gz")),
            P(("gx", "gy", "gz"), None),
            P(("gx", "gy", "gz"), None),
            P("gx", "gy", "gz", None),
        ),
        out_specs=P("gx", "gy", "gz", None),
        check_vma=False,
    )
```

time: 53.4 us -> 49.6 us (0.929)
  the two profiles are of different devices: /device:TPU:96 before, /device:TPU:33 now
where the time goes in v3:
time: 49.6 us; the launch traced here: 49.3 us
  starting transfers between devices  30.2 us (61%)
  Pallas kernels  10.6 us (21%)
  waiting for transfers between devices  8.16 us (16%)
    ppermute x8, starting transfers between devices, swapped(): return lax.ppermute(edge, axis, pairs(lax.axis_size(axis), odd))  24.4 us
    ppermute x8, waiting for transfers between devices, swapped(): return lax.ppermute(edge, axis, pairs(lax.axis_size(axis), odd))  8.16 us
    ppermute x1, starting transfers between devices, body(): got_s = lax.ppermute(relayed, ('gy', 'gz'), swap_route(both, second_bit))  5.81 us
    pallas_call x1, Pallas kernels, body(): pl.pallas_call(functools.partial(kept_kernel, fx, fz), out_shape=(grams,...  5.47 us
    pallas_call x1, Pallas kernels, body(): pl.pallas_call(functools.partial(given_kernel, fx, fz), out_shape=(load,...  2.72 us
    pallas_call x1, Pallas kernels, body(): pl.pallas_call(second_kernel, out_shape=jax.ShapeDtypeStruct((own, column...  0.99 us
  transfers between devices with their start and end apart: 9, of which 2 were waited for; matrix products, arithmetic and copies ran while one was open for 0% of the time, Pallas kernels for 11%

profile of v3, /device:TPU:33, one launch (start us, length us, event | category | flops | bytes accessed | tf_op | source)
XLA Modules:
  0.0 49.3 jit_solution(14325400402743960314)
XLA Ops:
  0.0 0.0 copy-start.3
  0.0 0.0 copy-start.5
  0.0 0.0 copy-start.4
  0.0 0.0 copy-start.2
  0.0 0.0 copy-start.1
  0.0 2.7 %given.1 = (bf16[416,128]{1,0:T(8,128)(2,1)S(1)}, bf16[16,256]{1,0:T(8,128)(2,1)S(1)}, bf16[16,256]{1,0:T(8,128)(2,1)S(1)}, bf16[16,256]{1,0:T(8,128)(2,1)S(1)}) custom-call(s32[3]{0:T(128)} %f.3, s32[12]{0:T(128)} %order.1, bf16[12,384,384]{2,1,0:T(8,128)(2,1)} %factor.3, bf16[12,384,128]{2,1,0:T(8,128)(2,1)} %coupling.3, bf16[256,256]{1,0:T(8,128)(2,1)} %bitcast.4), custom_call_target="tpu_custom_call" | custom-call | flops 150994944 | bytes 1179648 | tf_op jit(solution)/shard_map/given/pallas_call | solution.py:278
  2.8 0.0 copy-start
  2.8 3.3 %collective-permute-start = (bf16[416,128]{1,0:T(8,128)(2,1)S(1)}, bf16[416,128]{1,0:T(8,128)(2,1)S(1)}, u32[]{:S(2)}, u32[]{:S(2)}) collective-permute-start(bf16[416,128]{1,0:T(8,128)(2,1)S(1)} %get-tuple-element.28), channel_id=1, source_target_pairs={{0,1},{1,0},{2,3},{3,2},{4,5},{5,4},{6,7},{7,6},{8,9},{9,8},{10,11... | collective-permute-start | bytes 319496 | tf_op jit(solution)/shard_map/ppermute | solution.py:243
  6.0 0.0 copy-done.3
  6.0 0.0 copy-done.5
  6.0 0.0 copy-done.4
  6.1 0.0 copy-done.2
  6.1 0.0 copy-done.1
  6.1 5.5 %kept.1 = (bf16[384,128]{1,0:T(8,128)(2,1)S(1)}, f32[256,320]{1,0:T(8,128)S(1)}, bf16[256,768]{1,0:T(8,128)(2,1)S(1)}, bf16[320,768]{1,0:T(8,128)(2,1)S(1)}) custom-call(s32[3]{0:T(128)S(1)} %copy-done.3, s32[3]{0:T(128)S(1)} %copy-done.4, s32[12]{0:T(128)S(1)} %copy-done.5, s32[12,128]{1,0:T(8,128)S(1)} %copy-done.1, s32[12,128]{1,0:T(8,128)S(1)} %copy-done.2, ...), custom_call_target="tpu_custom_call" | custom-call | flops 603979776 | bytes 4718592 | tf_op jit(solution)/shard_map/kept/pallas_call | solution.py:298
  11.6 0.0 collective-permute-done.got
  11.6 0.6 %relay.1 = bf16[384,128]{1,0:T(8,128)(2,1)S(1)} custom-call(s32[3]{0:T(128)S(1)} %copy-done.3, s32[3]{0:T(128)S(1)} %copy-done.4, bf16[384,128]{1,0:T(8,128)(2,1)S(1)} %get-tuple-element.30.given, bf16[416,128]{1,0:T(8,128)(2,1)S(1)} %collective-permute-done.got), custom_call_target="tpu_custom_call" | custom-call | tf_op jit(solution)/shard_map/relay/pallas_call | solution.py:322
  12.2 5.8 %collective-permute-start.1 = (bf16[384,128]{1,0:T(8,128)(2,1)S(1)}, bf16[384,128]{1,0:T(8,128)(2,1)S(1)}, u32[]{:S(2)}, u32[]{:S(2)}) collective-permute-start(bf16[384,128]{1,0:T(8,128)(2,1)S(1)} %relay.1), channel_id=1, source_target_pairs={{0,32},{1,33},{2,34},{3,35},{4,36},{5,37},{6,38},{7,39},{8,40},{9,... | collective-permute-start | bytes 294920 | tf_op jit(solution)/shard_map/ppermute | solution.py:332
  18.0 3.1 %collective-permute-start.2 = (bf16[16,256]{1,0:T(8,128)(2,1)S(1)}, bf16[16,256]{1,0:T(8,128)(2,1)S(1)}, u32[]{:S(2)}, u32[]{:S(2)}) collective-permute-start(bf16[16,256]{1,0:T(8,128)(2,1)S(1)} %get-tuple-element.34), channel_id=1, source_target_pairs={{0,128},{128,0},{256,384},{384,256},{1,129},{129,1},{257,385},{385... | collective-permute-start | bytes 24584 | tf_op jit(solution)/shard_map/ppermute | solution.py:243
  21.1 3.9 %collective-permute-start.3 = (bf16[16,256]{1,0:T(8,128)(2,1)S(1)}, bf16[16,256]{1,0:T(8,128)(2,1)S(1)}, u32[]{:S(2)}, u32[]{:S(2)}) collective-permute-start(bf16[16,256]{1,0:T(8,128)(2,1)S(1)} %get-tuple-element.35), channel_id=1, source_target_pairs={{128,256},{256,128},{129,257},{257,129},{130,258},{258,130},{131,2... | collective-permute-start | bytes 24584 | tf_op jit(solution)/shard_map/ppermute | solution.py:243
  25.0 3.6 %collective-permute-start.4 = (bf16[16,256]{1,0:T(8,128)(2,1)S(1)}, bf16[16,256]{1,0:T(8,128)(2,1)S(1)}, u32[]{:S(2)}, u32[]{:S(2)}) collective-permute-start(bf16[16,256]{1,0:T(8,128)(2,1)S(1)} %get-tuple-element.36), channel_id=1, source_target_pairs={{1,2},{2,1},{3,4},{4,3},{5,6},{6,5},{7,8},{8,7},{9,10},{10,9},{11,... | collective-permute-start | bytes 24584 | tf_op jit(solution)/shard_map/ppermute | solution.py:243
  28.6 0.0 collective-permute-done.2.h0
  28.7 0.0 collective-permute-done.3.h1
  28.7 4.1 %collective-permute-done.4.h3 = bf16[16,256]{1,0:T(8,128)(2,1)S(1)} collective-permute-done((bf16[16,256]{1,0:T(8,128)(2,1)S(1)}, bf16[16,256]{1,0:T(8,128)(2,1)S(1)}, u32[]{:S(2)}, u32[]{:S(2)}) %collective-permute-start.4) | collective-permute-done | bytes 8224 | tf_op jit(solution)/shard_map/ppermute | solution.py:243
  32.7 0.0 collective-permute-done.1.got_s
  32.8 0.0 copy-done
  32.8 0.9 %first.1 = (bf16[512,320]{1,0:T(8,128)(2,1)S(1)}, bf16[256,256]{1,0:T(8,128)(2,1)S(1)}, bf16[16,256]{1,0:T(8,128)(2,1)S(1)}, bf16[16,256]{1,0:T(8,128)(2,1)S(1)}...) custom-call(bf16[416,128]{1,0:T(8,128)(2,1)S(1)} %collective-permute-done.got, ...), custom_call_target="tpu_custom_call" | custom-call | tf_op jit(solution)/shard_map/first/pallas_call | solution.py:337
  33.6 1.9 %collective-permute-start.5 = (bf16[16,256]{1,0:T(8,128)(2,1)S(1)}, bf16[16,256]{1,0:T(8,128)(2,1)S(1)}, u32[]{:S(2)}, u32[]{:S(2)}) collective-permute-start(bf16[16,256]{1,0:T(8,128)(2,1)S(1)} %get-tuple-element.39), channel_id=1, source_target_pairs={{0,128},{128,0},{256,384},{384,256},{1,129},{129,1},{257,385},{385... | collective-permute-start | bytes 24584 | tf_op jit(solution)/shard_map/ppermute | solution.py:243
  35.6 3.1 %collective-permute-start.6 = (bf16[16,256]{1,0:T(8,128)(2,1)S(1)}, bf16[16,256]{1,0:T(8,128)(2,1)S(1)}, u32[]{:S(2)}, u32[]{:S(2)}) collective-permute-start(bf16[16,256]{1,0:T(8,128)(2,1)S(1)} %get-tuple-element.40), channel_id=1, source_target_pairs={{128,256},{256,128},{129,257},{257,129},{130,258},{258,130},{131,2... | collective-permute-start | bytes 24584 | tf_op jit(solution)/shard_map/ppermute | solution.py:243
  38.6 1.9 %collective-permute-start.7 = (bf16[16,256]{1,0:T(8,128)(2,1)S(1)}, bf16[16,256]{1,0:T(8,128)(2,1)S(1)}, u32[]{:S(2)}, u32[]{:S(2)}) collective-permute-start(bf16[16,256]{1,0:T(8,128)(2,1)S(1)} %get-tuple-element.41), channel_id=1, source_target_pairs={{0,1},{1,0},{2,3},{3,2},{4,5},{5,4},{6,7},{7,6},{8,9},{9,8},{10,11... | collective-permute-start | bytes 24584 | tf_op jit(solution)/shard_map/ppermute | solution.py:243
  40.6 3.6 %collective-permute-start.8 = (bf16[16,256]{1,0:T(8,128)(2,1)S(1)}, bf16[16,256]{1,0:T(8,128)(2,1)S(1)}, u32[]{:S(2)}, u32[]{:S(2)}) collective-permute-start(bf16[16,256]{1,0:T(8,128)(2,1)S(1)} %get-tuple-element.42), channel_id=1, source_target_pairs={{1,2},{2,1},{3,4},{4,3},{5,6},{6,5},{7,8},{8,7},{9,10},{10,9},{11,... | collective-permute-start | bytes 24584 | tf_op jit(solution)/shard_map/ppermute | solution.py:243
  44.2 0.0 collective-permute-done.5.h0
  44.2 0.0 collective-permute-done.6.h1
  44.2 0.0 collective-permute-done.7.h2
  44.2 4.1 %collective-permute-done.8.h3 = bf16[16,256]{1,0:T(8,128)(2,1)S(1)} collective-permute-done((bf16[16,256]{1,0:T(8,128)(2,1)S(1)}, bf16[16,256]{1,0:T(8,128)(2,1)S(1)}, u32[]{:S(2)}, u32[]{:S(2)}) %collective-permute-start.8) | collective-permute-done | bytes 8224 | tf_op jit(solution)/shard_map/ppermute | solution.py:243
  48.3 1.0 %second.1 = f32[256,256]{1,0:T(8,128)} custom-call(bf16[512,320]{1,0:T(8,128)(2,1)S(1)} %get-tuple-element.37.matrix, bf16[256,256]{1,0:T(8,128)(2,1)S(1)} %get-tuple-element.38.first, bf16[16,256]{1,0:T(8,128)(2,1)S(1)} %collective-permute-done.5.h0, bf16[16,256]{1,0:T(8,128)(2,1)S(1)} %collective-permute-done.6.h1, ...), custom_call_target="tpu_custom_call" | custom-call | tf_op jit(solution)/shard_map/second/pallas_call | solution.py:355
Async XLA Ops:
  0.0 6.0 %copy-start.3 = (s32[3]{0:T(128)S(1)}, s32[3]{0:T(128)}, u32[]{:S(2)}) copy-start(s32[3]{0:T(128)} %f.3) | copy-start | bytes 40
  0.0 6.0 %copy-start.5 = (s32[12]{0:T(128)S(1)}, s32[12]{0:T(128)}, u32[]{:S(2)}) copy-start(s32[12]{0:T(128)} %order.1) | copy-start | bytes 148
  0.0 6.0 %copy-start.4 = (s32[3]{0:T(128)S(1)}, s32[3]{0:T(128)}, u32[]{:S(2)}) copy-start(s32[3]{0:T(128)} %s.1) | copy-start | bytes 40
  0.0 6.1 %copy-start.2 = (s32[12,128]{1,0:T(8,128)S(1)}, s32[12,128]{1,0:T(8,128)}, u32[]{:S(2)}) copy-start(s32[12,128]{1,0:T(8,128)} %writes.1) | copy-start | bytes 18436
  0.0 6.1 %copy-start.1 = (s32[12,128]{1,0:T(8,128)S(1)}, s32[12,128]{1,0:T(8,128)}, u32[]{:S(2)}) copy-start(s32[12,128]{1,0:T(8,128)} %reads.1) | copy-start | bytes 18436
  2.8 30.0 %copy-start = (bf16[16,1,16,256]{3,2,1,0:T(8,128)(2,1)S(1)}, bf16[16,1,16,256]{3,2,1,0:T(8,128)(2,1)}, u32[]{:S(2)}) copy-start(bf16[16,1,16,256]{3,2,1,0:T(8,128)(2,1)} %param.15) | copy-start | bytes 393220
  2.8 8.8 %collective-permute-start = (bf16[416,128]{1,0:T(8,128)(2,1)S(1)}, bf16[416,128]{1,0:T(8,128)(2,1)S(1)}, u32[]{:S(2)}, u32[]{:S(2)}) collective-permute-start(bf16[416,128]{1,0:T(8,128)(2,1)S(1)} %get-tuple-element.28), channel_id=1, source_target_pairs={{0,1},{1,0},{2,3},{3,2},{4,5},{5,4},{6,7},{7,6},{8,9},{9,8},{10,11... | collective-permute-start | bytes 319496 | tf_op jit(solution)/shard_map/ppermute | solution.py:243
  12.2 20.6 %collective-permute-start.1 = (bf16[384,128]{1,0:T(8,128)(2,1)S(1)}, bf16[384,128]{1,0:T(8,128)(2,1)S(1)}, u32[]{:S(2)}, u32[]{:S(2)}) collective-permute-start(bf16[384,128]{1,0:T(8,128)(2,1)S(1)} %relay.1), channel_id=1, source_target_pairs={{0,32},{1,33},{2,34},{3,35},{4,36},{5,37},{6,38},{7,39},{8,40},{9,... | collective-permute-start | bytes 294920 | tf_op jit(solution)/shard_map/ppermute | solution.py:332
  18.0 10.7 %collective-permute-start.2 = (bf16[16,256]{1,0:T(8,128)(2,1)S(1)}, bf16[16,256]{1,0:T(8,128)(2,1)S(1)}, u32[]{:S(2)}, u32[]{:S(2)}) collective-permute-start(bf16[16,256]{1,0:T(8,128)(2,1)S(1)} %get-tuple-element.34), channel_id=1, source_target_pairs={{0,128},{128,0},{256,384},{384,256},{1,129},{129,1},{257,385},{385... | collective-permute-start | bytes 24584 | tf_op jit(solution)/shard_map/ppermute | solution.py:243
  21.1 7.5 %collective-permute-start.3 = (bf16[16,256]{1,0:T(8,128)(2,1)S(1)}, bf16[16,256]{1,0:T(8,128)(2,1)S(1)}, u32[]{:S(2)}, u32[]{:S(2)}) collective-permute-start(bf16[16,256]{1,0:T(8,128)(2,1)S(1)} %get-tuple-element.35), channel_id=1, source_target_pairs={{128,256},{256,128},{129,257},{257,129},{130,258},{258,130},{131,2... | collective-permute-start | bytes 24584 | tf_op jit(solution)/shard_map/ppermute | solution.py:243
  25.0 7.7 %collective-permute-start.4 = (bf16[16,256]{1,0:T(8,128)(2,1)S(1)}, bf16[16,256]{1,0:T(8,128)(2,1)S(1)}, u32[]{:S(2)}, u32[]{:S(2)}) collective-permute-start(bf16[16,256]{1,0:T(8,128)(2,1)S(1)} %get-tuple-element.36), channel_id=1, source_target_pairs={{1,2},{2,1},{3,4},{4,3},{5,6},{6,5},{7,8},{8,7},{9,10},{10,9},{11,... | collective-permute-start | bytes 24584 | tf_op jit(solution)/shard_map/ppermute | solution.py:243
  33.6 10.6 %collective-permute-start.5 = (bf16[16,256]{1,0:T(8,128)(2,1)S(1)}, bf16[16,256]{1,0:T(8,128)(2,1)S(1)}, u32[]{:S(2)}, u32[]{:S(2)}) collective-permute-start(bf16[16,256]{1,0:T(8,128)(2,1)S(1)} %get-tuple-element.39), channel_id=1, source_target_pairs={{0,128},{128,0},{256,384},{384,256},{1,129},{129,1},{257,385},{385... | collective-permute-start | bytes 24584 | tf_op jit(solution)/shard_map/ppermute | solution.py:243
  35.6 8.6 %collective-permute-start.6 = (bf16[16,256]{1,0:T(8,128)(2,1)S(1)}, bf16[16,256]{1,0:T(8,128)(2,1)S(1)}, u32[]{:S(2)}, u32[]{:S(2)}) collective-permute-start(bf16[16,256]{1,0:T(8,128)(2,1)S(1)} %get-tuple-element.40), channel_id=1, source_target_pairs={{128,256},{256,128},{129,257},{257,129},{130,258},{258,130},{131,2... | collective-permute-start | bytes 24584 | tf_op jit(solution)/shard_map/ppermute | solution.py:243
  38.6 5.6 %collective-permute-start.7 = (bf16[16,256]{1,0:T(8,128)(2,1)S(1)}, bf16[16,256]{1,0:T(8,128)(2,1)S(1)}, u32[]{:S(2)}, u32[]{:S(2)}) collective-permute-start(bf16[16,256]{1,0:T(8,128)(2,1)S(1)} %get-tuple-element.41), channel_id=1, source_target_pairs={{0,1},{1,0},{2,3},{3,2},{4,5},{5,4},{6,7},{7,6},{8,9},{9,8},{10,11... | collective-permute-start | bytes 24584 | tf_op jit(solution)/shard_map/ppermute | solution.py:243
  40.6 7.7 %collective-permute-start.8 = (bf16[16,256]{1,0:T(8,128)(2,1)S(1)}, bf16[16,256]{1,0:T(8,128)(2,1)S(1)}, u32[]{:S(2)}, u32[]{:S(2)}) collective-permute-start(bf16[16,256]{1,0:T(8,128)(2,1)S(1)} %get-tuple-element.42), channel_id=1, source_target_pairs={{1,2},{2,1},{3,4},{4,3},{5,6},{6,5},{7,8},{8,7},{9,10},{10,9},{11,... | collective-permute-start | bytes 24584 | tf_op jit(solution)/shard_map/ppermute | solution.py:243

commit v4 on v3

--- a/solution.py
+++ b/solution.py
@@ -16,7 +16,7 @@
 
 
 def params(mebibytes):
-    return pltpu.CompilerParams(vmem_limit_bytes=mebibytes << 20)
+    return pltpu.CompilerParams(vmem_limit_bytes=int(mebibytes * 1048576))
 
 
 def swap_route(count, bit):
@@ -33,18 +33,29 @@
 
 
 def grams_of(slots, order, fbuf, cbuf):
-    products = [dot(fbuf[i], cbuf[i], ((1,), (0,))) for i in range(len(slots))]
+    products = [dot(fbuf[i], cbuf[i], ((1,), (0,))).astype(BF16) for i in range(len(slots))]
     operators = []
     for slot, product in zip(slots, products):
-        width = product.shape[0] * (2 + order[slot]) // 4
-        keep = lax.broadcasted_iota(I32, product.shape, 0) < width
-        operators.append(jnp.where(keep, product, 0.0).astype(BF16))
+        rows = product.shape[0]
+        bounds = [rows * (2 + c) // 4 for c in range(3)]
+        parts = [product[: bounds[0]]]
+        for c in (1, 2):
+            part = product[bounds[c - 1] : bounds[c]]
+            parts.append(jnp.where(order[slot] >= c, part, jnp.zeros_like(part)))
+        operators.append(jnp.concatenate(parts, axis=0))
     return [dot(operator, operator, ((0,), (0,))) for operator in operators]
 
 
 def one_hot(index, rows):
-    hit = lax.broadcasted_iota(I32, (rows, index.shape[1]), 0) == index
-    return jnp.where(hit, 1.0, 0.0).astype(BF16)
+    tile = 16
+    shape = (tile, index.shape[1])
+    here = lax.broadcasted_iota(I32, shape, 0) == (index & (tile - 1))
+    block = jnp.where(here, index >> 4, -1).astype(F32).astype(BF16)
+    one, zero = jnp.ones(shape, BF16), jnp.zeros(shape, BF16)
+    return jnp.concatenate(
+        [jnp.where(block == jnp.full(shape, i, BF16), one, zero) for i in range(rows // tile)],
+        axis=0,
+    )
 
 
 def parities():
@@ -132,67 +143,80 @@
 
 
 def kept_kernel(
-    fx, fz, f, s, order, reads, writes, factor, coupling, given, part, moved_to, moved_from,
-    fbuf, cbuf, to, origin, kept, sem,
+    fx, fz, f, s, order, reads, writes, factor, coupling,
+    given, part, moved_to, moved_from, relayed,
+    to, origin, left, grams, places, rest,
 ):
     slots, moves = reads.shape[0], f.shape[0]
     unknowns = reads.shape[1]
     most = slots - moves
     own, cells = fx * fz, origin.shape[0]
-    for i in range(slots):
-        kept[i] = 0
+
+    def among(slot, moved):
+        found = moved[0] == slot
+        for j in range(1, moves):
+            found = found | (moved[j] == slot)
+        return found
+
     count = jnp.int32(0)
     for slot in range(slots):
-        moved = f[0] == slot
-        for i in range(moves):
-            moved = moved | (f[i] == slot) | (s[i] == slot)
-        kept[count] = slot
-        count = count + jnp.where(moved, 0, 1)
-    wanted = [s[i] for i in range(moves)] + [kept[i] for i in range(most)]
-    copies = fetch(wanted, factor, coupling, fbuf, cbuf, sem)
+        rest[count] = slot
+        count = count + jnp.where(among(slot, f), 0, 1)
+    wanted = [rest[i] for i in range(most)]
+    places[...] = cell_of(reads[...], fx, fz)
 
     def place(slot, valid, to_ref, from_ref, i):
-        read = jnp.where(valid, cell_of(reads[pl.ds(slot, 1), :], fx, fz), -1)
+        read = jnp.where(valid, places[pl.ds(slot, 1), :], -1)
         write = jnp.where(valid, writes[pl.ds(slot, 1), :], -1)
         columns = pl.ds(i * unknowns, unknowns)
         to_ref[:, columns] = one_hot(write, own)
         from_ref[:, columns] = one_hot(read, cells)
 
+    tile = (16, unknowns)
     for i in range(moves):
         place(s[i], True, moved_to, moved_from, i)
-        stays = f[i] != s[0]
-        for j in range(1, moves):
-            stays = stays & (f[i] != s[j])
-        place(f[i], stays, moved_to, moved_from, moves + i)
-    for i in range(most):
-        place(kept[i], i < count, to, origin, i)
-
-    waited(copies)
-    grams = grams_of(wanted, order, fbuf, cbuf)
+        place(f[i], jnp.logical_not(among(f[i], s)), moved_to, moved_from, moves + i)
+        for j in range(moves):
+            same = jnp.where(s[i] == f[j], 1.0, 0.0)
+            relayed[pl.ds((i * moves + j) * 16, 16), :] = jnp.full(tile, same, F32).astype(BF16)
+    for i, slot in enumerate(wanted):
+        place(slot, jnp.logical_not(among(slot, s)), to, origin, i)
+
+    factors, couplings = [factor[slot] for slot in wanted], [coupling[slot] for slot in wanted]
+    for i, exact in enumerate(grams_of(wanted, order, factors, couplings)):
+        columns = pl.ds(i * unknowns, unknowns)
+        high, low = halves(exact)
+        grams[columns, :] = high
+        scatter = to[:, columns]
+        spread = dot(
+            jnp.concatenate([scatter, scatter], axis=1),
+            jnp.concatenate([high, low], axis=0),
+            ((1,), (0,)),
+        )
+        high, low = halves(spread)
+        left[:own, columns] = high
+        left[own:, columns] = low
+    both = dot(left[...], origin[...], ((1,), (1,)))
+    part[...] = both[:own] + both[own:]
     for i in range(moves):
-        given[pl.ds(i * unknowns, unknowns), :] = grams[i].astype(BF16)
-    highs, lows = [], []
-    for i in range(most):
-        scatter = to[:, pl.ds(i * unknowns, unknowns)]
-        gram = jnp.concatenate(halves(grams[moves + i]), axis=0)
-        spread = dot(jnp.concatenate([scatter, scatter], axis=1), gram, ((1,), (0,)))
-        high, low = halves(spread)
-        highs.append(high)
-        lows.append(low)
-    left = jnp.concatenate(
-        [jnp.concatenate(highs, axis=1), jnp.concatenate(lows, axis=1)], axis=0
-    )
-    both = dot(left, origin[...], ((1,), (1,)))
-    part[...] = both[:own] + both[own:]
-
-
-def relay_kernel(f, s, given, got, out):
-    moves = f.shape[0]
+        at = s[i]
+        for j in range(moves):
+            at = at - jnp.where(f[j] < s[i], 1, 0)
+        at = jnp.minimum(at, most - 1)
+        source = pl.ds(pl.multiple_of(at * unknowns, unknowns), unknowns)
+        given[pl.ds(i * unknowns, unknowns), :] = grams[source, :]
+
+
+def relay_kernel(moves, relayed, given, got, out):
     unknowns = given.shape[0] // moves
     for i in range(moves):
         value = given[pl.ds(i * unknowns, unknowns), :]
         for j in range(moves):
-            value = jnp.where(s[i] == f[j], got[pl.ds(j * unknowns, unknowns), :], value)
+            same = relayed[pl.ds((i * moves + j) * 16, 16), :]
+            same = jnp.concatenate([same] * (unknowns // 16), axis=0)
+            value = jnp.where(
+                same > jnp.zeros_like(same), got[pl.ds(j * unknowns, unknowns), :], value
+            )
         out[pl.ds(i * unknowns, unknowns), :] = value
 
 
@@ -260,7 +284,6 @@
     def in_hbm(array):
         return pltpu.with_memory_space_constraint(array, pltpu.MemorySpace.HBM)
 
-    gram_factor, coupling = in_hbm(gram_factor), in_hbm(coupling)
 
     def element_cost(count):
         return pl.CostEstimate(
@@ -288,45 +311,52 @@
             pltpu.SemaphoreType.DMA((moves, 2)),
             pltpu.SemaphoreType.DMA((3,)),
         ],
-        compiler_params=params(12),
+        compiler_params=params(53),
         cost_estimate=element_cost(moves),
         name="given",
-    )(in_hbm(first_moves), in_hbm(order_class), gram_factor, coupling, in_hbm(field))
-    given, t0, t1, t3, second_moves = lax.optimization_barrier((given, t0, t1, t3, second_moves))
+    )(
+        in_hbm(first_moves), in_hbm(order_class), in_hbm(gram_factor), in_hbm(coupling),
+        in_hbm(field),
+    )
+    given, t0, t1, t3, gram_factor, coupling = lax.optimization_barrier(
+        (given, t0, t1, t3, gram_factor, coupling)
+    )
     got = swapped(given, "gz", 0)
 
-    given_s, part, moved_to, moved_from = pl.pallas_call(
+    given_s, part, moved_to, moved_from, same = pl.pallas_call(
         functools.partial(kept_kernel, fx, fz),
         out_shape=(
             grams,
             jax.ShapeDtypeStruct((own, cells), F32),
             jax.ShapeDtypeStruct((own, 2 * moves * unknowns), BF16),
             jax.ShapeDtypeStruct((cells, 2 * moves * unknowns), BF16),
+            jax.ShapeDtypeStruct((16 * moves * moves, unknowns), BF16),
         ),
-        in_specs=[SMEM] * 3 + [VMEM] * 2 + [HBM] * 2,
-        out_specs=(VMEM,) * 4,
+        in_specs=[SMEM] * 3 + [VMEM] * 4,
+        out_specs=(VMEM,) * 5,
         scratch_shapes=[
-            *buffers(slots),
             pltpu.VMEM((own, most * unknowns), BF16),
             pltpu.VMEM((cells, most * unknowns), BF16),
+            pltpu.VMEM((2 * own, most * unknowns), BF16),
+            pltpu.VMEM((most * unknowns, unknowns), BF16),
+            pltpu.VMEM((slots, unknowns), I32),
             pltpu.SMEM((slots,), I32),
-            pltpu.SemaphoreType.DMA((slots, 2)),
         ],
         compiler_params=params(24),
-        cost_estimate=element_cost(slots),
+        cost_estimate=element_cost(most),
         name="kept",
     )(
         first_moves, second_moves, order_class, trace_index, owner_index, gram_factor, coupling
     )
 
     relayed = pl.pallas_call(
-        relay_kernel,
+        functools.partial(relay_kernel, moves),
         out_shape=grams,
-        in_specs=[SMEM] * 2 + [VMEM] * 2,
+        in_specs=[VMEM] * 3,
         out_specs=VMEM,
         compiler_params=params(2),
         name="relay",
-    )(first_moves, second_moves, given_s, got)
+    )(same, given_s, got)
     both = lax.axis_size("gy") * lax.axis_size("gz")
     second_bit = lax.axis_size("gz").bit_length() - 1
     got_s = lax.ppermute(relayed, ("gy", "gz"), swap_route(both, second_bit))

time: 49.6 us -> 47.2 us (0.952)
  Pallas kernels: 10.6 us -> 8.01 us
  starting transfers between devices: 30.2 us -> 31.7 us
  waiting for transfers between devices: 8.16 us -> 6.84 us
    pallas_call x1, Pallas kernels: 5.47 us -> 2.92 us  [body(): pl.pallas_call(functools.partial(kept_kernel, fx, fz), out_shape=(grams,...]
    ppermute x8, starting transfers between devices: 24.4 us -> 25.9 us  [swapped(): return lax.ppermute(edge, axis, pairs(lax.axis_size(axis), odd))]
    ppermute x8, waiting for transfers between devices: 8.16 us -> 6.83 us  [swapped(): return lax.ppermute(edge, axis, pairs(lax.axis_size(axis), odd))]
    pallas_call x1, Pallas kernels: 0.58 us -> 0.03 us  [body(): pl.pallas_call(functools.partial(relay_kernel, moves), out_shape=grams, i...]
  transfers between devices with their start and end apart: 9 -> 9, of which waited for: 2 -> 2; matrix products, arithmetic and copies ran while one was open for 0% -> 0% of each run, Pallas kernels for 11% -> 6%
where the time goes in v4:
time: 47.2 us; the launch traced here: 46.9 us
  starting transfers between devices  31.7 us (67%)
  Pallas kernels  8.01 us (17%)
  waiting for transfers between devices  6.84 us (14%)
    ppermute x8, starting transfers between devices, swapped(): return lax.ppermute(edge, axis, pairs(lax.axis_size(axis), odd))  25.9 us
    ppermute x8, waiting for transfers between devices, swapped(): return lax.ppermute(edge, axis, pairs(lax.axis_size(axis), odd))  6.83 us
    ppermute x1, starting transfers between devices, body(): got_s = lax.ppermute(relayed, ('gy', 'gz'), swap_route(both, second_bit))  5.81 us
    pallas_call x1, Pallas kernels, body(): pl.pallas_call(functools.partial(given_kernel, fx, fz), out_shape=(load,...  3.18 us
    pallas_call x1, Pallas kernels, body(): pl.pallas_call(functools.partial(kept_kernel, fx, fz), out_shape=(grams,...  2.92 us
    pallas_call x1, Pallas kernels, body(): pl.pallas_call(second_kernel, out_shape=jax.ShapeDtypeStruct((own, column...  1 us
  transfers between devices with their start and end apart: 9, of which 2 were waited for; matrix products, arithmetic and copies ran while one was open for 0% of the time, Pallas kernels for 6%

profile of v4, /device:TPU:33, one launch (start us, length us, event | category | flops | bytes accessed | tf_op | source)
XLA Modules:
  0.0 46.9 jit_solution(13468629143630694174)
XLA Ops:
  0.0 0.0 copy-start.5
  0.0 0.0 copy-start.6
  0.0 0.0 copy-start.1
  0.0 0.0 copy-start
  0.0 0.0 copy-start.4
  0.0 0.0 copy-start.3
  0.0 0.0 copy-start.7
  0.0 3.2 %given.1 = (bf16[416,128]{1,0:T(8,128)(2,1)S(1)}, bf16[16,256]{1,0:T(8,128)(2,1)S(1)}, bf16[16,256]{1,0:T(8,128)(2,1)S(1)}, bf16[16,256]{1,0:T(8,128)(2,1)S(1)}) custom-call(s32[3]{0:T(128)} %f.1, s32[12]{0:T(128)} %order.1, bf16[12,384,384]{2,1,0:T(8,128)(2,1)} %factor.2, bf16[12,384,128]{2,1,0:T(8,128)(2,1)} %coupling.2, bf16[256,256]{1,0:T(8,128)(2,1)} %bitcast.4), custom_call_target="tpu_custom_call" | custom-call | flops 150994944 | bytes 1179648 | tf_op jit(solution)/shard_map/given/pallas_call | solution.py:301
  3.2 0.0 copy-start.2
  3.2 3.3 %collective-permute-start = (bf16[416,128]{1,0:T(8,128)(2,1)S(1)}, bf16[416,128]{1,0:T(8,128)(2,1)S(1)}, u32[]{:S(2)}, u32[]{:S(2)}) collective-permute-start(bf16[416,128]{1,0:T(8,128)(2,1)S(1)} %get-tuple-element.30), channel_id=1, source_target_pairs={{0,1},{1,0},{2,3},{3,2},{4,5},{5,4},{6,7},{7,6},{8,9},{9,8},{10,11... | collective-permute-start | bytes 319496 | tf_op jit(solution)/shard_map/ppermute | solution.py:267
  6.5 0.0 copy-done.5
  6.5 0.0 copy-done.6
  6.5 0.0 copy-done.1
  6.5 0.0 copy-done
  6.5 0.0 copy-done.4
  6.6 0.0 copy-done.3
  6.6 0.0 copy-done.7
  6.6 2.9 %kept.1 = (bf16[384,128]{1,0:T(8,128)(2,1)S(1)}, f32[256,320]{1,0:T(8,128)S(1)}, bf16[256,768]{1,0:T(8,128)(2,1)S(1)}, bf16[320,768]{1,0:T(8,128)(2,1)S(1)}, bf16[144,128]{1,0:T(8,128)(2,1)S(1)}) custom-call(s32[3]{0:T(128)S(1)} %copy-done.5, s32[3]{0:T(128)S(1)} %copy-done.7, s32[12]{0:T(128)S(1)} %copy-done.6, s32[12,128]{1,0:T(8,128)S(1)} %copy-done.3, ...), custom_call_target="tpu_custom_call" | custom-call | flops 452984832 | bytes 3538944 | tf_op jit(solution)/shard_map/kept/pallas_call | solution.py:326
  9.5 0.0 collective-permute-done.got
  9.5 5.8 %collective-permute-start.1 = (bf16[384,128]{1,0:T(8,128)(2,1)S(1)}, bf16[384,128]{1,0:T(8,128)(2,1)S(1)}, u32[]{:S(2)}, u32[]{:S(2)}) collective-permute-start(bf16[384,128]{1,0:T(8,128)(2,1)S(1)} %relay.1), channel_id=1, source_target_pairs={{0,32},{1,33},{2,34},{3,35},{4,36},{5,37},{6,38},{7,39},{8,40},{9,... | collective-permute-start | bytes 294920 | tf_op jit(solution)/shard_map/ppermute | solution.py:362
  15.4 3.3 %collective-permute-start.2 = (bf16[16,256]{1,0:T(8,128)(2,1)S(1)}, bf16[16,256]{1,0:T(8,128)(2,1)S(1)}, u32[]{:S(2)}, u32[]{:S(2)}) collective-permute-start(bf16[16,256]{1,0:T(8,128)(2,1)S(1)} %get-tuple-element.38), channel_id=1, source_target_pairs={{0,128},{128,0},{256,384},{384,256},{1,129},{129,1},{257,385},{385... | collective-permute-start | bytes 24584 | tf_op jit(solution)/shard_map/ppermute | solution.py:267
  18.7 3.9 %collective-permute-start.3 = (bf16[16,256]{1,0:T(8,128)(2,1)S(1)}, bf16[16,256]{1,0:T(8,128)(2,1)S(1)}, u32[]{:S(2)}, u32[]{:S(2)}) collective-permute-start(bf16[16,256]{1,0:T(8,128)(2,1)S(1)} %get-tuple-element.39), channel_id=1, source_target_pairs={{128,256},{256,128},{129,257},{257,129},{130,258},{258,130},{131,2... | collective-permute-start | bytes 24584 | tf_op jit(solution)/shard_map/ppermute | solution.py:267
  22.6 4.3 %collective-permute-start.4 = (bf16[16,256]{1,0:T(8,128)(2,1)S(1)}, bf16[16,256]{1,0:T(8,128)(2,1)S(1)}, u32[]{:S(2)}, u32[]{:S(2)}) collective-permute-start(bf16[16,256]{1,0:T(8,128)(2,1)S(1)} %get-tuple-element.40), channel_id=1, source_target_pairs={{1,2},{2,1},{3,4},{4,3},{5,6},{6,5},{7,8},{8,7},{9,10},{10,9},{11,... | collective-permute-start | bytes 24584 | tf_op jit(solution)/shard_map/ppermute | solution.py:267
  26.9 0.0 collective-permute-done.2.h0
  26.9 0.0 collective-permute-done.3.h1
  26.9 3.4 %collective-permute-done.4.h3 = bf16[16,256]{1,0:T(8,128)(2,1)S(1)} collective-permute-done((bf16[16,256]{1,0:T(8,128)(2,1)S(1)}, bf16[16,256]{1,0:T(8,128)(2,1)S(1)}, u32[]{:S(2)}, u32[]{:S(2)}) %collective-permute-start.4) | collective-permute-done | bytes 8224 | tf_op jit(solution)/shard_map/ppermute | solution.py:267
  30.3 0.0 collective-permute-done.1.got_s
  30.3 0.0 copy-done.2
  30.3 0.9 %first.1 = (bf16[512,320]{1,0:T(8,128)(2,1)S(1)}, bf16[256,256]{1,0:T(8,128)(2,1)S(1)}, bf16[16,256]{1,0:T(8,128)(2,1)S(1)}, bf16[16,256]{1,0:T(8,128)(2,1)S(1)}...) custom-call(bf16[416,128]{1,0:T(8,128)(2,1)S(1)} %collective-permute-done.got, ...), custom_call_target="tpu_custom_call" | custom-call | tf_op jit(solution)/shard_map/first/pallas_call | solution.py:367
  31.2 1.9 %collective-permute-start.5 = (bf16[16,256]{1,0:T(8,128)(2,1)S(1)}, bf16[16,256]{1,0:T(8,128)(2,1)S(1)}, u32[]{:S(2)}, u32[]{:S(2)}) collective-permute-start(bf16[16,256]{1,0:T(8,128)(2,1)S(1)} %get-tuple-element.43), channel_id=1, source_target_pairs={{0,128},{128,0},{256,384},{384,256},{1,129},{129,1},{257,385},{385... | collective-permute-start | bytes 24584 | tf_op jit(solution)/shard_map/ppermute | solution.py:267
  33.1 3.1 %collective-permute-start.6 = (bf16[16,256]{1,0:T(8,128)(2,1)S(1)}, bf16[16,256]{1,0:T(8,128)(2,1)S(1)}, u32[]{:S(2)}, u32[]{:S(2)}) collective-permute-start(bf16[16,256]{1,0:T(8,128)(2,1)S(1)} %get-tuple-element.44), channel_id=1, source_target_pairs={{128,256},{256,128},{129,257},{257,129},{130,258},{258,130},{131,2... | collective-permute-start | bytes 24584 | tf_op jit(solution)/shard_map/ppermute | solution.py:267
  36.2 1.9 %collective-permute-start.7 = (bf16[16,256]{1,0:T(8,128)(2,1)S(1)}, bf16[16,256]{1,0:T(8,128)(2,1)S(1)}, u32[]{:S(2)}, u32[]{:S(2)}) collective-permute-start(bf16[16,256]{1,0:T(8,128)(2,1)S(1)} %get-tuple-element.45), channel_id=1, source_target_pairs={{0,1},{1,0},{2,3},{3,2},{4,5},{5,4},{6,7},{7,6},{8,9},{9,8},{10,11... | collective-permute-start | bytes 24584 | tf_op jit(solution)/shard_map/ppermute | solution.py:267
  38.1 4.3 %collective-permute-start.8 = (bf16[16,256]{1,0:T(8,128)(2,1)S(1)}, bf16[16,256]{1,0:T(8,128)(2,1)S(1)}, u32[]{:S(2)}, u32[]{:S(2)}) collective-permute-start(bf16[16,256]{1,0:T(8,128)(2,1)S(1)} %get-tuple-element.46), channel_id=1, source_target_pairs={{1,2},{2,1},{3,4},{4,3},{5,6},{6,5},{7,8},{8,7},{9,10},{10,9},{11,... | collective-permute-start | bytes 24584 | tf_op jit(solution)/shard_map/ppermute | solution.py:267
  42.4 0.0 collective-permute-done.5.h0
  42.4 0.0 collective-permute-done.6.h1
  42.4 0.0 collective-permute-done.7.h2
  42.5 3.4 %collective-permute-done.8.h3 = bf16[16,256]{1,0:T(8,128)(2,1)S(1)} collective-permute-done((bf16[16,256]{1,0:T(8,128)(2,1)S(1)}, bf16[16,256]{1,0:T(8,128)(2,1)S(1)}, u32[]{:S(2)}, u32[]{:S(2)}) %collective-permute-start.8) | collective-permute-done | bytes 8224 | tf_op jit(solution)/shard_map/ppermute | solution.py:267
  45.9 1.0 %second.1 = f32[256,256]{1,0:T(8,128)} custom-call(bf16[512,320]{1,0:T(8,128)(2,1)S(1)} %get-tuple-element.41.matrix, bf16[256,256]{1,0:T(8,128)(2,1)S(1)} %get-tuple-element.42.first, bf16[16,256]{1,0:T(8,128)(2,1)S(1)} %collective-permute-done.5.h0, bf16[16,256]{1,0:T(8,128)(2,1)S(1)} %collective-permute-done.6.h1, ...), custom_call_target="tpu_custom_call" | custom-call | tf_op jit(solution)/shard_map/second/pallas_call | solution.py:385
  (1 shorter events, 0.0 us)
Async XLA Ops:
  0.0 6.5 %copy-start.5 = (s32[3]{0:T(128)S(1)}, s32[3]{0:T(128)}, u32[]{:S(2)}) copy-start(s32[3]{0:T(128)} %f.1) | copy-start | bytes 40
  0.0 6.5 %copy-start.6 = (s32[12]{0:T(128)S(1)}, s32[12]{0:T(128)}, u32[]{:S(2)}) copy-start(s32[12]{0:T(128)} %order.1) | copy-start | bytes 148
  0.0 6.5 %copy-start.1 = (bf16[12,384,128]{2,1,0:T(8,128)(2,1)S(1)}, bf16[12,384,128]{2,1,0:T(8,128)(2,1)}, u32[]{:S(2)}) copy-start(bf16[12,384,128]{2,1,0:T(8,128)(2,1)} %coupling.2) | copy-start | bytes 3538948
  0.0 6.5 %copy-start = (bf16[12,384,384]{2,1,0:T(8,128)(2,1)S(1)}, bf16[12,384,384]{2,1,0:T(8,128)(2,1)}, u32[]{:S(2)}) copy-start(bf16[12,384,384]{2,1,0:T(8,128)(2,1)} %factor.2) | copy-start | bytes 10616836
  0.0 6.5 %copy-start.4 = (s32[12,128]{1,0:T(8,128)S(1)}, s32[12,128]{1,0:T(8,128)}, u32[]{:S(2)}) copy-start(s32[12,128]{1,0:T(8,128)} %writes.1) | copy-start | bytes 18436
  0.0 6.5 %copy-start.3 = (s32[12,128]{1,0:T(8,128)S(1)}, s32[12,128]{1,0:T(8,128)}, u32[]{:S(2)}) copy-start(s32[12,128]{1,0:T(8,128)} %reads.1) | copy-start | bytes 18436
  0.0 6.5 %copy-start.7 = (s32[3]{0:T(128)S(1)}, s32[3]{0:T(128)}, u32[]{:S(2)}) copy-start(s32[3]{0:T(128)} %s.1) | copy-start | bytes 40
  3.2 27.1 %copy-start.2 = (bf16[16,1,16,256]{3,2,1,0:T(8,128)(2,1)S(1)}, bf16[16,1,16,256]{3,2,1,0:T(8,128)(2,1)}, u32[]{:S(2)}) copy-start(bf16[16,1,16,256]{3,2,1,0:T(8,128)(2,1)} %param.15) | copy-start | bytes 393220
  3.2 6.3 %collective-permute-start = (bf16[416,128]{1,0:T(8,128)(2,1)S(1)}, bf16[416,128]{1,0:T(8,128)(2,1)S(1)}, u32[]{:S(2)}, u32[]{:S(2)}) collective-permute-start(bf16[416,128]{1,0:T(8,128)(2,1)S(1)} %get-tuple-element.30), channel_id=1, source_target_pairs={{0,1},{1,0},{2,3},{3,2},{4,5},{5,4},{6,7},{7,6},{8,9},{9,8},{10,11... | collective-permute-start | bytes 319496 | tf_op jit(solution)/shard_map/ppermute | solution.py:267
  9.5 20.8 %collective-permute-start.1 = (bf16[384,128]{1,0:T(8,128)(2,1)S(1)}, bf16[384,128]{1,0:T(8,128)(2,1)S(1)}, u32[]{:S(2)}, u32[]{:S(2)}) collective-permute-start(bf16[384,128]{1,0:T(8,128)(2,1)S(1)} %relay.1), channel_id=1, source_target_pairs={{0,32},{1,33},{2,34},{3,35},{4,36},{5,37},{6,38},{7,39},{8,40},{9,... | collective-permute-start | bytes 294920 | tf_op jit(solution)/shard_map/ppermute | solution.py:362
  15.4 11.5 %collective-permute-start.2 = (bf16[16,256]{1,0:T(8,128)(2,1)S(1)}, bf16[16,256]{1,0:T(8,128)(2,1)S(1)}, u32[]{:S(2)}, u32[]{:S(2)}) collective-permute-start(bf16[16,256]{1,0:T(8,128)(2,1)S(1)} %get-tuple-element.38), channel_id=1, source_target_pairs={{0,128},{128,0},{256,384},{384,256},{1,129},{129,1},{257,385},{385... | collective-permute-start | bytes 24584 | tf_op jit(solution)/shard_map/ppermute | solution.py:267
  18.7 8.2 %collective-permute-start.3 = (bf16[16,256]{1,0:T(8,128)(2,1)S(1)}, bf16[16,256]{1,0:T(8,128)(2,1)S(1)}, u32[]{:S(2)}, u32[]{:S(2)}) collective-permute-start(bf16[16,256]{1,0:T(8,128)(2,1)S(1)} %get-tuple-element.39), channel_id=1, source_target_pairs={{128,256},{256,128},{129,257},{257,129},{130,258},{258,130},{131,2... | collective-permute-start | bytes 24584 | tf_op jit(solution)/shard_map/ppermute | solution.py:267
  22.6 7.7 %collective-permute-start.4 = (bf16[16,256]{1,0:T(8,128)(2,1)S(1)}, bf16[16,256]{1,0:T(8,128)(2,1)S(1)}, u32[]{:S(2)}, u32[]{:S(2)}) collective-permute-start(bf16[16,256]{1,0:T(8,128)(2,1)S(1)} %get-tuple-element.40), channel_id=1, source_target_pairs={{1,2},{2,1},{3,4},{4,3},{5,6},{6,5},{7,8},{8,7},{9,10},{10,9},{11,... | collective-permute-start | bytes 24584 | tf_op jit(solution)/shard_map/ppermute | solution.py:267
  31.2 11.2 %collective-permute-start.5 = (bf16[16,256]{1,0:T(8,128)(2,1)S(1)}, bf16[16,256]{1,0:T(8,128)(2,1)S(1)}, u32[]{:S(2)}, u32[]{:S(2)}) collective-permute-start(bf16[16,256]{1,0:T(8,128)(2,1)S(1)} %get-tuple-element.43), channel_id=1, source_target_pairs={{0,128},{128,0},{256,384},{384,256},{1,129},{129,1},{257,385},{385... | collective-permute-start | bytes 24584 | tf_op jit(solution)/shard_map/ppermute | solution.py:267
  33.1 9.3 %collective-permute-start.6 = (bf16[16,256]{1,0:T(8,128)(2,1)S(1)}, bf16[16,256]{1,0:T(8,128)(2,1)S(1)}, u32[]{:S(2)}, u32[]{:S(2)}) collective-permute-start(bf16[16,256]{1,0:T(8,128)(2,1)S(1)} %get-tuple-element.44), channel_id=1, source_target_pairs={{128,256},{256,128},{129,257},{257,129},{130,258},{258,130},{131,2... | collective-permute-start | bytes 24584 | tf_op jit(solution)/shard_map/ppermute | solution.py:267
  36.2 6.2 %collective-permute-start.7 = (bf16[16,256]{1,0:T(8,128)(2,1)S(1)}, bf16[16,256]{1,0:T(8,128)(2,1)S(1)}, u32[]{:S(2)}, u32[]{:S(2)}) collective-permute-start(bf16[16,256]{1,0:T(8,128)(2,1)S(1)} %get-tuple-element.45), channel_id=1, source_target_pairs={{0,1},{1,0},{2,3},{3,2},{4,5},{5,4},{6,7},{7,6},{8,9},{9,8},{10,11... | collective-permute-start | bytes 24584 | tf_op jit(solution)/shard_map/ppermute | solution.py:267
  38.1 7.7 %collective-permute-start.8 = (bf16[16,256]{1,0:T(8,128)(2,1)S(1)}, bf16[16,256]{1,0:T(8,128)(2,1)S(1)}, u32[]{:S(2)}, u32[]{:S(2)}) collective-permute-start(bf16[16,256]{1,0:T(8,128)(2,1)S(1)} %get-tuple-element.46), channel_id=1, source_target_pairs={{1,2},{2,1},{3,4},{4,3},{5,6},{6,5},{7,8},{8,7},{9,10},{10,9},{11,... | collective-permute-start | bytes 24584 | tf_op jit(solution)/shard_map/ppermute | solution.py:267

commit v5 on v4

--- a/solution.py
+++ b/solution.py
@@ -251,9 +251,17 @@
     e0[...], e1[...], e2[...], e3[...] = edges_of(field, fx, fz)
 
 
+def own_kernel(matrix, first, out):
+    own = first.shape[0]
+    both = dot(matrix[:, :own], first[...], ((1,), (0,)))
+    out[...] = both[:own] + both[own:]
+
+
 def second_kernel(matrix, first, h0, h1, h2, h3, out):
+    own = first.shape[0]
     frame = jnp.concatenate([h0[...], h1[...], h2[...], h3[...]], axis=0)
-    out[...] = applied(matrix[...], first[...], frame)
+    both = dot(matrix[:, own:], frame, ((1,), (0,)))
+    out[...] = first[...] + (both[:own] + both[own:])
 
 
 def pairs(count, odd):
@@ -382,6 +390,14 @@
     h2 = swapped(e2, "gz", 0)
     h3 = swapped(e3, "gz", 1)
     h0 = swapped(e0, "gx", 0)
+    inner = pl.pallas_call(
+        own_kernel,
+        out_shape=jax.ShapeDtypeStruct((own, columns), F32),
+        in_specs=[VMEM] * 2,
+        out_specs=VMEM,
+        compiler_params=params(4),
+        name="own",
+    )(matrix, first)
     second = pl.pallas_call(
         second_kernel,
         out_shape=jax.ShapeDtypeStruct((own, columns), F32),
@@ -389,7 +405,7 @@
         out_specs=VMEM,
         compiler_params=params(6),
         name="second",
-    )(matrix, first, h0, h1, h2, h3)
+    )(matrix, inner, h0, h1, h2, h3)
     return second.reshape(traces.shape)
 
 

time: 47.2 us -> 47.1 us (level)
  transfers between devices with their start and end apart: 9 -> 9, of which waited for: 2 -> 2; matrix products, arithmetic and copies ran while one was open for 0% -> 0% of each run, Pallas kernels for 6% -> 7%
where the time goes in v5:
time: 47.1 us; the launch traced here: 46.8 us
  starting transfers between devices  31.7 us (67%)
  Pallas kernels  8.14 us (17%)
  waiting for transfers between devices  6.6 us (14%)
    ppermute x8, starting transfers between devices, swapped(): return lax.ppermute(edge, axis, pairs(lax.axis_size(axis), odd))  25.9 us
    ppermute x8, waiting for transfers between devices, swapped(): return lax.ppermute(edge, axis, pairs(lax.axis_size(axis), odd))  6.6 us
    ppermute x1, starting transfers between devices, body(): got_s = lax.ppermute(relayed, ('gy', 'gz'), swap_route(both, second_bit))  5.81 us
    pallas_call x1, Pallas kernels, body(): pl.pallas_call(functools.partial(given_kernel, fx, fz), out_shape=(load,...  3.18 us
    pallas_call x1, Pallas kernels, body(): pl.pallas_call(functools.partial(kept_kernel, fx, fz), out_shape=(grams,...  2.92 us
  transfers between devices with their start and end apart: 9, of which 2 were waited for; matrix products, arithmetic and copies ran while one was open for 0% of the time, Pallas kernels for 7%

profile of v5, /device:TPU:33, one launch (start us, length us, event | category | flops | bytes accessed | tf_op | source)
XLA Modules:
  0.0 46.8 jit_solution(8394323189451347113)
XLA Ops:
  0.0 0.0 copy-start.5
  0.0 0.0 copy-start.6
  0.0 0.0 copy-start.1
  0.0 0.0 copy-start
  0.0 0.0 copy-start.4
  0.0 0.0 copy-start.3
  0.0 0.0 copy-start.7
  0.0 3.2 %given.1 = (bf16[416,128]{1,0:T(8,128)(2,1)S(1)}, bf16[16,256]{1,0:T(8,128)(2,1)S(1)}, bf16[16,256]{1,0:T(8,128)(2,1)S(1)}, bf16[16,256]{1,0:T(8,128)(2,1)S(1)}) custom-call(s32[3]{0:T(128)} %f.1, s32[12]{0:T(128)} %order.1, bf16[12,384,384]{2,1,0:T(8,128)(2,1)} %factor.2, bf16[12,384,128]{2,1,0:T(8,128)(2,1)} %coupling.2, bf16[256,256]{1,0:T(8,128)(2,1)} %bitcast.4), custom_call_target="tpu_custom_call" | custom-call | flops 150994944 | bytes 1179648 | tf_op jit(solution)/shard_map/given/pallas_call | solution.py:309
  3.2 0.0 copy-start.2
  3.2 3.3 %collective-permute-start = (bf16[416,128]{1,0:T(8,128)(2,1)S(1)}, bf16[416,128]{1,0:T(8,128)(2,1)S(1)}, u32[]{:S(2)}, u32[]{:S(2)}) collective-permute-start(bf16[416,128]{1,0:T(8,128)(2,1)S(1)} %get-tuple-element.30), channel_id=1, source_target_pairs={{0,1},{1,0},{2,3},{3,2},{4,5},{5,4},{6,7},{7,6},{8,9},{9,8},{10,11... | collective-permute-start | bytes 319496 | tf_op jit(solution)/shard_map/ppermute | solution.py:275
  6.5 0.0 copy-done.5
  6.5 0.0 copy-done.6
  6.5 0.0 copy-done.1
  6.5 0.0 copy-done
  6.5 0.0 copy-done.4
  6.6 0.0 copy-done.3
  6.6 0.0 copy-done.7
  6.6 2.9 %kept.1 = (bf16[384,128]{1,0:T(8,128)(2,1)S(1)}, f32[256,320]{1,0:T(8,128)S(1)}, bf16[256,768]{1,0:T(8,128)(2,1)S(1)}, bf16[320,768]{1,0:T(8,128)(2,1)S(1)}, bf16[144,128]{1,0:T(8,128)(2,1)S(1)}) custom-call(s32[3]{0:T(128)S(1)} %copy-done.5, s32[3]{0:T(128)S(1)} %copy-done.7, s32[12]{0:T(128)S(1)} %copy-done.6, s32[12,128]{1,0:T(8,128)S(1)} %copy-done.3, ...), custom_call_target="tpu_custom_call" | custom-call | flops 452984832 | bytes 3538944 | tf_op jit(solution)/shard_map/kept/pallas_call | solution.py:334
  9.5 0.0 collective-permute-done.got
  9.5 5.8 %collective-permute-start.1 = (bf16[384,128]{1,0:T(8,128)(2,1)S(1)}, bf16[384,128]{1,0:T(8,128)(2,1)S(1)}, u32[]{:S(2)}, u32[]{:S(2)}) collective-permute-start(bf16[384,128]{1,0:T(8,128)(2,1)S(1)} %relay.1), channel_id=1, source_target_pairs={{0,32},{1,33},{2,34},{3,35},{4,36},{5,37},{6,38},{7,39},{8,40},{9,... | collective-permute-start | bytes 294920 | tf_op jit(solution)/shard_map/ppermute | solution.py:370
  15.4 3.3 %collective-permute-start.2 = (bf16[16,256]{1,0:T(8,128)(2,1)S(1)}, bf16[16,256]{1,0:T(8,128)(2,1)S(1)}, u32[]{:S(2)}, u32[]{:S(2)}) collective-permute-start(bf16[16,256]{1,0:T(8,128)(2,1)S(1)} %get-tuple-element.38), channel_id=1, source_target_pairs={{0,128},{128,0},{256,384},{384,256},{1,129},{129,1},{257,385},{385... | collective-permute-start | bytes 24584 | tf_op jit(solution)/shard_map/ppermute | solution.py:275
  18.7 3.9 %collective-permute-start.3 = (bf16[16,256]{1,0:T(8,128)(2,1)S(1)}, bf16[16,256]{1,0:T(8,128)(2,1)S(1)}, u32[]{:S(2)}, u32[]{:S(2)}) collective-permute-start(bf16[16,256]{1,0:T(8,128)(2,1)S(1)} %get-tuple-element.39), channel_id=1, source_target_pairs={{128,256},{256,128},{129,257},{257,129},{130,258},{258,130},{131,2... | collective-permute-start | bytes 24584 | tf_op jit(solution)/shard_map/ppermute | solution.py:275
  22.6 4.3 %collective-permute-start.4 = (bf16[16,256]{1,0:T(8,128)(2,1)S(1)}, bf16[16,256]{1,0:T(8,128)(2,1)S(1)}, u32[]{:S(2)}, u32[]{:S(2)}) collective-permute-start(bf16[16,256]{1,0:T(8,128)(2,1)S(1)} %get-tuple-element.40), channel_id=1, source_target_pairs={{1,2},{2,1},{3,4},{4,3},{5,6},{6,5},{7,8},{8,7},{9,10},{10,9},{11,... | collective-permute-start | bytes 24584 | tf_op jit(solution)/shard_map/ppermute | solution.py:275
  26.9 0.0 collective-permute-done.2.h0
  26.9 0.0 collective-permute-done.3.h1
  26.9 3.4 %collective-permute-done.4.h3 = bf16[16,256]{1,0:T(8,128)(2,1)S(1)} collective-permute-done((bf16[16,256]{1,0:T(8,128)(2,1)S(1)}, bf16[16,256]{1,0:T(8,128)(2,1)S(1)}, u32[]{:S(2)}, u32[]{:S(2)}) %collective-permute-start.4) | collective-permute-done | bytes 8224 | tf_op jit(solution)/shard_map/ppermute | solution.py:275
  30.3 0.0 collective-permute-done.1.got_s
  30.3 0.0 copy-done.2
  30.3 0.9 %first.1 = (bf16[512,320]{1,0:T(8,128)(2,1)S(1)}, bf16[256,256]{1,0:T(8,128)(2,1)S(1)}, bf16[16,256]{1,0:T(8,128)(2,1)S(1)}, bf16[16,256]{1,0:T(8,128)(2,1)S(1)}...) custom-call(bf16[416,128]{1,0:T(8,128)(2,1)S(1)} %collective-permute-done.got, ...), custom_call_target="tpu_custom_call" | custom-call | tf_op jit(solution)/shard_map/first/pallas_call | solution.py:375
  31.2 1.9 %collective-permute-start.5 = (bf16[16,256]{1,0:T(8,128)(2,1)S(1)}, bf16[16,256]{1,0:T(8,128)(2,1)S(1)}, u32[]{:S(2)}, u32[]{:S(2)}) collective-permute-start(bf16[16,256]{1,0:T(8,128)(2,1)S(1)} %get-tuple-element.43), channel_id=1, source_target_pairs={{0,128},{128,0},{256,384},{384,256},{1,129},{129,1},{257,385},{385... | collective-permute-start | bytes 24584 | tf_op jit(solution)/shard_map/ppermute | solution.py:275
  33.1 3.1 %collective-permute-start.6 = (bf16[16,256]{1,0:T(8,128)(2,1)S(1)}, bf16[16,256]{1,0:T(8,128)(2,1)S(1)}, u32[]{:S(2)}, u32[]{:S(2)}) collective-permute-start(bf16[16,256]{1,0:T(8,128)(2,1)S(1)} %get-tuple-element.44), channel_id=1, source_target_pairs={{128,256},{256,128},{129,257},{257,129},{130,258},{258,130},{131,2... | collective-permute-start | bytes 24584 | tf_op jit(solution)/shard_map/ppermute | solution.py:275
  36.2 1.9 %collective-permute-start.7 = (bf16[16,256]{1,0:T(8,128)(2,1)S(1)}, bf16[16,256]{1,0:T(8,128)(2,1)S(1)}, u32[]{:S(2)}, u32[]{:S(2)}) collective-permute-start(bf16[16,256]{1,0:T(8,128)(2,1)S(1)} %get-tuple-element.45), channel_id=1, source_target_pairs={{0,1},{1,0},{2,3},{3,2},{4,5},{5,4},{6,7},{7,6},{8,9},{9,8},{10,11... | collective-permute-start | bytes 24584 | tf_op jit(solution)/shard_map/ppermute | solution.py:275
  38.1 4.3 %collective-permute-start.8 = (bf16[16,256]{1,0:T(8,128)(2,1)S(1)}, bf16[16,256]{1,0:T(8,128)(2,1)S(1)}, u32[]{:S(2)}, u32[]{:S(2)}) collective-permute-start(bf16[16,256]{1,0:T(8,128)(2,1)S(1)} %get-tuple-element.46), channel_id=1, source_target_pairs={{1,2},{2,1},{3,4},{4,3},{5,6},{6,5},{7,8},{8,7},{9,10},{10,9},{11,... | collective-permute-start | bytes 24584 | tf_op jit(solution)/shard_map/ppermute | solution.py:275
  42.4 0.2 own.1.first
  42.7 0.0 collective-permute-done.5.h0
  42.7 0.0 collective-permute-done.6.h1
  42.7 0.0 collective-permute-done.7.h2
  42.7 3.2 %collective-permute-done.8.h3 = bf16[16,256]{1,0:T(8,128)(2,1)S(1)} collective-permute-done((bf16[16,256]{1,0:T(8,128)(2,1)S(1)}, bf16[16,256]{1,0:T(8,128)(2,1)S(1)}, u32[]{:S(2)}, u32[]{:S(2)}) %collective-permute-start.8) | collective-permute-done | bytes 8224 | tf_op jit(solution)/shard_map/ppermute | solution.py:275
  45.9 0.9 %second.1 = f32[256,256]{1,0:T(8,128)} custom-call(bf16[512,320]{1,0:T(8,128)(2,1)S(1)} %get-tuple-element.41.matrix, f32[256,256]{1,0:T(8,128)S(1)} %own.1.first, bf16[16,256]{1,0:T(8,128)(2,1)S(1)} %collective-permute-done.5.h0, bf16[16,256]{1,0:T(8,128)(2,1)S(1)} %collective-permute-done.6.h1, bf16[16,256]{1,0:T(8,128)(2,1)S(1)} %collective-permute-done.7.h2, ...), custom_call_target="tpu_custom_call" | custom-call | tf_op jit(solution)/shard_map/second/pallas_call | solution.py:401
  (1 shorter events, 0.0 us)
Async XLA Ops:
  0.0 6.5 %copy-start.5 = (s32[3]{0:T(128)S(1)}, s32[3]{0:T(128)}, u32[]{:S(2)}) copy-start(s32[3]{0:T(128)} %f.1) | copy-start | bytes 40
  0.0 6.5 %copy-start.6 = (s32[12]{0:T(128)S(1)}, s32[12]{0:T(128)}, u32[]{:S(2)}) copy-start(s32[12]{0:T(128)} %order.1) | copy-start | bytes 148
  0.0 6.5 %copy-start.1 = (bf16[12,384,128]{2,1,0:T(8,128)(2,1)S(1)}, bf16[12,384,128]{2,1,0:T(8,128)(2,1)}, u32[]{:S(2)}) copy-start(bf16[12,384,128]{2,1,0:T(8,128)(2,1)} %coupling.2) | copy-start | bytes 3538948
  0.0 6.5 %copy-start = (bf16[12,384,384]{2,1,0:T(8,128)(2,1)S(1)}, bf16[12,384,384]{2,1,0:T(8,128)(2,1)}, u32[]{:S(2)}) copy-start(bf16[12,384,384]{2,1,0:T(8,128)(2,1)} %factor.2) | copy-start | bytes 10616836
  0.0 6.5 %copy-start.4 = (s32[12,128]{1,0:T(8,128)S(1)}, s32[12,128]{1,0:T(8,128)}, u32[]{:S(2)}) copy-start(s32[12,128]{1,0:T(8,128)} %writes.1) | copy-start | bytes 18436
  0.0 6.5 %copy-start.3 = (s32[12,128]{1,0:T(8,128)S(1)}, s32[12,128]{1,0:T(8,128)}, u32[]{:S(2)}) copy-start(s32[12,128]{1,0:T(8,128)} %reads.1) | copy-start | bytes 18436
  0.0 6.5 %copy-start.7 = (s32[3]{0:T(128)S(1)}, s32[3]{0:T(128)}, u32[]{:S(2)}) copy-start(s32[3]{0:T(128)} %s.1) | copy-start | bytes 40
  3.2 27.1 %copy-start.2 = (bf16[16,1,16,256]{3,2,1,0:T(8,128)(2,1)S(1)}, bf16[16,1,16,256]{3,2,1,0:T(8,128)(2,1)}, u32[]{:S(2)}) copy-start(bf16[16,1,16,256]{3,2,1,0:T(8,128)(2,1)} %param.15) | copy-start | bytes 393220
  3.2 6.3 %collective-permute-start = (bf16[416,128]{1,0:T(8,128)(2,1)S(1)}, bf16[416,128]{1,0:T(8,128)(2,1)S(1)}, u32[]{:S(2)}, u32[]{:S(2)}) collective-permute-start(bf16[416,128]{1,0:T(8,128)(2,1)S(1)} %get-tuple-element.30), channel_id=1, source_target_pairs={{0,1},{1,0},{2,3},{3,2},{4,5},{5,4},{6,7},{7,6},{8,9},{9,8},{10,11... | collective-permute-start | bytes 319496 | tf_op jit(solution)/shard_map/ppermute | solution.py:275
  9.5 20.8 %collective-permute-start.1 = (bf16[384,128]{1,0:T(8,128)(2,1)S(1)}, bf16[384,128]{1,0:T(8,128)(2,1)S(1)}, u32[]{:S(2)}, u32[]{:S(2)}) collective-permute-start(bf16[384,128]{1,0:T(8,128)(2,1)S(1)} %relay.1), channel_id=1, source_target_pairs={{0,32},{1,33},{2,34},{3,35},{4,36},{5,37},{6,38},{7,39},{8,40},{9,... | collective-permute-start | bytes 294920 | tf_op jit(solution)/shard_map/ppermute | solution.py:370
  15.4 11.5 %collective-permute-start.2 = (bf16[16,256]{1,0:T(8,128)(2,1)S(1)}, bf16[16,256]{1,0:T(8,128)(2,1)S(1)}, u32[]{:S(2)}, u32[]{:S(2)}) collective-permute-start(bf16[16,256]{1,0:T(8,128)(2,1)S(1)} %get-tuple-element.38), channel_id=1, source_target_pairs={{0,128},{128,0},{256,384},{384,256},{1,129},{129,1},{257,385},{385... | collective-permute-start | bytes 24584 | tf_op jit(solution)/shard_map/ppermute | solution.py:275
  18.7 8.2 %collective-permute-start.3 = (bf16[16,256]{1,0:T(8,128)(2,1)S(1)}, bf16[16,256]{1,0:T(8,128)(2,1)S(1)}, u32[]{:S(2)}, u32[]{:S(2)}) collective-permute-start(bf16[16,256]{1,0:T(8,128)(2,1)S(1)} %get-tuple-element.39), channel_id=1, source_target_pairs={{128,256},{256,128},{129,257},{257,129},{130,258},{258,130},{131,2... | collective-permute-start | bytes 24584 | tf_op jit(solution)/shard_map/ppermute | solution.py:275
  22.6 7.7 %collective-permute-start.4 = (bf16[16,256]{1,0:T(8,128)(2,1)S(1)}, bf16[16,256]{1,0:T(8,128)(2,1)S(1)}, u32[]{:S(2)}, u32[]{:S(2)}) collective-permute-start(bf16[16,256]{1,0:T(8,128)(2,1)S(1)} %get-tuple-element.40), channel_id=1, source_target_pairs={{1,2},{2,1},{3,4},{4,3},{5,6},{6,5},{7,8},{8,7},{9,10},{10,9},{11,... | collective-permute-start | bytes 24584 | tf_op jit(solution)/shard_map/ppermute | solution.py:275
  31.2 11.4 %collective-permute-start.5 = (bf16[16,256]{1,0:T(8,128)(2,1)S(1)}, bf16[16,256]{1,0:T(8,128)(2,1)S(1)}, u32[]{:S(2)}, u32[]{:S(2)}) collective-permute-start(bf16[16,256]{1,0:T(8,128)(2,1)S(1)} %get-tuple-element.43), channel_id=1, source_target_pairs={{0,128},{128,0},{256,384},{384,256},{1,129},{129,1},{257,385},{385... | collective-permute-start | bytes 24584 | tf_op jit(solution)/shard_map/ppermute | solution.py:275
  33.1 9.5 %collective-permute-start.6 = (bf16[16,256]{1,0:T(8,128)(2,1)S(1)}, bf16[16,256]{1,0:T(8,128)(2,1)S(1)}, u32[]{:S(2)}, u32[]{:S(2)}) collective-permute-start(bf16[16,256]{1,0:T(8,128)(2,1)S(1)} %get-tuple-element.44), channel_id=1, source_target_pairs={{128,256},{256,128},{129,257},{257,129},{130,258},{258,130},{131,2... | collective-permute-start | bytes 24584 | tf_op jit(solution)/shard_map/ppermute | solution.py:275
  36.2 6.5 %collective-permute-start.7 = (bf16[16,256]{1,0:T(8,128)(2,1)S(1)}, bf16[16,256]{1,0:T(8,128)(2,1)S(1)}, u32[]{:S(2)}, u32[]{:S(2)}) collective-permute-start(bf16[16,256]{1,0:T(8,128)(2,1)S(1)} %get-tuple-element.45), channel_id=1, source_target_pairs={{0,1},{1,0},{2,3},{3,2},{4,5},{5,4},{6,7},{7,6},{8,9},{9,8},{10,11... | collective-permute-start | bytes 24584 | tf_op jit(solution)/shard_map/ppermute | solution.py:275
  38.1 7.7 %collective-permute-start.8 = (bf16[16,256]{1,0:T(8,128)(2,1)S(1)}, bf16[16,256]{1,0:T(8,128)(2,1)S(1)}, u32[]{:S(2)}, u32[]{:S(2)}) collective-permute-start(bf16[16,256]{1,0:T(8,128)(2,1)S(1)} %get-tuple-element.46), channel_id=1, source_target_pairs={{1,2},{2,1},{3,4},{4,3},{5,6},{6,5},{7,8},{8,7},{9,10},{10,9},{11,... | collective-permute-start | bytes 24584 | tf_op jit(solution)/shard_map/ppermute | solution.py:275

commit v6 on v5

--- a/solution.py
+++ b/solution.py
@@ -143,11 +143,16 @@
 
 
 def kept_kernel(
-    fx, fz, f, s, order, reads, writes, factor, coupling,
+    fx, fz, f_from, s_from, order_from, reads, writes, factor, coupling,
     given, part, moved_to, moved_from, relayed,
-    to, origin, left, grams, places, rest,
+    to, origin, left, grams, places, rest, f, s, order, small,
 ):
     slots, moves = reads.shape[0], f.shape[0]
+    copies = started(
+        pltpu.make_async_copy(f_from, f, small.at[0]),
+        pltpu.make_async_copy(s_from, s, small.at[1]),
+        pltpu.make_async_copy(order_from, order, small.at[2]),
+    )
     unknowns = reads.shape[1]
     most = slots - moves
     own, cells = fx * fz, origin.shape[0]
@@ -158,12 +163,13 @@
             found = found | (moved[j] == slot)
         return found
 
+    places[...] = cell_of(reads[...], fx, fz)
+    waited(copies)
     count = jnp.int32(0)
     for slot in range(slots):
         rest[count] = slot
         count = count + jnp.where(among(slot, f), 0, 1)
     wanted = [rest[i] for i in range(most)]
-    places[...] = cell_of(reads[...], fx, fz)
 
     def place(slot, valid, to_ref, from_ref, i):
         read = jnp.where(valid, places[pl.ds(slot, 1), :], -1)
@@ -340,7 +346,7 @@
             jax.ShapeDtypeStruct((cells, 2 * moves * unknowns), BF16),
             jax.ShapeDtypeStruct((16 * moves * moves, unknowns), BF16),
         ),
-        in_specs=[SMEM] * 3 + [VMEM] * 4,
+        in_specs=[HBM] * 3 + [VMEM] * 4,
         out_specs=(VMEM,) * 5,
         scratch_shapes=[
             pltpu.VMEM((own, most * unknowns), BF16),
@@ -349,6 +355,10 @@
             pltpu.VMEM((most * unknowns, unknowns), BF16),
             pltpu.VMEM((slots, unknowns), I32),
             pltpu.SMEM((slots,), I32),
+            pltpu.SMEM((moves,), I32),
+            pltpu.SMEM((moves,), I32),
+            pltpu.SMEM((slots,), I32),
+            pltpu.SemaphoreType.DMA((3,)),
         ],
         compiler_params=params(24),
         cost_estimate=element_cost(most),

time: 47.1 us -> 47.1 us (level)
  no operation moved by 1% of the time
where the time goes in v6:
time: 47.1 us; the launch traced here: 46.8 us
  starting transfers between devices  31.7 us (67%)
  Pallas kernels  8.21 us (17%)
  waiting for transfers between devices  6.6 us (14%)
    ppermute x8, starting transfers between devices, swapped(): return lax.ppermute(edge, axis, pairs(lax.axis_size(axis), odd))  25.9 us
    ppermute x8, waiting for transfers between devices, swapped(): return lax.ppermute(edge, axis, pairs(lax.axis_size(axis), odd))  6.6 us
    ppermute x1, starting transfers between devices, body(): got_s = lax.ppermute(relayed, ('gy', 'gz'), swap_route(both, second_bit))  5.81 us
    pallas_call x1, Pallas kernels, body(): pl.pallas_call(functools.partial(given_kernel, fx, fz), out_shape=(load,...  3.18 us
    pallas_call x1, Pallas kernels, body(): pl.pallas_call(functools.partial(kept_kernel, fx, fz), out_shape=(grams,...  2.99 us
  transfers between devices with their start and end apart: 9, of which 2 were waited for; matrix products, arithmetic and copies ran while one was open for 0% of the time, Pallas kernels for 7%

profile of v6, /device:TPU:33, one launch (start us, length us, event | category | flops | bytes accessed | tf_op | source)
XLA Modules:
  0.0 46.8 jit_solution(2804034649604930965)
XLA Ops:
  0.0 0.0 copy-start.5
  0.0 0.0 copy-start.6
  0.0 0.0 copy-start.1
  0.0 0.0 copy-start
  0.0 0.0 copy-start.4
  0.0 0.0 copy-start.3
  0.0 0.0 copy-start.7
  0.0 3.2 %given.1 = (bf16[416,128]{1,0:T(8,128)(2,1)S(1)}, bf16[16,256]{1,0:T(8,128)(2,1)S(1)}, bf16[16,256]{1,0:T(8,128)(2,1)S(1)}, bf16[16,256]{1,0:T(8,128)(2,1)S(1)}) custom-call(s32[3]{0:T(128)} %f_from.1, s32[12]{0:T(128)} %order_from.1, bf16[12,384,384]{2,1,0:T(8,128)(2,1)} %factor.2, bf16[12,384,128]{2,1,0:T(8,128)(2,1)} %coupling.2, bf16[256,256]{1,0:T(8,128)(2,1)} %bitcast.4), custom_call_target="tpu_custom_call" | custom-call | flops 150994944 | bytes 1179648 | tf_op jit(solution)/shard_map/given/pallas_call | solution.py:315
  3.2 0.0 copy-start.2
  3.2 3.3 %collective-permute-start = (bf16[416,128]{1,0:T(8,128)(2,1)S(1)}, bf16[416,128]{1,0:T(8,128)(2,1)S(1)}, u32[]{:S(2)}, u32[]{:S(2)}) collective-permute-start(bf16[416,128]{1,0:T(8,128)(2,1)S(1)} %get-tuple-element.30), channel_id=1, source_target_pairs={{0,1},{1,0},{2,3},{3,2},{4,5},{5,4},{6,7},{7,6},{8,9},{9,8},{10,11... | collective-permute-start | bytes 319496 | tf_op jit(solution)/shard_map/ppermute | solution.py:281
  6.5 0.0 copy-done.5
  6.5 0.0 copy-done.6
  6.5 0.0 copy-done.1
  6.5 0.0 copy-done
  6.5 0.0 copy-done.4
  6.6 0.0 copy-done.3
  6.6 0.0 copy-done.7
  6.6 3.0 %kept.1 = (bf16[384,128]{1,0:T(8,128)(2,1)S(1)}, f32[256,320]{1,0:T(8,128)S(1)}, bf16[256,768]{1,0:T(8,128)(2,1)S(1)}, bf16[320,768]{1,0:T(8,128)(2,1)S(1)}, bf16[144,128]{1,0:T(8,128)(2,1)S(1)}) custom-call(s32[3]{0:T(128)S(1)} %copy-done.5, s32[3]{0:T(128)S(1)} %copy-done.7, s32[12]{0:T(128)S(1)} %copy-done.6, s32[12,128]{1,0:T(8,128)S(1)} %copy-done.3, ...), custom_call_target="tpu_custom_call" | custom-call | flops 452984832 | bytes 3538944 | tf_op jit(solution)/shard_map/kept/pallas_call | solution.py:340
  9.6 0.0 collective-permute-done.got
  9.6 5.8 %collective-permute-start.1 = (bf16[384,128]{1,0:T(8,128)(2,1)S(1)}, bf16[384,128]{1,0:T(8,128)(2,1)S(1)}, u32[]{:S(2)}, u32[]{:S(2)}) collective-permute-start(bf16[384,128]{1,0:T(8,128)(2,1)S(1)} %relay.1), channel_id=1, source_target_pairs={{0,32},{1,33},{2,34},{3,35},{4,36},{5,37},{6,38},{7,39},{8,40},{9,... | collective-permute-start | bytes 294920 | tf_op jit(solution)/shard_map/ppermute | solution.py:380
  15.4 3.3 %collective-permute-start.2 = (bf16[16,256]{1,0:T(8,128)(2,1)S(1)}, bf16[16,256]{1,0:T(8,128)(2,1)S(1)}, u32[]{:S(2)}, u32[]{:S(2)}) collective-permute-start(bf16[16,256]{1,0:T(8,128)(2,1)S(1)} %get-tuple-element.38), channel_id=1, source_target_pairs={{0,128},{128,0},{256,384},{384,256},{1,129},{129,1},{257,385},{385... | collective-permute-start | bytes 24584 | tf_op jit(solution)/shard_map/ppermute | solution.py:281
  18.7 3.9 %collective-permute-start.3 = (bf16[16,256]{1,0:T(8,128)(2,1)S(1)}, bf16[16,256]{1,0:T(8,128)(2,1)S(1)}, u32[]{:S(2)}, u32[]{:S(2)}) collective-permute-start(bf16[16,256]{1,0:T(8,128)(2,1)S(1)} %get-tuple-element.39), channel_id=1, source_target_pairs={{128,256},{256,128},{129,257},{257,129},{130,258},{258,130},{131,2... | collective-permute-start | bytes 24584 | tf_op jit(solution)/shard_map/ppermute | solution.py:281
  22.6 4.3 %collective-permute-start.4 = (bf16[16,256]{1,0:T(8,128)(2,1)S(1)}, bf16[16,256]{1,0:T(8,128)(2,1)S(1)}, u32[]{:S(2)}, u32[]{:S(2)}) collective-permute-start(bf16[16,256]{1,0:T(8,128)(2,1)S(1)} %get-tuple-element.40), channel_id=1, source_target_pairs={{1,2},{2,1},{3,4},{4,3},{5,6},{6,5},{7,8},{8,7},{9,10},{10,9},{11,... | collective-permute-start | bytes 24584 | tf_op jit(solution)/shard_map/ppermute | solution.py:281
  26.9 0.0 collective-permute-done.2.h0
  26.9 0.0 collective-permute-done.3.h1
  26.9 3.4 %collective-permute-done.4.h3 = bf16[16,256]{1,0:T(8,128)(2,1)S(1)} collective-permute-done((bf16[16,256]{1,0:T(8,128)(2,1)S(1)}, bf16[16,256]{1,0:T(8,128)(2,1)S(1)}, u32[]{:S(2)}, u32[]{:S(2)}) %collective-permute-start.4) | collective-permute-done | bytes 8224 | tf_op jit(solution)/shard_map/ppermute | solution.py:281
  30.3 0.0 collective-permute-done.1.got_s
  30.3 0.0 copy-done.2
  30.3 0.9 %first.1 = (bf16[512,320]{1,0:T(8,128)(2,1)S(1)}, bf16[256,256]{1,0:T(8,128)(2,1)S(1)}, bf16[16,256]{1,0:T(8,128)(2,1)S(1)}, bf16[16,256]{1,0:T(8,128)(2,1)S(1)}...) custom-call(bf16[416,128]{1,0:T(8,128)(2,1)S(1)} %collective-permute-done.got, ...), custom_call_target="tpu_custom_call" | custom-call | tf_op jit(solution)/shard_map/first/pallas_call | solution.py:385
  31.2 1.9 %collective-permute-start.5 = (bf16[16,256]{1,0:T(8,128)(2,1)S(1)}, bf16[16,256]{1,0:T(8,128)(2,1)S(1)}, u32[]{:S(2)}, u32[]{:S(2)}) collective-permute-start(bf16[16,256]{1,0:T(8,128)(2,1)S(1)} %get-tuple-element.43), channel_id=1, source_target_pairs={{0,128},{128,0},{256,384},{384,256},{1,129},{129,1},{257,385},{385... | collective-permute-start | bytes 24584 | tf_op jit(solution)/shard_map/ppermute | solution.py:281
  33.1 3.1 %collective-permute-start.6 = (bf16[16,256]{1,0:T(8,128)(2,1)S(1)}, bf16[16,256]{1,0:T(8,128)(2,1)S(1)}, u32[]{:S(2)}, u32[]{:S(2)}) collective-permute-start(bf16[16,256]{1,0:T(8,128)(2,1)S(1)} %get-tuple-element.44), channel_id=1, source_target_pairs={{128,256},{256,128},{129,257},{257,129},{130,258},{258,130},{131,2... | collective-permute-start | bytes 24584 | tf_op jit(solution)/shard_map/ppermute | solution.py:281
  36.2 1.9 %collective-permute-start.7 = (bf16[16,256]{1,0:T(8,128)(2,1)S(1)}, bf16[16,256]{1,0:T(8,128)(2,1)S(1)}, u32[]{:S(2)}, u32[]{:S(2)}) collective-permute-start(bf16[16,256]{1,0:T(8,128)(2,1)S(1)} %get-tuple-element.45), channel_id=1, source_target_pairs={{0,1},{1,0},{2,3},{3,2},{4,5},{5,4},{6,7},{7,6},{8,9},{9,8},{10,11... | collective-permute-start | bytes 24584 | tf_op jit(solution)/shard_map/ppermute | solution.py:281
  38.1 4.3 %collective-permute-start.8 = (bf16[16,256]{1,0:T(8,128)(2,1)S(1)}, bf16[16,256]{1,0:T(8,128)(2,1)S(1)}, u32[]{:S(2)}, u32[]{:S(2)}) collective-permute-start(bf16[16,256]{1,0:T(8,128)(2,1)S(1)} %get-tuple-element.46), channel_id=1, source_target_pairs={{1,2},{2,1},{3,4},{4,3},{5,6},{6,5},{7,8},{8,7},{9,10},{10,9},{11,... | collective-permute-start | bytes 24584 | tf_op jit(solution)/shard_map/ppermute | solution.py:281
  42.4 0.2 own.1.first
  42.7 0.0 collective-permute-done.5.h0
  42.7 0.0 collective-permute-done.6.h1
  42.7 0.0 collective-permute-done.7.h2
  42.7 3.2 %collective-permute-done.8.h3 = bf16[16,256]{1,0:T(8,128)(2,1)S(1)} collective-permute-done((bf16[16,256]{1,0:T(8,128)(2,1)S(1)}, bf16[16,256]{1,0:T(8,128)(2,1)S(1)}, u32[]{:S(2)}, u32[]{:S(2)}) %collective-permute-start.8) | collective-permute-done | bytes 8224 | tf_op jit(solution)/shard_map/ppermute | solution.py:281
  45.9 0.9 %second.1 = f32[256,256]{1,0:T(8,128)} custom-call(bf16[512,320]{1,0:T(8,128)(2,1)S(1)} %get-tuple-element.41.matrix, f32[256,256]{1,0:T(8,128)S(1)} %own.1.first, bf16[16,256]{1,0:T(8,128)(2,1)S(1)} %collective-permute-done.5.h0, bf16[16,256]{1,0:T(8,128)(2,1)S(1)} %collective-permute-done.6.h1, bf16[16,256]{1,0:T(8,128)(2,1)S(1)} %collective-permute-done.7.h2, ...), custom_call_target="tpu_custom_call" | custom-call | tf_op jit(solution)/shard_map/second/pallas_call | solution.py:411
  (1 shorter events, 0.0 us)
Async XLA Ops:
  0.0 6.5 %copy-start.5 = (s32[3]{0:T(128)S(1)}, s32[3]{0:T(128)}, u32[]{:S(2)}) copy-start(s32[3]{0:T(128)} %f_from.1) | copy-start | bytes 40
  0.0 6.5 %copy-start.6 = (s32[12]{0:T(128)S(1)}, s32[12]{0:T(128)}, u32[]{:S(2)}) copy-start(s32[12]{0:T(128)} %order_from.1) | copy-start | bytes 148
  0.0 6.5 %copy-start.1 = (bf16[12,384,128]{2,1,0:T(8,128)(2,1)S(1)}, bf16[12,384,128]{2,1,0:T(8,128)(2,1)}, u32[]{:S(2)}) copy-start(bf16[12,384,128]{2,1,0:T(8,128)(2,1)} %coupling.2) | copy-start | bytes 3538948
  0.0 6.5 %copy-start = (bf16[12,384,384]{2,1,0:T(8,128)(2,1)S(1)}, bf16[12,384,384]{2,1,0:T(8,128)(2,1)}, u32[]{:S(2)}) copy-start(bf16[12,384,384]{2,1,0:T(8,128)(2,1)} %factor.2) | copy-start | bytes 10616836
  0.0 6.5 %copy-start.4 = (s32[12,128]{1,0:T(8,128)S(1)}, s32[12,128]{1,0:T(8,128)}, u32[]{:S(2)}) copy-start(s32[12,128]{1,0:T(8,128)} %writes.1) | copy-start | bytes 18436
  0.0 6.5 %copy-start.3 = (s32[12,128]{1,0:T(8,128)S(1)}, s32[12,128]{1,0:T(8,128)}, u32[]{:S(2)}) copy-start(s32[12,128]{1,0:T(8,128)} %reads.1) | copy-start | bytes 18436
  0.0 6.5 %copy-start.7 = (s32[3]{0:T(128)S(1)}, s32[3]{0:T(128)}, u32[]{:S(2)}) copy-start(s32[3]{0:T(128)} %s_from.1) | copy-start | bytes 40
  3.2 27.1 %copy-start.2 = (bf16[16,1,16,256]{3,2,1,0:T(8,128)(2,1)S(1)}, bf16[16,1,16,256]{3,2,1,0:T(8,128)(2,1)}, u32[]{:S(2)}) copy-start(bf16[16,1,16,256]{3,2,1,0:T(8,128)(2,1)} %param.15) | copy-start | bytes 393220
  3.2 6.3 %collective-permute-start = (bf16[416,128]{1,0:T(8,128)(2,1)S(1)}, bf16[416,128]{1,0:T(8,128)(2,1)S(1)}, u32[]{:S(2)}, u32[]{:S(2)}) collective-permute-start(bf16[416,128]{1,0:T(8,128)(2,1)S(1)} %get-tuple-element.30), channel_id=1, source_target_pairs={{0,1},{1,0},{2,3},{3,2},{4,5},{5,4},{6,7},{7,6},{8,9},{9,8},{10,11... | collective-permute-start | bytes 319496 | tf_op jit(solution)/shard_map/ppermute | solution.py:281
  9.6 20.7 %collective-permute-start.1 = (bf16[384,128]{1,0:T(8,128)(2,1)S(1)}, bf16[384,128]{1,0:T(8,128)(2,1)S(1)}, u32[]{:S(2)}, u32[]{:S(2)}) collective-permute-start(bf16[384,128]{1,0:T(8,128)(2,1)S(1)} %relay.1), channel_id=1, source_target_pairs={{0,32},{1,33},{2,34},{3,35},{4,36},{5,37},{6,38},{7,39},{8,40},{9,... | collective-permute-start | bytes 294920 | tf_op jit(solution)/shard_map/ppermute | solution.py:380
  15.4 11.5 %collective-permute-start.2 = (bf16[16,256]{1,0:T(8,128)(2,1)S(1)}, bf16[16,256]{1,0:T(8,128)(2,1)S(1)}, u32[]{:S(2)}, u32[]{:S(2)}) collective-permute-start(bf16[16,256]{1,0:T(8,128)(2,1)S(1)} %get-tuple-element.38), channel_id=1, source_target_pairs={{0,128},{128,0},{256,384},{384,256},{1,129},{129,1},{257,385},{385... | collective-permute-start | bytes 24584 | tf_op jit(solution)/shard_map/ppermute | solution.py:281
  18.7 8.2 %collective-permute-start.3 = (bf16[16,256]{1,0:T(8,128)(2,1)S(1)}, bf16[16,256]{1,0:T(8,128)(2,1)S(1)}, u32[]{:S(2)}, u32[]{:S(2)}) collective-permute-start(bf16[16,256]{1,0:T(8,128)(2,1)S(1)} %get-tuple-element.39), channel_id=1, source_target_pairs={{128,256},{256,128},{129,257},{257,129},{130,258},{258,130},{131,2... | collective-permute-start | bytes 24584 | tf_op jit(solution)/shard_map/ppermute | solution.py:281
  22.6 7.7 %collective-permute-start.4 = (bf16[16,256]{1,0:T(8,128)(2,1)S(1)}, bf16[16,256]{1,0:T(8,128)(2,1)S(1)}, u32[]{:S(2)}, u32[]{:S(2)}) collective-permute-start(bf16[16,256]{1,0:T(8,128)(2,1)S(1)} %get-tuple-element.40), channel_id=1, source_target_pairs={{1,2},{2,1},{3,4},{4,3},{5,6},{6,5},{7,8},{8,7},{9,10},{10,9},{11,... | collective-permute-start | bytes 24584 | tf_op jit(solution)/shard_map/ppermute | solution.py:281
  31.2 11.4 %collective-permute-start.5 = (bf16[16,256]{1,0:T(8,128)(2,1)S(1)}, bf16[16,256]{1,0:T(8,128)(2,1)S(1)}, u32[]{:S(2)}, u32[]{:S(2)}) collective-permute-start(bf16[16,256]{1,0:T(8,128)(2,1)S(1)} %get-tuple-element.43), channel_id=1, source_target_pairs={{0,128},{128,0},{256,384},{384,256},{1,129},{129,1},{257,385},{385... | collective-permute-start | bytes 24584 | tf_op jit(solution)/shard_map/ppermute | solution.py:281
  33.1 9.5 %collective-permute-start.6 = (bf16[16,256]{1,0:T(8,128)(2,1)S(1)}, bf16[16,256]{1,0:T(8,128)(2,1)S(1)}, u32[]{:S(2)}, u32[]{:S(2)}) collective-permute-start(bf16[16,256]{1,0:T(8,128)(2,1)S(1)} %get-tuple-element.44), channel_id=1, source_target_pairs={{128,256},{256,128},{129,257},{257,129},{130,258},{258,130},{131,2... | collective-permute-start | bytes 24584 | tf_op jit(solution)/shard_map/ppermute | solution.py:281
  36.2 6.5 %collective-permute-start.7 = (bf16[16,256]{1,0:T(8,128)(2,1)S(1)}, bf16[16,256]{1,0:T(8,128)(2,1)S(1)}, u32[]{:S(2)}, u32[]{:S(2)}) collective-permute-start(bf16[16,256]{1,0:T(8,128)(2,1)S(1)} %get-tuple-element.45), channel_id=1, source_target_pairs={{0,1},{1,0},{2,3},{3,2},{4,5},{5,4},{6,7},{7,6},{8,9},{9,8},{10,11... | collective-permute-start | bytes 24584 | tf_op jit(solution)/shard_map/ppermute | solution.py:281
  38.1 7.7 %collective-permute-start.8 = (bf16[16,256]{1,0:T(8,128)(2,1)S(1)}, bf16[16,256]{1,0:T(8,128)(2,1)S(1)}, u32[]{:S(2)}, u32[]{:S(2)}) collective-permute-start(bf16[16,256]{1,0:T(8,128)(2,1)S(1)} %get-tuple-element.46), channel_id=1, source_target_pairs={{1,2},{2,1},{3,4},{4,3},{5,6},{6,5},{7,8},{8,7},{9,10},{10,9},{11,... | collective-permute-start | bytes 24584 | tf_op jit(solution)/shard_map/ppermute | solution.py:281
